TPU v7x, 128 devices: a whole 4x4x4 slice. The times are simulated.
128 devices in a mesh: gx: 16 (over z, y), gz: 8 (over x, core).
Axes of the slice: x: 4, y: 4, z: 4, core: 2. Of those that a mesh axis runs over, the one named last changes fastest.
Arguments:
- density: float32 [1024, 128, 128], P('gx', 'gz'), may hold values from 1 to 2
- momentum: float32 [3, 1024, 128, 128], P(None, 'gx', 'gz'), may hold values from -1 to 1
- energy: float32 [1024, 128, 128], P('gx', 'gz'), may hold values from 4 to 6
- metric: float32 [1024, 128, 128], P('gx', 'gz'), may hold values from 0.5 to 1.5
- deriv_matrix: float32 [1024, 1024], replicated, may hold values from -0.1875 to 0.1875
- smooth_matrix: float32 [1024, 1024], replicated, may hold values from -0.046875 to 0.046875
- panel_of_cell: int32 [1024, 128], P('gx', 'gz'), may hold values from 0 to 63, as said below
- shape_index: int32 [1024, 128], P('gx', 'gz'), may hold values from 0 to 255
- mode_table: float32 [256, 128], replicated, may hold values from -0.375 to 0.375
Outputs:
- new_density: float32 [1024, 128, 128], P('gx', 'gz')
- new_momentum: float32 [3, 1024, 128, 128], P(None, 'gx', 'gz')
- new_energy: float32 [1024, 128, 128], P('gx', 'gz')
- panel_forces: float32 [64, 128], P('gx')
Inputs may be any that keep to these rules, and one draw needn't show every extreme that they name: `panel_of_cell`: each of the 64 panels is one of 8 contiguous uneven runs of streamwise cells times one of 8 contiguous uneven runs of spanwise cells, panel number = run across the span * 8 + run along the stream; every panel has cells.
All inputs are finite; a program needn't handle non-finite values.
Results may differ from a plain program's by a relative error of at most 0.0003.
Values sent between devices are 32-bit elements; how exact they have to be, the bound alone decides.
No kernel may reach another device: no remote copies, remote signals or barrier semaphores. Data moves between devices by JAX's collectives and lax.ppermute only.
A program may use at most 128 MiB of HBM per device.

v0:
```python
import jax
import jax.numpy as jnp
from jax import lax
from jax.sharding import PartitionSpec as P

NP = 64


time_step = 0.05
gas_factor = 0.4
pressure_ref = 2.0


def with_halo(cells, sides, width):
    for axis, dim in sides:
        count = lax.axis_size(axis)
        head = lax.slice_in_dim(cells, 0, width, axis=dim)
        tail = lax.slice_in_dim(cells, cells.shape[dim] - width, cells.shape[dim], axis=dim)
        cells = jnp.concatenate(
            [
                lax.ppermute(tail, axis, [(i, (i + 1) % count) for i in range(count)]),
                cells,
                lax.ppermute(head, axis, [((i + 1) % count, i) for i in range(count)]),
            ],
            axis=dim,
        )
    return cells


def pressure_of(state):
    kinetic = 0.5 * (state[1] * state[1] + state[2] * state[2] + state[3] * state[3]) / state[0]
    return gas_factor * (state[4] - kinetic)


def fluxes(state, direction):
    pressure = pressure_of(state)
    speed = state[1 + direction] / state[0]
    parts = [state[1 + direction]]
    for component in range(3):
        term = state[1 + component] * speed
        if component == direction:
            term = term + pressure
        parts.append(term)
    parts.append((state[4] + pressure) * speed)
    return jnp.stack(parts)


def slope_y(padded):
    return (
        8.0 * (padded[..., 3:-1] - padded[..., 1:-3]) - (padded[..., 4:] - padded[..., :-4])
    ) / 12.0


def along_y(field):
    return slope_y(jnp.pad(field, ((0, 0), (0, 0), (0, 0), (2, 2))))


def along_z(padded):
    return (
        8.0 * (padded[:, :, 3:-1] - padded[:, :, 1:-3]) - (padded[:, :, 4:] - padded[:, :, :-4])
    ) / 12.0


def span_slope(state):
    padded = with_halo(fluxes(state, 2), (("gz", 2),), 2)
    return along_z(padded)


def x_terms(state, deriv_matrix, smooth_matrix):
    flux = fluxes(state, 0)
    smooth = jnp.einsum("ij,kjzy->kizy", smooth_matrix, state, precision=lax.Precision.HIGHEST)
    slope = jnp.einsum("ij,kjzy->kizy", deriv_matrix, flux, precision=lax.Precision.HIGHEST)
    return smooth - slope


def rate(state, metric, deriv_matrix, smooth_matrix):
    pencil = lax.all_to_all(state, "gx", split_axis=2, concat_axis=1, tiled=True)
    across = lax.all_to_all(
        x_terms(pencil, deriv_matrix, smooth_matrix), "gx", split_axis=1, concat_axis=2, tiled=True
    )
    total = across - along_y(fluxes(state, 1)) - span_slope(state)
    return metric * total


def body(
    density,
    momentum,
    energy,
    metric,
    deriv_matrix,
    smooth_matrix,
    panel_of_cell,
    shape_index,
    mode_table,
):
    state = jnp.concatenate([density[None], momentum, energy[None]], axis=0)
    first = state + time_step * rate(state, metric, deriv_matrix, smooth_matrix)
    final = 0.5 * state + 0.5 * (
        first + time_step * rate(first, metric, deriv_matrix, smooth_matrix)
    )
    load = ((pressure_of(final[:, :, :, 0]) - pressure_ref) * metric[:, :, 0]).reshape(-1)
    panels = panel_of_cell.reshape(-1)
    shapes = shape_index.reshape(-1)
    shape_hits = (
        shapes[:, None] == jnp.arange(mode_table.shape[0], dtype=jnp.int32)[None, :]
    ).astype(jnp.float32)
    panel_hits = (panels[:, None] == jnp.arange(NP, dtype=jnp.int32)[None, :]).astype(jnp.float32)
    summed = jnp.dot(panel_hits.T, shape_hits * load[:, None], precision=lax.Precision.HIGHEST)
    partial_forces = jnp.dot(summed, mode_table, precision=lax.Precision.HIGHEST)
    owned = NP // lax.axis_size("gx")
    everything = lax.psum(partial_forces, ("gx", "gz"))
    forces = lax.dynamic_slice_in_dim(everything, lax.axis_index("gx") * owned, owned, 0)
    return (final[0], final[1:4], final[4], forces)


def solution(mesh):
    in_specs = (
        P("gx", "gz", None),
        P(None, "gx", "gz", None),
        P("gx", "gz", None),
        P("gx", "gz", None),
        P(),
        P(),
        P("gx", "gz"),
        P("gx", "gz"),
        P(),
    )
    out_specs = (P("gx", "gz", None), P(None, "gx", "gz", None), P("gx", "gz", None), P("gx", None))
    return jax.shard_map(body, mesh=mesh, in_specs=in_specs, out_specs=out_specs, check_vma=False)
```

profile of v0, /device:TPU:0, one launch (start us, length us, event | category | flops | bytes accessed | tf_op | source)
XLA Modules:
  0.0 447.2 jit_solution(15006222062434276283)
XLA Ops:
  8.3 4.4 pad_maximum_fusion.4
  12.7 6.0 %copy.335 = f32[5,64,16,128]{3,1,0,2:T(8,128)} copy(f32[5,64,16,128]{1,2,3,0:T(8,128)} %pad_maximum_fusion.4) | data formatting | bytes 5242880 | tf_op jit(solution)/shard_map/concatenate | solution.py:96
  18.7 8.4 %all-to-all-start = ((f32[5,64,16,128]{3,1,0,2:T(8,128)}), f32[5,64,16,128]{3,1,0,2:T(8,128)}, u32[]{:S(2)}, u32[]{:S(2)}) async-start(f32[5,64,16,128]{3,1,0,2:T(8,128)} %copy.335), calls=%async_computation | async-start | bytes 5242880 | tf_op jit(solution)/shard_map/all_to_all | solution.py:77
  28.2 38.7 %all-to-all-done = f32[5,64,16,128]{3,1,0,2:T(8,128)} async-done(((f32[5,64,16,128]{3,1,0,2:T(8,128)}), f32[5,64,16,128]{3,1,0,2:T(8,128)}, u32[]{:S(2)}, u32[]{:S(2)}) %all-to-all-start) | async-done | bytes 2621472 | tf_op jit(solution)/shard_map/all_to_all | solution.py:77
  92.4 10.4 %fusion.26 = f32[5,128,1024]{2,1,0:T(8,128)S(1)} fusion(f32[1024,1024]{1,0:T(8,128)S(1)} %copy-done.10, f32[5,1024,1,128]{1,3,0,2:T(8,128)} %multiply_dynamic-update-slice_fusion.9), kind=kOutput, calls=%fused_computation.41 | convolution fusion | flops 8053063680 | bytes 9437184 | tf_op jit(solution)/shard_map/ij,kjzy->kizy/dot_general | solution.py:72
  102.8 18.5 %subtract_bitcast_fusion.1 = f32[5,1024,1,128]{1,3,0,2:T(8,128)} fusion(f32[5,128,1024]{2,1,0:T(8,128)S(1)} %fusion.26, f32[5,1024,128]{2,1,0:T(8,128)S(1)} %bitcast.152, f32[1024,1024]{1,0:T(8,128)S(1)} %copy-done.8), kind=kOutput, calls=%fused_computation.50 | convolution fusion | flops 8053719040 | bytes 12058624 | tf_op jit(solution)/shard_map/ij,kjzy->kizy/dot_general | solution.py:71
  121.4 6.4 %copy.353 = f32[5,1024,1,128]{3,2,0,1:T(1,128)} copy(f32[5,1024,1,128]{1,3,0,2:T(8,128)} %subtract_bitcast_fusion.1) | data formatting | bytes 5242880 | tf_op jit(solution)/shard_map/sub | solution.py:73
  127.8 4.5 all-to-all-start.1
  157.4 12.2 %all-to-all-done.1 = f32[5,1024,1,128]{3,2,0,1:T(1,128)} async-done(((f32[5,1024,1,128]{3,2,0,1:T(1,128)}), f32[5,1024,1,128]{3,2,0,1:T(1,128)}, u32[]{:S(2)}, u32[]{:S(2)}) %all-to-all-start.1) | async-done | bytes 2621472 | tf_op jit(solution)/shard_map/all_to_all | solution.py:78
  173.0 5.1 %copy.355 = f32[5,16,64,1,128]{2,1,4,0,3:T(8,128)} copy(f32[5,16,64,1,128]{4,2,1,0,3:T(8,128)} %bitcast.155) | data formatting | bytes 5242880 | tf_op jit(solution)/shard_map/all_to_all | solution.py:78
  178.1 21.6 %fusion.20 = f32[5,64,16,128]{1,2,3,0:T(8,128)} fusion(f32[5,64,2,128]{1,2,3,0:T(2,128)} %copy.367, f32[5,64,16,128]{1,2,3,0:T(8,128)} %copy-done.15, f32[5,64,2,128]{1,2,3,0:T(2,128)} %copy.365, f32[5,16,64,1,128]{2,1,4,0,3:T(8,128)} %copy.355, f32[5,64,16,128]{1,2,3,0:T(8,128)} %get-tuple-element.69, f32[64,16,128]{0,1,2:T(8,128)} %copy.334, ...), kind=kLoop, calls=%fused_computation.28 | loop fusion | flops 13762560 | bytes 14286848 | tf_op jit(solution)/shard_map/add | solution.py:97
  199.6 6.0 %copy.368 = f32[5,64,16,128]{3,1,0,2:T(8,128)} copy(f32[5,64,16,128]{1,2,3,0:T(8,128)} %fusion.20) | data formatting | bytes 5242880 | tf_op jit(solution)/shard_map/add | solution.py:97
  205.6 4.6 %all-to-all-start.2 = ((f32[5,64,16,128]{3,1,0,2:T(8,128)}), f32[5,64,16,128]{3,1,0,2:T(8,128)}, u32[]{:S(2)}, u32[]{:S(2)}) async-start(f32[5,64,16,128]{3,1,0,2:T(8,128)} %copy.368), calls=%async_computation.2 | async-start | bytes 5242880 | tf_op jit(solution)/shard_map/all_to_all | solution.py:77
  216.0 29.8 %all-to-all-done.2 = f32[5,64,16,128]{3,1,0,2:T(8,128)} async-done(((f32[5,64,16,128]{3,1,0,2:T(8,128)}), f32[5,64,16,128]{3,1,0,2:T(8,128)}, u32[]{:S(2)}, u32[]{:S(2)}) %all-to-all-start.2) | async-done | bytes 2621472 | tf_op jit(solution)/shard_map/all_to_all | solution.py:77
  266.4 10.4 %fusion.24 = f32[5,128,1024]{2,1,0:T(8,128)S(1)} fusion(f32[1024,1024]{1,0:T(8,128)S(1)} %copy-done.11, f32[5,1024,1,128]{1,3,0,2:T(8,128)} %multiply_dynamic-update-slice_fusion.6), kind=kOutput, calls=%fused_computation.39 | convolution fusion | flops 8053063680 | bytes 9437184 | tf_op jit(solution)/shard_map/ij,kjzy->kizy/dot_general | solution.py:72
  276.9 18.5 %subtract_bitcast_fusion = f32[5,1024,1,128]{1,3,0,2:T(8,128)} fusion(f32[5,128,1024]{2,1,0:T(8,128)S(1)} %fusion.24, f32[5,1024,128]{2,1,0:T(8,128)S(1)} %bitcast.154, f32[1024,1024]{1,0:T(8,128)S(1)} %copy-done.9), kind=kOutput, calls=%fused_computation.49 | convolution fusion | flops 8053719040 | bytes 12058624 | tf_op jit(solution)/shard_map/ij,kjzy->kizy/dot_general | solution.py:71
  295.3 6.5 %copy.386 = f32[5,1024,1,128]{3,2,0,1:T(1,128)} copy(f32[5,1024,1,128]{1,3,0,2:T(8,128)} %subtract_bitcast_fusion) | data formatting | bytes 5242880 | tf_op jit(solution)/shard_map/sub | solution.py:73
  301.8 4.6 %all-to-all-start.3 = ((f32[5,1024,1,128]{3,2,0,1:T(1,128)}), f32[5,1024,1,128]{3,2,0,1:T(1,128)}, u32[]{:S(2)}, u32[]{:S(2)}) async-start(f32[5,1024,1,128]{3,2,0,1:T(1,128)} %copy.386), calls=%async_computation.3 | async-start | bytes 5242880 | tf_op jit(solution)/shard_map/all_to_all | solution.py:78
  306.5 4.1 add_dynamic-update-slice_fusion.1
  320.4 3.9 collective-permute-done.3
  326.5 15.8 %all-to-all-done.3 = f32[5,1024,1,128]{3,2,0,1:T(1,128)} async-done(((f32[5,1024,1,128]{3,2,0,1:T(1,128)}), f32[5,1024,1,128]{3,2,0,1:T(1,128)}, u32[]{:S(2)}, u32[]{:S(2)}) %all-to-all-start.3) | async-done | bytes 2621472 | tf_op jit(solution)/shard_map/all_to_all | solution.py:78
  345.8 5.2 %copy.388 = f32[5,16,64,1,128]{2,1,4,0,3:T(8,128)} copy(f32[5,16,64,1,128]{4,2,1,0,3:T(8,128)} %bitcast.156) | data formatting | bytes 5242880 | tf_op jit(solution)/shard_map/all_to_all | solution.py:78
  351.1 21.3 %fusion.10 = f32[5,64,16,128]{1,2,3,0:T(8,128)S(1)} fusion(f32[5,64,16,128]{1,2,3,0:T(8,128)} %fusion.20, f32[5,64,2,128]{1,2,3,0:T(2,128)} %copy.392, f32[5,64,16,128]{1,2,3,0:T(8,128)} %copy-done.16, f32[5,64,2,128]{1,2,3,0:T(2,128)} %copy.390, f32[5,16,64,1,128]{2,1,4,0,3:T(8,128)} %copy.388, f32[5,64,16,128]{1,2,3,0:T(8,128)} %get-tuple-element.40, ...), kind=kLoop, calls=%fused_computation.18 | loop fusion | flops 15073280 | bytes 16908288 | tf_op jit(solution)/shard_map/add | solution.py:98
  382.6 63.9 %psum.7 = f32[64,128]{1,0:T(8,128)S(1)} all-reduce(f32[64,128]{1,0:T(8,128)S(1)} %fusion.66), channel_id=1, replica_groups=mesh['gx'=16,'gz'=8] {'gx','gz'}, use_global_device_ids=true, to_apply=%region_0.1 | all-reduce | flops 8192 | bytes 65536 | tf_op jit(solution)/shard_map/psum | solution.py:111
  (135 shorter events, 115.3 us)
Async XLA Ops:
  0.6 381.7 %copy-start = (f32[256,128]{1,0:T(8,128)S(1)}, f32[256,128]{1,0:T(8,128)}, u32[]{:S(2)}) copy-start(f32[256,128]{1,0:T(8,128)} %param.17) | copy-start | bytes 393220
  3.0 175.1 %copy-start.1 = (f32[3,64,16,128]{1,2,3,0:T(8,128)}, f32[3,64,16,128]{1,2,3,0:T(8,128)S(1)}, u32[]{:S(2)}) copy-start(f32[3,64,16,128]{1,2,3,0:T(8,128)S(1)} %copy.333) | copy-start | bytes 4718596
  18.7 48.2 %all-to-all-start = ((f32[5,64,16,128]{3,1,0,2:T(8,128)}), f32[5,64,16,128]{3,1,0,2:T(8,128)}, u32[]{:S(2)}, u32[]{:S(2)}) async-start(f32[5,64,16,128]{3,1,0,2:T(8,128)} %copy.335), calls=%async_computation | async-start | bytes 5242880 | tf_op jit(solution)/shard_map/all_to_all | solution.py:77
  84.1 7.2 %copy-start.17 = (f32[1,1024,1,128]{1,3,0,2:T(8,128)S(1)}, f32[1,1024,1,128]{1,3,0,2:T(8,128)}, u32[]{:S(2)}) copy-start(f32[1,1024,1,128]{1,3,0,2:T(8,128)} %copy.345) | copy-start | bytes 1572868
  84.1 7.2 %copy-start.19 = (f32[1,1024,1,128]{1,3,0,2:T(8,128)S(1)}, f32[1,1024,1,128]{1,3,0,2:T(8,128)}, u32[]{:S(2)}) copy-start(f32[1,1024,1,128]{1,3,0,2:T(8,128)} %copy.343) | copy-start | bytes 1572868
  84.1 7.2 %copy-start.21 = (f32[1,1024,1,128]{1,3,0,2:T(8,128)S(1)}, f32[1,1024,1,128]{1,3,0,2:T(8,128)}, u32[]{:S(2)}) copy-start(f32[1,1024,1,128]{1,3,0,2:T(8,128)} %copy.348) | copy-start | bytes 1572868
  84.1 8.3 %copy-start.10 = (f32[1024,1024]{1,0:T(8,128)S(1)}, f32[1024,1024]{1,0:T(8,128)}, u32[]{:S(2)}) copy-start(f32[1024,1024]{1,0:T(8,128)} %param.13) | copy-start | bytes 12582916
  92.4 10.4 %copy-start.6 = (f32[5,64,16,128]{3,1,2,0:T(8,128)S(1)}, f32[5,64,16,128]{3,1,2,0:T(8,128)}, u32[]{:S(2)}) copy-start(f32[5,64,16,128]{3,1,2,0:T(8,128)} %copy-done.5) | copy-start | bytes 7864324
  92.4 10.4 %copy-start.8 = (f32[1024,1024]{1,0:T(8,128)S(1)}, f32[1024,1024]{1,0:T(8,128)}, u32[]{:S(2)}) copy-start(f32[1024,1024]{1,0:T(8,128)} %param.14) | copy-start | bytes 12582916
  127.8 41.8 %all-to-all-start.1 = ((f32[5,1024,1,128]{3,2,0,1:T(1,128)}), f32[5,1024,1,128]{3,2,0,1:T(1,128)}, u32[]{:S(2)}, u32[]{:S(2)}) async-start(f32[5,1024,1,128]{3,2,0,1:T(1,128)} %copy.353), calls=%async_computation.1 | async-start | bytes 5242880 | tf_op jit(solution)/shard_map/all_to_all | solution.py:78
  145.1 8.0 %collective-permute-start.1 = (f32[5,64,2,128]{3,1,2,0:T(8,128)}, f32[5,64,2,128]{3,1,2,0:T(8,128)}, u32[]{:S(2)}, u32[]{:S(2)}) collective-permute-start(f32[5,64,2,128]{3,1,2,0:T(8,128)} %copy.366), channel_id=1, source_target_pairs={{0,1},{1,2},{2,3},{3,4},{4,5},{5,6},{6,7},{7,0},{8,9},{9,10},{10,1... | collective-permute-start | bytes 983048 | tf_op jit(solution)/shard_map/ppermute | solution.py:21
  147.1 8.1 %collective-permute-start = (f32[5,64,2,128]{3,1,2,0:T(8,128)}, f32[5,64,2,128]{3,1,2,0:T(8,128)}, u32[]{:S(2)}, u32[]{:S(2)}) collective-permute-start(f32[5,64,2,128]{3,1,2,0:T(8,128)} %copy.364), channel_id=1, source_target_pairs={{1,0},{2,1},{3,2},{4,3},{5,4},{6,5},{7,6},{0,7},{9,8},{10,9},{11,1... | collective-permute-start | bytes 983048 | tf_op jit(solution)/shard_map/ppermute | solution.py:23
  205.6 40.1 %all-to-all-start.2 = ((f32[5,64,16,128]{3,1,0,2:T(8,128)}), f32[5,64,16,128]{3,1,0,2:T(8,128)}, u32[]{:S(2)}, u32[]{:S(2)}) async-start(f32[5,64,16,128]{3,1,0,2:T(8,128)} %copy.368), calls=%async_computation.2 | async-start | bytes 5242880 | tf_op jit(solution)/shard_map/all_to_all | solution.py:77
  259.5 5.8 %copy-start.22 = (f32[1,1024,1,128]{1,3,0,2:T(8,128)S(1)}, f32[1,1024,1,128]{1,3,0,2:T(8,128)}, u32[]{:S(2)}) copy-start(f32[1,1024,1,128]{1,3,0,2:T(8,128)} %copy.381) | copy-start | bytes 1572868
  259.5 6.9 %copy-start.11 = (f32[1024,1024]{1,0:T(8,128)S(1)}, f32[1024,1024]{1,0:T(8,128)}, u32[]{:S(2)}) copy-start(f32[1024,1024]{1,0:T(8,128)} %param.13) | copy-start | bytes 12582916
  266.4 10.4 %copy-start.9 = (f32[1024,1024]{1,0:T(8,128)S(1)}, f32[1024,1024]{1,0:T(8,128)}, u32[]{:S(2)}) copy-start(f32[1024,1024]{1,0:T(8,128)} %param.14) | copy-start | bytes 12582916
  295.3 11.1 %copy-start.12 = (f32[1,64,16,128]{1,2,3,0:T(8,128)S(1)}, f32[1,64,16,128]{1,2,3,0:T(8,128)}, u32[]{:S(2)}) copy-start(f32[1,64,16,128]{1,2,3,0:T(8,128)} %get-tuple-element.31) | copy-start | bytes 1572868
  301.8 8.7 %slice-start = ((s8[5242880]{0:T(1024)(128)(4,1)}), s8[1048576]{0:T(1024)(128)(4,1)S(1)}, s32[]{:S(2)}) async-start(s8[5242880]{0:T(1024)(128)(4,1)} %bitcast.143), calls=%async_computation.4 | async-start | bytes 2097152
  301.8 40.5 %all-to-all-start.3 = ((f32[5,1024,1,128]{3,2,0,1:T(1,128)}), f32[5,1024,1,128]{3,2,0,1:T(1,128)}, u32[]{:S(2)}, u32[]{:S(2)}) async-start(f32[5,1024,1,128]{3,2,0,1:T(1,128)} %copy.386), calls=%async_computation.3 | async-start | bytes 5242880 | tf_op jit(solution)/shard_map/all_to_all | solution.py:78
  313.4 6.4 %copy-start.23 = (f32[64,16,128]{2,1,0:T(8,128)S(1)}, f32[64,16,128]{2,1,0:T(8,128)}, u32[]{:S(2)}) copy-start(f32[64,16,128]{2,1,0:T(8,128)} %param.12) | copy-start | bytes 1572868
  313.4 6.7 %copy-start.24 = (s32[64,16]{0,1:T(8,128)S(1)}, s32[64,16]{0,1:T(8,128)}, u32[]{:S(2)}) copy-start(s32[64,16]{0,1:T(8,128)} %param.16) | copy-start | bytes 12292
  313.4 6.9 %copy-start.25 = (s32[64,16]{0,1:T(8,128)S(1)}, s32[64,16]{0,1:T(8,128)}, u32[]{:S(2)}) copy-start(s32[64,16]{0,1:T(8,128)} %param.15) | copy-start | bytes 12292
  316.6 7.7 %collective-permute-start.3 = (f32[5,64,2,128]{3,1,2,0:T(8,128)S(1)}, f32[5,64,2,128]{3,1,2,0:T(8,128)S(1)}, u32[]{:S(2)}, u32[]{:S(2)}) collective-permute-start(f32[5,64,2,128]{3,1,2,0:T(8,128)S(1)} %copy.391), channel_id=1, source_target_pairs={{0,1},{1,2},{2,3},{3,4},{4,5},{5,6},{6,7},{7,0},{8,9},{9,10},{10,1... | collective-permute-start | bytes 983048 | tf_op jit(solution)/shard_map/ppermute | solution.py:21
  316.8 8.6 %collective-permute-start.2 = (f32[5,64,2,128]{3,1,2,0:T(8,128)S(1)}, f32[5,64,2,128]{3,1,2,0:T(8,128)S(1)}, u32[]{:S(2)}, u32[]{:S(2)}) collective-permute-start(f32[5,64,2,128]{3,1,2,0:T(8,128)S(1)} %copy.389), channel_id=1, source_target_pairs={{1,0},{2,1},{3,2},{4,3},{5,4},{6,5},{7,6},{0,7},{9,8},{10,9},{11,1... | collective-permute-start | bytes 983048 | tf_op jit(solution)/shard_map/ppermute | solution.py:23
  (12 other events, 47.0 us)
where the time goes:
time: 452 us; the launch traced here: 447 us
  local copies, waits for them, and re-layouts  114 us (25%)
  waiting for transfers between devices  101 us (22%)
  other arithmetic  79.7 us (18%)
  blocking collectives  63.9 us (14%)
  matrix products  59.2 us (13%)
  starting transfers between devices  28 us (6%)
    all_to_all x2, waiting for transfers between devices, rate(): lax.all_to_all(state, 'gx', split_axis=2, concat_axis=1, tiled=True)  68.5 us
    psum x1, blocking collectives, body(): everything = lax.psum(partial_forces, ('gx', 'gz'))  63.9 us
    dot_general x2, matrix products, x_terms(): jnp.einsum('ij,kjzy->kizy', smooth_matrix, state, precision=lax.Precision...  37 us
    unnamed x69, local copies, waits for them, and re-layouts  29.8 us
    all_to_all x2, waiting for transfers between devices, rate(): lax.all_to_all(x_terms(pencil, deriv_matrix, smooth_matrix), 'gx', split_...  28 us
    unnamed x16, other arithmetic  27.4 us
    add x1, other arithmetic, body(): first = state + time_step * rate(state, metric, deriv_matrix, smooth_matrix)  21.6 us
    add x1, other arithmetic, body(): 0.5 * state  21.3 us
  transfers between devices with their start and end apart: 8, of which 6 were waited for; matrix products, arithmetic and copies ran while one was open for 8% of the time, Pallas kernels for 0%

commit v1 on v0

v1 whole, which is shorter than its diff:
```python
import functools

import jax
import jax.numpy as jnp
from jax import lax
from jax.experimental import pallas as pl
from jax.experimental.pallas import tpu as pltpu
from jax.sharding import PartitionSpec as P

NP = 64
NSHAPE = 256
XB = 64
ZB = 16
YB = 8
LANES = 128
HALF = 64

time_step = 0.05
gas_factor = 0.4
pressure_ref = 2.0
middle = (1.5, 0.0, 0.0, 0.0, 5.0)
near = 8.0 / 12.0
far = 1.0 / 12.0

f32 = jnp.float32
bf16 = jnp.bfloat16


def params():
    return pltpu.CompilerParams()


def cost(flops, nbytes):
    return pl.CostEstimate(flops=flops, bytes_accessed=nbytes, transcendentals=0)


def pressure_of(q, inverse):
    return gas_factor * (q[4] - 0.5 * (q[1] * q[1] + q[2] * q[2] + q[3] * q[3]) * inverse)


def flux(q, pressure, inverse, direction):
    speed = q[1 + direction] * inverse
    parts = [q[1 + direction]]
    for component in range(3):
        term = q[1 + component] * speed
        if component == direction:
            term = term + pressure
        parts.append(term)
    parts.append((q[4] + pressure) * speed)
    return parts


def pack_kernel(d_ref, m_ref, e_ref, g_ref, panel_ref, shape_ref, out_ref, code_ref):
    for zp in range(8):
        for f in range(6):
            if f == 0:
                src = d_ref
            elif f < 4:
                src = m_ref.at[f - 1]
            elif f == 4:
                src = e_ref
            else:
                src = g_ref
            low = src[pl.ds(zp, XB, stride=ZB), :]
            high = src[pl.ds(zp + 8, XB, stride=ZB), :]
            tile = jnp.concatenate([low, high], axis=0).T
            out_ref[:, f * 8 + zp] = tile.reshape(16, YB, LANES)
    turned = (panel_ref[...] * NSHAPE + shape_ref[...]).astype(f32)
    code_ref[:, 0:HALF] = turned[0:8]
    code_ref[:, HALF:LANES] = turned[8:16]
    code = code_ref[...]
    for peer in range(16):
        out_ref[peer, 48] = code


def pack(density, momentum, energy, metric, panels, shapes):
    vm = pl.BlockSpec(memory_space=pltpu.VMEM)
    return pl.pallas_call(
        pack_kernel,
        out_shape=jax.ShapeDtypeStruct((16, 49, YB, LANES), f32),
        in_specs=[vm] * 6,
        out_specs=vm,
        scratch_shapes=[pltpu.VMEM((8, LANES), f32)],
        compiler_params=params(),
        cost_estimate=cost(1000000, 6400000),
        name="pack",
    )(
        density.reshape(XB * ZB, LANES),
        momentum.reshape(3, XB * ZB, LANES),
        energy.reshape(XB * ZB, LANES),
        metric.reshape(XB * ZB, LANES),
        panels.T,
        shapes.T,
    )


def emit_operands(q, q_ref, fhi_ref, flo_ref, ytop_ref, ybot_ref, ztop_ref, zbot_ref):
    inverse = 1.0 / q[0]
    pressure = pressure_of(q, inverse)
    stream = flux(q, pressure, inverse, 0)
    for f in range(5):
        rows = pl.ds(f * 128, 128)
        q_ref[rows, :] = (q[f] - middle[f]).reshape(128, LANES).astype(bf16)
        value = stream[f].reshape(128, LANES)
        high = value.astype(bf16)
        fhi_ref[rows, :] = high
        flo_ref[rows, :] = (value - high.astype(f32)).astype(bf16)
    row = lax.broadcasted_iota(jnp.int32, (YB, LANES), 0)
    normal = flux(q, pressure, inverse, 1)
    for f in range(5):
        for zq in range(4):
            top = normal[f][zq * 4]
            bot = normal[f][zq * 4]
            top = pltpu.roll(top, 2, 0)
            for z4 in range(1, 4):
                plane = normal[f][zq * 4 + z4]
                mine = (row >= 2 * z4) & (row < 2 * z4 + 2)
                shift = (2 * z4 + 2) % 8
                top = jnp.where(mine, pltpu.roll(plane, shift, 0) if shift else plane, top)
                bot = jnp.where(mine, pltpu.roll(plane, 2 * z4, 0), bot)
            ytop_ref[f, zq] = top
            ybot_ref[f, zq] = bot
    low = [q[f][0:2] for f in range(5)]
    high = [q[f][14:16] for f in range(5)]
    zlow = flux(low, pressure[0:2], inverse[0:2], 2)
    zhigh = flux(high, pressure[14:16], inverse[14:16], 2)
    for f in range(5):
        zbot_ref[f] = zlow[f]
        ztop_ref[f] = zhigh[f]


operand_shapes = [
    jax.ShapeDtypeStruct((640, 1024), bf16),
    jax.ShapeDtypeStruct((640, 1024), bf16),
    jax.ShapeDtypeStruct((640, 1024), bf16),
    jax.ShapeDtypeStruct((5, 4, YB, 1024), f32),
    jax.ShapeDtypeStruct((5, 4, YB, 1024), f32),
    jax.ShapeDtypeStruct((5, 2, YB, 1024), f32),
    jax.ShapeDtypeStruct((5, 2, YB, 1024), f32),
]
flat_spec = pl.BlockSpec((640, LANES), lambda s: (0, s))
yedge_spec = pl.BlockSpec((5, 4, YB, LANES), lambda s: (0, 0, 0, s))
zedge_spec = pl.BlockSpec((5, 2, YB, LANES), lambda s: (0, 0, 0, s))
operand_specs = [flat_spec] * 3 + [yedge_spec] * 2 + [zedge_spec] * 2
line_spec = pl.BlockSpec((5, ZB, YB, LANES), lambda s: (0, 0, 0, s))
cell_spec = pl.BlockSpec((ZB, YB, LANES), lambda s: (0, 0, s))
code_spec = pl.BlockSpec((ZB, LANES), lambda s: (0, s))


def join(a, b):
    lane = lax.broadcasted_iota(jnp.int32, a.shape, a.ndim - 1)
    axis = a.ndim - 1
    low = jnp.where(lane < HALF, a, pltpu.roll(b, HALF, axis))
    high = jnp.where(lane < HALF, pltpu.roll(a, HALF, axis), b)
    return jnp.concatenate([low, high], axis=0)


def unpack_kernel(in_ref, line_ref, metric_ref, code_ref, *operands):
    q = []
    for f in range(5):
        field = join(in_ref[0, f * 8 : f * 8 + 8], in_ref[1, f * 8 : f * 8 + 8])
        line_ref[f] = field
        q.append(field)
    metric_ref[...] = join(in_ref[0, 40:48], in_ref[1, 40:48])
    code_ref[...] = join(in_ref[0, 48], in_ref[1, 48])
    emit_operands(q, *operands)


def unpack(packed):
    return pl.pallas_call(
        unpack_kernel,
        grid=(8,),
        out_shape=[
            jax.ShapeDtypeStruct((5, ZB, YB, 1024), f32),
            jax.ShapeDtypeStruct((ZB, YB, 1024), f32),
            jax.ShapeDtypeStruct((ZB, 1024), f32),
            *operand_shapes,
        ],
        in_specs=[pl.BlockSpec((2, 49, YB, LANES), lambda s: (s, 0, 0, 0))],
        out_specs=[line_spec, cell_spec, code_spec, *operand_specs],
        compiler_params=params(),
        cost_estimate=cost(10000000, 12000000),
        name="unpack",
    )(packed)


def lines_kernel(q_ref, fhi_ref, flo_ref, smooth_ref, dhi_ref, dlo_ref, sums_ref, out_ref):
    dot = functools.partial(jnp.dot, preferred_element_type=f32)
    fhi = fhi_ref[...]
    slope = dot(fhi, dhi_ref[...]) + dot(flo_ref[...], dhi_ref[...]) + dot(fhi, dlo_ref[...])
    total = dot(q_ref[...], smooth_ref[...]) - slope
    sums = sums_ref[...]
    for f in range(5):
        rows = slice(f * 128, f * 128 + 128)
        part = total[rows]
        out_ref[rows, :] = part + middle[f] * sums if middle[f] else part


def lines(q, fhi, flo, smooth, dhi, dlo, sums):
    wide = 256
    whole = pl.BlockSpec((640, 1024), lambda n: (0, 0))
    part = pl.BlockSpec((1024, wide), lambda n: (0, n))
    out = pl.pallas_call(
        lines_kernel,
        grid=(1024 // wide,),
        out_shape=jax.ShapeDtypeStruct((640, 1024), f32),
        in_specs=[whole] * 3 + [part] * 3 + [pl.BlockSpec((1, wide), lambda n: (0, n))],
        out_specs=pl.BlockSpec((640, wide), lambda n: (0, n)),
        compiler_params=params(),
        cost_estimate=cost(8 * 640 * 1024 * 1024, 14000000),
        name="lines",
    )(q, fhi, flo, smooth, dhi, dlo, sums)
    return out.reshape(5, ZB, YB, 1024)


def slopes(q, ylo_ref, yhi_ref, zlo_ref, zhi_ref):
    inverse = 1.0 / q[0]
    pressure = pressure_of(q, inverse)
    normal = flux(q, pressure, inverse, 1)
    span = flux(q, pressure, inverse, 2)
    row = lax.broadcasted_iota(jnp.int32, (YB, LANES), 0)
    result = []
    for f in range(5):
        planes = [zlo_ref[f, 0], zlo_ref[f, 1]]
        planes += [span[f][z] for z in range(ZB)]
        planes += [zhi_ref[f, 0], zhi_ref[f, 1]]
        rows = []
        for z in range(ZB):
            g = normal[f][z]
            zq, z4 = z // 4, z % 4
            below = ylo_ref[f, zq]
            above = yhi_ref[f, zq]

            def turn(v, shift):
                shift = shift % 8
                return pltpu.roll(v, shift, 0) if shift else v

            back1 = jnp.where(row < 1, turn(below, -2 * z4 - 1), turn(g, 1))
            back2 = jnp.where(row < 2, turn(below, -2 * z4), turn(g, 2))
            ahead1 = jnp.where(row > 6, turn(above, 7 - 2 * z4), turn(g, -1))
            ahead2 = jnp.where(row > 5, turn(above, 6 - 2 * z4), turn(g, -2))
            slope_y = near * (ahead1 - back1) - far * (ahead2 - back2)
            slope_z = near * (planes[z + 3] - planes[z + 1]) - far * (planes[z + 4] - planes[z])
            rows.append(slope_y + slope_z)
        result.append(jnp.stack(rows))
    return result


def first_kernel(line_ref, metric_ref, x_ref, ylo, yhi, zlo, zhi, out_ref, *operands):
    q = [line_ref[f] for f in range(5)]
    cross = slopes(q, ylo, yhi, zlo, zhi)
    scale = time_step * metric_ref[...]
    new = []
    for f in range(5):
        value = q[f] + scale * (x_ref[f] - cross[f])
        out_ref[f] = value
        new.append(value)
    emit_operands(new, *operands)


def first_section(line, metric, x, halos):
    return pl.pallas_call(
        first_kernel,
        grid=(8,),
        out_shape=[jax.ShapeDtypeStruct((5, ZB, YB, 1024), f32), *operand_shapes],
        in_specs=[line_spec, cell_spec, line_spec, yedge_spec, yedge_spec, zedge_spec, zedge_spec],
        out_specs=[line_spec, *operand_specs],
        compiler_params=params(),
        cost_estimate=cost(20000000, 16000000),
        name="first",
    )(line, metric, x, *halos)


def final_kernel(line_ref, first_ref, metric_ref, x_ref, ylo, yhi, zlo, zhi, out_ref, load_ref):
    q = [first_ref[f] for f in range(5)]
    cross = slopes(q, ylo, yhi, zlo, zhi)
    metric = metric_ref[...]
    scale = time_step * metric
    lane = lax.broadcasted_iota(jnp.int32, (8, YB, LANES), 2)
    final = []
    for f in range(5):
        value = 0.5 * line_ref[f] + 0.5 * (q[f] + scale * (x_ref[f] - cross[f]))
        final.append(value)
        low, high = value[0:8], value[8:16]
        out_ref[0, f * 8 : f * 8 + 8] = jnp.where(lane < HALF, low, pltpu.roll(high, HALF, 2))
        out_ref[1, f * 8 : f * 8 + 8] = jnp.where(lane < HALF, pltpu.roll(low, HALF, 2), high)
    pressure = pressure_of(final, 1.0 / final[0])
    load_ref[...] = (pressure - pressure_ref) * metric


def final_section(line, first, metric, x, halos):
    return pl.pallas_call(
        final_kernel,
        grid=(8,),
        out_shape=[
            jax.ShapeDtypeStruct((16, 40, YB, LANES), f32),
            jax.ShapeDtypeStruct((ZB, YB, 1024), f32),
        ],
        in_specs=[
            line_spec,
            line_spec,
            cell_spec,
            line_spec,
            yedge_spec,
            yedge_spec,
            zedge_spec,
            zedge_spec,
        ],
        out_specs=[pl.BlockSpec((2, 40, YB, LANES), lambda s: (s, 0, 0, 0)), cell_spec],
        compiler_params=params(),
        cost_estimate=cost(20000000, 14000000),
        name="final",
    )(line, first, metric, x, *halos)


def home_kernel(in_ref, d_ref, m_ref, e_ref):
    for zp in range(8):
        for f in range(5):
            tile = in_ref[:, f * 8 + zp].reshape(LANES, LANES).T
            if f == 0:
                dst = d_ref
            elif f < 4:
                dst = m_ref.at[f - 1]
            else:
                dst = e_ref
            dst[pl.ds(zp, XB, stride=ZB), :] = tile[0:HALF]
            dst[pl.ds(zp + 8, XB, stride=ZB), :] = tile[HALF:LANES]


def home(packed):
    vm = pl.BlockSpec(memory_space=pltpu.VMEM)
    d, m, e = pl.pallas_call(
        home_kernel,
        out_shape=[
            jax.ShapeDtypeStruct((XB * ZB, LANES), f32),
            jax.ShapeDtypeStruct((3, XB * ZB, LANES), f32),
            jax.ShapeDtypeStruct((XB * ZB, LANES), f32),
        ],
        in_specs=[vm],
        out_specs=[vm] * 3,
        compiler_params=params(),
        cost_estimate=cost(1000000, 5300000),
        name="home",
    )(packed)
    return (
        d.reshape(XB, ZB, LANES),
        m.reshape(3, XB, ZB, LANES),
        e.reshape(XB, ZB, LANES),
    )


def forces_kernel(load_ref, code_ref, table_ref, out_ref, sum_ref):
    sum_ref[...] = jnp.zeros_like(sum_ref)
    panel_row = lax.broadcasted_iota(jnp.int32, (NP, 1024), 0)
    shape_row = lax.broadcasted_iota(jnp.int32, (NSHAPE, 1024), 0)

    def step(z, carry):
        load = load_ref[z, pl.ds(0, 1), :]
        code = code_ref[pl.ds(z, 1), :].astype(jnp.int32)
        panel = code >> 8
        shape = code & 255
        high = load.astype(bf16)
        rest = load - high.astype(f32)
        middle = rest.astype(bf16)
        low = (rest - middle.astype(f32)).astype(bf16)
        hits = panel_row == panel
        pieces = [jnp.where(hits, piece.astype(f32), 0.0).astype(bf16) for piece in (high, middle, low)]
        shape_hits = jnp.where(shape_row == shape, 1.0, 0.0).astype(bf16)
        sum_ref[...] += lax.dot_general(
            jnp.concatenate(pieces, axis=0),
            shape_hits,
            (((1,), (1,)), ((), ())),
            preferred_element_type=f32,
        )
        return carry

    lax.fori_loop(0, ZB, step, 0)
    summed = sum_ref[0:NP] + sum_ref[NP : 2 * NP] + sum_ref[2 * NP : 3 * NP]
    out_ref[...] = jnp.dot(
        summed, table_ref[...], precision=lax.Precision.HIGHEST, preferred_element_type=f32
    )


def forces(load, code, table):
    vm = pl.BlockSpec(memory_space=pltpu.VMEM)
    return pl.pallas_call(
        forces_kernel,
        out_shape=jax.ShapeDtypeStruct((NP, LANES), f32),
        in_specs=[vm] * 3,
        out_specs=vm,
        scratch_shapes=[pltpu.VMEM((3 * NP, NSHAPE), f32)],
        compiler_params=params(),
        cost_estimate=cost(2 * 192 * 256 * 16384, 700000),
        name="forces",
    )(load, code, table)


def spread_forces(partial):
    me = lax.axis_index("gx")
    held = partial
    bit = 8
    while bit:
        half = held.shape[0] // 2
        pairs = [(g, g + bit) for g in range(0, 16, 2 * bit)]
        got = lax.ppermute(held[half:], "gx", pairs)
        held = jnp.where((me & bit) != 0, got, held[:half])
        bit //= 2
    for bit in (1, 2, 4):
        held = held + lax.ppermute(held, "gz", [(g, g ^ bit) for g in range(8)])
    return held


def exchange(ytop, ybot, ztop, zbot):
    up = [(g, g + 1) for g in range(15)]
    down = [(g + 1, g) for g in range(15)]
    right = [(g, (g + 1) % 8) for g in range(8)]
    left = [((g + 1) % 8, g) for g in range(8)]
    return (
        lax.ppermute(ytop, "gx", up),
        lax.ppermute(ybot, "gx", down),
        lax.ppermute(ztop, "gz", right),
        lax.ppermute(zbot, "gz", left),
    )


def split(matrix):
    high = lax.reduce_precision(matrix, 8, 7)
    return high.astype(bf16), (matrix - high).astype(bf16)


def body(
    density,
    momentum,
    energy,
    metric,
    deriv_matrix,
    smooth_matrix,
    panel_of_cell,
    shape_index,
    mode_table,
):
    outgoing = pack(density, momentum, energy, metric, panel_of_cell, shape_index)
    packed = lax.all_to_all(outgoing, "gx", split_axis=0, concat_axis=0, tiled=True)
    dhi, dlo = split(deriv_matrix.T)
    smooth = smooth_matrix.T.astype(bf16)
    sums = jnp.sum(smooth_matrix, axis=1).reshape(1, -1)
    packed, dhi, dlo, smooth, sums = lax.optimization_barrier((packed, dhi, dlo, smooth, sums))

    line, cells, code, q, fhi, flo, *edges = unpack(packed)
    halos = exchange(*edges)
    x = lines(q, fhi, flo, smooth, dhi, dlo, sums)
    first, q, fhi, flo, *edges = first_section(line, cells, x, halos)
    halos = exchange(*edges)
    x = lines(q, fhi, flo, smooth, dhi, dlo, sums)
    returning, load = final_section(line, first, cells, x, halos)

    packed = lax.all_to_all(returning, "gx", split_axis=0, concat_axis=0, tiled=True)
    panel_forces = spread_forces(forces(load, code, mode_table))
    new_density, new_momentum, new_energy = home(packed)
    return new_density, new_momentum, new_energy, panel_forces


def solution(mesh):
    in_specs = (
        P("gx", "gz", None),
        P(None, "gx", "gz", None),
        P("gx", "gz", None),
        P("gx", "gz", None),
        P(),
        P(),
        P("gx", "gz"),
        P("gx", "gz"),
        P(),
    )
    out_specs = (P("gx", "gz", None), P(None, "gx", "gz", None), P("gx", "gz", None), P("gx", None))
    return jax.shard_map(body, mesh=mesh, in_specs=in_specs, out_specs=out_specs, check_vma=False)
```

time: 452 us -> 194 us (0.43)
  the two profiles are of different devices: /device:TPU:0 before, /device:TPU:120 now
where the time goes in v1:
time: 194 us; the launch traced here: 192 us
  Pallas kernels  63.4 us (33%)
  waiting for transfers between devices  55.9 us (29%)
  starting transfers between devices  46.2 us (24%)
  local copies, waits for them, and re-layouts  16.3 us (8%)
  other arithmetic  9.49 us (5%)
    all_to_all x1, waiting for transfers between devices, body(): lax.all_to_all(outgoing, 'gx', split_axis=0, concat_axis=0, tiled=True)  26.7 us
    ppermute x4, waiting for transfers between devices, spread_forces(): got = lax.ppermute(held[half:], 'gx', pairs)  23.4 us
    pallas_call x2, Pallas kernels, lines(): pl.pallas_call(lines_kernel, grid=(1024 // wide,), out_shape=jax.ShapeDty...  20.2 us
    unnamed x22, local copies, waits for them, and re-layouts  15.6 us
    all_to_all x1, starting transfers between devices, body(): lax.all_to_all(returning, 'gx', split_axis=0, concat_axis=0, tiled=True)  14.4 us
    pallas_call x1, Pallas kernels, first_section(): pl.pallas_call(first_kernel, grid=(8,), out_shape=[jax.ShapeDtypeStruct((...  10.2 us
    ppermute x2, starting transfers between devices, exchange(): lax.ppermute(ybot, 'gx', down)  9.17 us
    pallas_call x1, Pallas kernels, final_section(): pl.pallas_call(final_kernel, grid=(8,), out_shape=[jax.ShapeDtypeStruct((...  8.9 us
  transfers between devices with their start and end apart: 17, of which 5 were waited for; matrix products, arithmetic and copies ran while one was open for 11% of the time, Pallas kernels for 14%

profile of v1, /device:TPU:120, one launch (start us, length us, event | category | flops | bytes accessed | tf_op | source)
XLA Modules:
  0.0 192.2 jit_solution(6158527472078498535)
XLA Ops:
  0.6 4.5 %pack.1 = f32[16,49,8,128]{3,2,1,0:T(8,128)} custom-call(f32[1024,128]{1,0:T(8,128)} %bitcast.23, f32[3,1024,128]{2,1,0:T(8,128)} %bitcast.22, f32[1024,128]{1,0:T(8,128)} %bitcast.24, f32[1024,128]{1,0:T(8,128)} %bitcast.25, s32[16,64]{1,0:T(8,128)} %bitcast.26, s32[16,64]{1,0:T(8,128)} %bitcast.27), custom_call_target="tpu_custom_call" | custom-call | flops 1000000 | bytes 6400000 | tf_op jit(solution)/shard_map/pack/pallas_call | solution.py:78
  5.1 6.8 %all-to-all-start = ((f32[16,49,8,128]{3,2,1,0:T(8,128)}), f32[16,49,8,128]{3,2,1,0:T(8,128)S(1)}, u32[]{:S(2)}, u32[]{:S(2)}) async-start(f32[16,49,8,128]{3,2,1,0:T(8,128)} %pack.1), calls=%async_computation | async-start | bytes 6422528 | tf_op jit(solution)/shard_map/all_to_all | solution.py:443
  11.9 5.3 %copy.13 = f32[1024,1024]{0,1:T(8,128)} copy(f32[1024,1024]{1,0:T(8,128)} %param.13) | data formatting | bytes 8388608 | tf_op args[4]
  17.3 4.6 %copy.14 = bf16[1024,1024]{0,1:T(8,128)(2,1)} copy(f32[1024,1024]{1,0:T(8,128)} %param.14) | data formatting | bytes 6291456 | tf_op args[5]
  21.9 3.0 %reduce_sum.9 = f32[1024]{0:T(1024)} reduce(f32[1024,1024]{1,0:T(8,128)} %param.14, f32[]{:T(128)} %constant.2.clone.1), dimensions={1}, to_apply=%region_0.0 | reduce | flops 1047552 | bytes 4198404 | tf_op jit(solution)/shard_map/reduce_sum | solution.py:446
  25.0 5.1 %fusion = (bf16[1024,1024]{1,0:T(8,128)(2,1)}, bf16[1024,1024]{1,0:T(8,128)(2,1)}) fusion(f32[1024,1024]{0,1:T(8,128)} %copy.13), kind=kLoop, calls=%fused_computation.2 | loop fusion | flops 4194304 | bytes 8388608 | tf_op jit(solution)/shard_map/convert_element_type | solution.py:428
  30.1 26.7 %all-to-all-done.in_ref = f32[16,49,8,128]{3,2,1,0:T(8,128)S(1)} async-done(((f32[16,49,8,128]{3,2,1,0:T(8,128)}), f32[16,49,8,128]{3,2,1,0:T(8,128)S(1)}, u32[]{:S(2)}, u32[]{:S(2)}) %all-to-all-start) | async-done | bytes 3211296 | tf_op jit(solution)/shard_map/all_to_all | solution.py:443
  56.7 1.7 copy-done
  58.4 7.7 %unpack.1 = (f32[5,16,8,1024]{3,2,1,0:T(8,128)}, f32[16,8,1024]{2,1,0:T(8,128)}, f32[16,1024]{1,0:T(8,128)}, bf16[640,1024]{1,0:T(8,128)(2,1)}, bf16[640,1024]{1...) custom-call(f32[16,49,8,128]{3,2,1,0:T(8,128)} %copy-done), custom_call_target="tpu_custom_call" | custom-call | flops 10000000 | bytes 12000000 | tf_op jit(solution)/shard_map/unpack/pallas_call | solution.py:170
  67.4 4.6 %collective-permute-start.1 = (f32[5,4,8,1024]{3,2,1,0:T(8,128)}, f32[5,4,8,1024]{3,2,1,0:T(8,128)S(1)}, u32[]{:S(2)}, u32[]{:S(2)}) collective-permute-start(f32[5,4,8,1024]{3,2,1,0:T(8,128)} %get-tuple-element.43), channel_id=1, source_target_pairs={{8,0},{16,8},{24,16},{32,24},{40,32},{48,40},{56,48},{64,56},{72,6... | collective-permute-start | bytes 1966088 | tf_op jit(solution)/shard_map/ppermute | solution.py:420
  72.0 2.9 %collective-permute-start.3 = (f32[5,2,8,1024]{3,2,1,0:T(8,128)}, f32[5,2,8,1024]{3,2,1,0:T(8,128)S(1)}, u32[]{:S(2)}, u32[]{:S(2)}) collective-permute-start(f32[5,2,8,1024]{3,2,1,0:T(8,128)} %get-tuple-element.45), channel_id=1, source_target_pairs={{1,0},{2,1},{3,2},{4,3},{5,4},{6,5},{7,6},{0,7},{9,8},{10,9},{11,1... | collective-permute-start | bytes 983048 | tf_op jit(solution)/shard_map/ppermute | solution.py:422
  75.0 10.1 %lines.2 = f32[640,1024]{1,0:T(8,128)} custom-call(bf16[640,1024]{1,0:T(8,128)(2,1)} %get-tuple-element.35.q_ref, bf16[640,1024]{1,0:T(8,128)(2,1)} %get-tuple-element.36.fhi_ref, bf16[640,1024]{1,0:T(8,128)(2,1)} %get-tuple-element.37.flo_ref, bf16[1024,1024]{1,0:T(8,128)(2,1)} %bitcast.20, bf16[1024,1024]{1,0:T(8,128)(2,1)} %get-tuple-element.39.dhi_ref, ...), custom_call_target="tpu_custom_call" | custom-call | flops 5368709120 | bytes 14000000 | tf_op jit(solution)/shard_map/lines/pallas_call | solution.py:203
  86.4 10.2 %first.1 = (f32[5,16,8,1024]{3,2,1,0:T(8,128)}, bf16[640,1024]{1,0:T(8,128)(2,1)}, bf16[640,1024]{1,0:T(8,128)(2,1)}, bf16[640,1024]{1,0:T(8,128)(2,1)}, f32[5,4...) custom-call(f32[5,16,8,1024]{3,2,1,0:T(8,128)} %get-tuple-element.33.line, ...), custom_call_target="tpu_custom_call" | custom-call | flops 20000000 | bytes 16000000 | tf_op jit(solution)/shard_map/first/pallas_call | solution.py:262
  97.8 4.6 %collective-permute-start.5 = (f32[5,4,8,1024]{3,2,1,0:T(8,128)}, f32[5,4,8,1024]{3,2,1,0:T(8,128)S(1)}, u32[]{:S(2)}, u32[]{:S(2)}) collective-permute-start(f32[5,4,8,1024]{3,2,1,0:T(8,128)} %get-tuple-element.51), channel_id=1, source_target_pairs={{8,0},{16,8},{24,16},{32,24},{40,32},{48,40},{56,48},{64,56},{72,6... | collective-permute-start | bytes 1966088 | tf_op jit(solution)/shard_map/ppermute | solution.py:420
  102.5 2.9 %collective-permute-start.7 = (f32[5,2,8,1024]{3,2,1,0:T(8,128)}, f32[5,2,8,1024]{3,2,1,0:T(8,128)S(1)}, u32[]{:S(2)}, u32[]{:S(2)}) collective-permute-start(f32[5,2,8,1024]{3,2,1,0:T(8,128)} %get-tuple-element.53), channel_id=1, source_target_pairs={{1,0},{2,1},{3,2},{4,3},{5,4},{6,5},{7,6},{0,7},{9,8},{10,9},{11,1... | collective-permute-start | bytes 983048 | tf_op jit(solution)/shard_map/ppermute | solution.py:422
  105.4 10.1 %lines.3 = f32[640,1024]{1,0:T(8,128)} custom-call(bf16[640,1024]{1,0:T(8,128)(2,1)} %get-tuple-element.47.q_ref, bf16[640,1024]{1,0:T(8,128)(2,1)} %get-tuple-element.48.fhi_ref, bf16[640,1024]{1,0:T(8,128)(2,1)} %get-tuple-element.49.flo_ref, bf16[1024,1024]{1,0:T(8,128)(2,1)} %bitcast.21, bf16[1024,1024]{1,0:T(8,128)(2,1)} %get-tuple-element.39.dhi_ref, ...), custom_call_target="tpu_custom_call" | custom-call | flops 5368709120 | bytes 14000000 | tf_op jit(solution)/shard_map/lines/pallas_call | solution.py:203
  116.8 8.9 %final.1 = (f32[16,40,8,128]{3,2,1,0:T(8,128)}, f32[16,8,1024]{2,1,0:T(8,128)}) custom-call(f32[5,16,8,1024]{3,2,1,0:T(8,128)} %get-tuple-element.33.line_ref, f32[5,16,8,1024]{3,2,1,0:T(8,128)} %get-tuple-element.46.first_ref, f32[16,8,1024]{2,1,0:T(8,128)} %get-tuple-element.34.metric_ref, f32[5,16,8,1024]{3,2,1,0:T(8,128)} %bitcast.18, ...), custom_call_target="tpu_custom_call" | custom-call | flops 20000000 | bytes 14000000 | tf_op jit(solution)/shard_map/final/pallas_call | solution.py:292
  125.7 14.4 %all-to-all-start.1 = ((f32[16,40,8,128]{3,2,1,0:T(8,128)}), f32[16,40,8,128]{3,2,1,0:T(8,128)S(1)}, u32[]{:S(2)}, u32[]{:S(2)}) async-start(f32[16,40,8,128]{3,2,1,0:T(8,128)} %get-tuple-element.54), calls=%async_computation.1 | async-start | bytes 5242880 | tf_op jit(solution)/shard_map/all_to_all | solution.py:457
  140.0 7.5 %forces.1 = f32[64,128]{1,0:T(8,128)} custom-call(f32[16,8,1024]{2,1,0:T(8,128)} %get-tuple-element.58.load_ref, f32[16,1024]{1,0:T(8,128)} %get-tuple-element.59.code_ref, f32[256,128]{1,0:T(8,128)} %table_ref.1), custom_call_target="tpu_custom_call" | custom-call | flops 1610612736 | bytes 700000 | tf_op jit(solution)/shard_map/forces/pallas_call | solution.py:386
  152.4 23.4 %collective-permute-done.11 = f32[4,128]{1,0:T(4,128)S(1)} collective-permute-done((f32[4,128]{1,0:T(4,128)S(1)}, f32[4,128]{1,0:T(4,128)S(1)}, u32[]{:S(2)}, u32[]{:S(2)}) %collective-permute-start.11) | collective-permute-done | bytes 2080 | tf_op jit(solution)/shard_map/ppermute | solution.py:405
  178.2 2.4 %collective-permute-done.13 = f32[4,128]{1,0:T(4,128)S(1)} collective-permute-done((f32[4,128]{1,0:T(4,128)S(1)}, f32[4,128]{1,0:T(4,128)S(1)}, u32[]{:S(2)}, u32[]{:S(2)}) %collective-permute-start.13) | collective-permute-done | bytes 2080 | tf_op jit(solution)/shard_map/ppermute | solution.py:409
  180.6 2.9 %collective-permute-start.14 = (f32[4,128]{1,0:T(4,128)S(1)}, f32[4,128]{1,0:T(4,128)S(1)}, u32[]{:S(2)}, u32[]{:S(2)}) collective-permute-start(f32[4,128]{1,0:T(4,128)S(1)} %add.10), channel_id=1, source_target_pairs={{0,4},{1,5},{2,6},{3,7},{4,0},{5,1},{6,2},{7,3},{8,12},{9,13},{10,... | collective-permute-start | bytes 6152 | tf_op jit(solution)/shard_map/ppermute | solution.py:409
  183.5 2.2 %collective-permute-done.14 = f32[4,128]{1,0:T(4,128)S(1)} collective-permute-done((f32[4,128]{1,0:T(4,128)S(1)}, f32[4,128]{1,0:T(4,128)S(1)}, u32[]{:S(2)}, u32[]{:S(2)}) %collective-permute-start.14) | collective-permute-done | bytes 2080 | tf_op jit(solution)/shard_map/ppermute | solution.py:409
  187.8 4.4 %home.1 = (f32[1024,128]{1,0:T(8,128)}, f32[3,1024,128]{2,1,0:T(8,128)}, f32[1024,128]{1,0:T(8,128)}) custom-call(f32[16,40,8,128]{3,2,1,0:T(8,128)} %copy-done.1), custom_call_target="tpu_custom_call" | custom-call | flops 1000000 | bytes 5300000 | tf_op jit(solution)/shard_map/home/pallas_call | solution.py:332
  (53 shorter events, 14.2 us)
Async XLA Ops:
  5.1 51.6 %all-to-all-start = ((f32[16,49,8,128]{3,2,1,0:T(8,128)}), f32[16,49,8,128]{3,2,1,0:T(8,128)S(1)}, u32[]{:S(2)}, u32[]{:S(2)}) async-start(f32[16,49,8,128]{3,2,1,0:T(8,128)} %pack.1), calls=%async_computation | async-start | bytes 6422528 | tf_op jit(solution)/shard_map/all_to_all | solution.py:443
  56.7 1.7 copy-start
  66.1 19.0 %collective-permute-start = (f32[5,4,8,1024]{3,2,1,0:T(8,128)}, f32[5,4,8,1024]{3,2,1,0:T(8,128)S(1)}, u32[]{:S(2)}, u32[]{:S(2)}) collective-permute-start(f32[5,4,8,1024]{3,2,1,0:T(8,128)} %get-tuple-element.42), channel_id=1, source_target_pairs={{0,8},{8,16},{16,24},{24,32},{32,40},{40,48},{48,56},{56,64},{64,7... | collective-permute-start | bytes 1966088 | tf_op jit(solution)/shard_map/ppermute | solution.py:419
  67.4 17.7 %collective-permute-start.1 = (f32[5,4,8,1024]{3,2,1,0:T(8,128)}, f32[5,4,8,1024]{3,2,1,0:T(8,128)S(1)}, u32[]{:S(2)}, u32[]{:S(2)}) collective-permute-start(f32[5,4,8,1024]{3,2,1,0:T(8,128)} %get-tuple-element.43), channel_id=1, source_target_pairs={{8,0},{16,8},{24,16},{32,24},{40,32},{48,40},{56,48},{64,56},{72,6... | collective-permute-start | bytes 1966088 | tf_op jit(solution)/shard_map/ppermute | solution.py:420
  72.0 13.1 %collective-permute-start.2 = (f32[5,2,8,1024]{3,2,1,0:T(8,128)}, f32[5,2,8,1024]{3,2,1,0:T(8,128)S(1)}, u32[]{:S(2)}, u32[]{:S(2)}) collective-permute-start(f32[5,2,8,1024]{3,2,1,0:T(8,128)} %get-tuple-element.44), channel_id=1, source_target_pairs={{0,1},{1,2},{2,3},{3,4},{4,5},{5,6},{6,7},{7,0},{8,9},{9,10},{10,1... | collective-permute-start | bytes 983048 | tf_op jit(solution)/shard_map/ppermute | solution.py:421
  72.0 13.0 %collective-permute-start.3 = (f32[5,2,8,1024]{3,2,1,0:T(8,128)}, f32[5,2,8,1024]{3,2,1,0:T(8,128)S(1)}, u32[]{:S(2)}, u32[]{:S(2)}) collective-permute-start(f32[5,2,8,1024]{3,2,1,0:T(8,128)} %get-tuple-element.45), channel_id=1, source_target_pairs={{1,0},{2,1},{3,2},{4,3},{5,4},{6,5},{7,6},{0,7},{9,8},{10,9},{11,1... | collective-permute-start | bytes 983048 | tf_op jit(solution)/shard_map/ppermute | solution.py:422
  85.1 1.0 copy-start.4
  85.1 1.2 copy-start.5
  96.5 19.0 %collective-permute-start.4 = (f32[5,4,8,1024]{3,2,1,0:T(8,128)}, f32[5,4,8,1024]{3,2,1,0:T(8,128)S(1)}, u32[]{:S(2)}, u32[]{:S(2)}) collective-permute-start(f32[5,4,8,1024]{3,2,1,0:T(8,128)} %get-tuple-element.50), channel_id=1, source_target_pairs={{0,8},{8,16},{16,24},{24,32},{32,40},{40,48},{48,56},{56,64},{64,7... | collective-permute-start | bytes 1966088 | tf_op jit(solution)/shard_map/ppermute | solution.py:419
  97.8 17.7 %collective-permute-start.5 = (f32[5,4,8,1024]{3,2,1,0:T(8,128)}, f32[5,4,8,1024]{3,2,1,0:T(8,128)S(1)}, u32[]{:S(2)}, u32[]{:S(2)}) collective-permute-start(f32[5,4,8,1024]{3,2,1,0:T(8,128)} %get-tuple-element.51), channel_id=1, source_target_pairs={{8,0},{16,8},{24,16},{32,24},{40,32},{48,40},{56,48},{64,56},{72,6... | collective-permute-start | bytes 1966088 | tf_op jit(solution)/shard_map/ppermute | solution.py:420
  102.4 13.1 %collective-permute-start.6 = (f32[5,2,8,1024]{3,2,1,0:T(8,128)}, f32[5,2,8,1024]{3,2,1,0:T(8,128)S(1)}, u32[]{:S(2)}, u32[]{:S(2)}) collective-permute-start(f32[5,2,8,1024]{3,2,1,0:T(8,128)} %get-tuple-element.52), channel_id=1, source_target_pairs={{0,1},{1,2},{2,3},{3,4},{4,5},{5,6},{6,7},{7,0},{8,9},{9,10},{10,1... | collective-permute-start | bytes 983048 | tf_op jit(solution)/shard_map/ppermute | solution.py:421
  102.5 13.0 %collective-permute-start.7 = (f32[5,2,8,1024]{3,2,1,0:T(8,128)}, f32[5,2,8,1024]{3,2,1,0:T(8,128)S(1)}, u32[]{:S(2)}, u32[]{:S(2)}) collective-permute-start(f32[5,2,8,1024]{3,2,1,0:T(8,128)} %get-tuple-element.53), channel_id=1, source_target_pairs={{1,0},{2,1},{3,2},{4,3},{5,4},{6,5},{7,6},{0,7},{9,8},{10,9},{11,1... | collective-permute-start | bytes 983048 | tf_op jit(solution)/shard_map/ppermute | solution.py:422
  115.5 0.8 copy-start.7
  115.5 1.0 copy-start.2
  115.6 1.2 copy-start.3
  125.7 60.6 %all-to-all-start.1 = ((f32[16,40,8,128]{3,2,1,0:T(8,128)}), f32[16,40,8,128]{3,2,1,0:T(8,128)S(1)}, u32[]{:S(2)}, u32[]{:S(2)}) async-start(f32[16,40,8,128]{3,2,1,0:T(8,128)} %get-tuple-element.54), calls=%async_computation.1 | async-start | bytes 5242880 | tf_op jit(solution)/shard_map/all_to_all | solution.py:457
  148.3 0.7 collective-permute-start.8
  149.7 0.7 collective-permute-start.9
  150.4 0.7 collective-permute-start.10
  151.1 24.7 %collective-permute-start.11 = (f32[4,128]{1,0:T(4,128)S(1)}, f32[4,128]{1,0:T(4,128)S(1)}, u32[]{:S(2)}, u32[]{:S(2)}) collective-permute-start(f32[4,128]{1,0:T(4,128)S(1)} %slice.30), channel_id=1, source_target_pairs={{0,8},{16,24},{32,40},{48,56},{64,72},{80,88},{96,104},{112,120},{... | collective-permute-start | bytes 6152 | tf_op jit(solution)/shard_map/ppermute | solution.py:405
  175.8 1.2 collective-permute-start.12
  177.0 3.6 %collective-permute-start.13 = (f32[4,128]{1,0:T(4,128)S(1)}, f32[4,128]{1,0:T(4,128)S(1)}, u32[]{:S(2)}, u32[]{:S(2)}) collective-permute-start(f32[4,128]{1,0:T(4,128)S(1)} %add.9), channel_id=1, source_target_pairs={{0,2},{1,3},{2,0},{3,1},{4,6},{5,7},{6,4},{7,5},{8,10},{9,11},{10,... | collective-permute-start | bytes 6152 | tf_op jit(solution)/shard_map/ppermute | solution.py:409
  180.6 5.1 %collective-permute-start.14 = (f32[4,128]{1,0:T(4,128)S(1)}, f32[4,128]{1,0:T(4,128)S(1)}, u32[]{:S(2)}, u32[]{:S(2)}) collective-permute-start(f32[4,128]{1,0:T(4,128)S(1)} %add.10), channel_id=1, source_target_pairs={{0,4},{1,5},{2,6},{3,7},{4,0},{5,1},{6,2},{7,3},{8,12},{9,13},{10,... | collective-permute-start | bytes 6152 | tf_op jit(solution)/shard_map/ppermute | solution.py:409
  186.3 1.5 copy-start.1
  (3 other events, 2.3 us)

commit v2 on v0

v2 whole, which is shorter than its diff:
```python
import functools

import jax
import jax.numpy as jnp
from jax import lax
from jax.experimental import pallas as pl
from jax.experimental.pallas import tpu as pltpu
from jax.sharding import PartitionSpec as P

NP = 64
NSHAPE = 256
XB = 64
ZB = 16
YB = 8
LANES = 128
HALF = 64

time_step = 0.05
gas_factor = 0.4
pressure_ref = 2.0
middle = (1.5, 0.0, 0.0, 0.0, 5.0)
near = 8.0 / 12.0
far = 1.0 / 12.0

f32 = jnp.float32
bf16 = jnp.bfloat16


def grant(mib):
    return pltpu.CompilerParams(vmem_limit_bytes=mib * 1024 * 1024)


def cost(flops, nbytes):
    return pl.CostEstimate(flops=flops, bytes_accessed=nbytes, transcendentals=0)


def shaped(*shape):
    return jax.ShapeDtypeStruct(shape, f32)


def pressure_of(q, inverse):
    return gas_factor * (q[4] - 0.5 * (q[1] * q[1] + q[2] * q[2] + q[3] * q[3]) * inverse)


def flux(q, pressure, inverse, direction):
    speed = q[1 + direction] * inverse
    parts = [q[1 + direction]]
    for component in range(3):
        term = q[1 + component] * speed
        if component == direction:
            term = term + pressure
        parts.append(term)
    parts.append((q[4] + pressure) * speed)
    return parts


def turn(v, shift):
    shift = shift % YB
    return pltpu.roll(v, shift, v.ndim - 2) if shift else v


def pack_kernel(d_hbm, m_hbm, e_hbm, g_hbm, panel_ref, shape_ref, out_hbm, raw, tiles, code_ref, in_sem, out_sem):
    sources = [d_hbm, m_hbm.at[0], m_hbm.at[1], m_hbm.at[2], e_hbm, g_hbm]
    loads = [pltpu.make_async_copy(sources[f], raw.at[f], in_sem.at[f]) for f in range(6)]
    for load in loads:
        load.start()
    turned = (panel_ref[...] * NSHAPE + shape_ref[...]).astype(f32)
    for peer in range(16):
        code_ref[peer, :, 0:HALF] = turned[0:8]
        code_ref[peer, :, HALF:LANES] = turned[8:16]
    stores = [pltpu.make_async_copy(code_ref, out_hbm.at[:, 48], out_sem.at[6])]
    stores[0].start()
    for f in range(6):
        loads[f].wait()
        for zp in range(8):
            low = raw[f, pl.ds(zp, XB, stride=ZB), :]
            high = raw[f, pl.ds(zp + 8, XB, stride=ZB), :]
            tile = jnp.concatenate([low, high], axis=0).T
            tiles[f, :, zp] = tile.reshape(16, YB, LANES)
        store = pltpu.make_async_copy(tiles.at[f], out_hbm.at[:, f * 8 : f * 8 + 8], out_sem.at[f])
        store.start()
        stores.append(store)
    for store in stores:
        store.wait()


def pack(density, momentum, energy, metric, panels, shapes):
    vm = pl.BlockSpec(memory_space=pltpu.VMEM)
    hbm = pl.BlockSpec(memory_space=pl.ANY)
    return pl.pallas_call(
        pack_kernel,
        out_shape=shaped(16, 49, YB, LANES),
        in_specs=[hbm] * 4 + [vm] * 2,
        out_specs=hbm,
        scratch_shapes=[
            pltpu.VMEM((6, XB * ZB, LANES), f32),
            pltpu.VMEM((6, 16, 8, YB, LANES), f32),
            pltpu.VMEM((16, YB, LANES), f32),
            pltpu.SemaphoreType.DMA((6,)),
            pltpu.SemaphoreType.DMA((7,)),
        ],
        compiler_params=pltpu.CompilerParams(),
        cost_estimate=cost(1000000, 6400000),
        name="pack",
    )(
        density.reshape(XB * ZB, LANES),
        momentum.reshape(3, XB * ZB, LANES),
        energy.reshape(XB * ZB, LANES),
        metric.reshape(XB * ZB, LANES),
        panels.T,
        shapes.T,
    )


def emit_edges(q, inverse, pressure, up_ref, down_ref, right_ref, left_ref):
    row = lax.broadcasted_iota(jnp.int32, (YB, LANES), 0)
    even = row % 2 == 0
    normal = flux(q, pressure, inverse, 1)
    for f in range(5):
        for zq in range(4):
            top = bottom = None
            for z4 in range(4):
                plane = normal[f][zq * 4 + z4]
                last = turn(plane, 2 * z4 + 2)
                head = turn(plane, 2 * z4)
                mine = (row >= 2 * z4) & (row < 2 * z4 + 2)
                top = last if top is None else jnp.where(mine, last, top)
                bottom = head if bottom is None else jnp.where(mine, head, bottom)
            up_ref[f, zq] = far * top - jnp.where(even, near * turn(top, -1), 0.0)
            bottom = jnp.where(even, 0.0, near * turn(bottom, 1)) - far * bottom
            down_ref[f, zq] = turn(bottom, 6)
    ends = [q[f][0:2] for f in range(5)], [q[f][14:16] for f in range(5)]
    low = flux(ends[0], pressure[0:2], inverse[0:2], 2)
    high = flux(ends[1], pressure[14:16], inverse[14:16], 2)
    for f in range(5):
        left_ref[f, 0] = -far * low[f][0]
        left_ref[f, 1] = near * low[f][0] - far * low[f][1]
        right_ref[f, 0] = far * high[f][0] - near * high[f][1]
        right_ref[f, 1] = far * high[f][1]


edge_shapes = [shaped(5, 4, YB, 1024)] * 2 + [shaped(5, 2, YB, 1024)] * 2
yedge_spec = pl.BlockSpec((5, 4, YB, LANES), lambda s: (0, 0, 0, s))
zedge_spec = pl.BlockSpec((5, 2, YB, LANES), lambda s: (0, 0, 0, s))
edge_specs = [yedge_spec] * 2 + [zedge_spec] * 2
line_spec = pl.BlockSpec((5, ZB, YB, LANES), lambda s: (0, 0, 0, s))
cell_spec = pl.BlockSpec((ZB, YB, LANES), lambda s: (0, 0, s))
code_spec = pl.BlockSpec((ZB, LANES), lambda s: (0, s))


def missing(f, z, up_ref, down_ref, right_ref, left_ref):
    row = lax.broadcasted_iota(jnp.int32, (YB, LANES), 0)
    zq, z4 = z // 4, z % 4
    mine = (row >= 2 * z4) & (row < 2 * z4 + 2)
    both = turn(jnp.where(mine, up_ref[f, zq], down_ref[f, zq]), -2 * z4)
    value = jnp.where((row < 2) | (row > 5), both, 0.0)
    if z < 2:
        value = value + right_ref[f, z]
    if z > 13:
        value = value + left_ref[f, z - 14]
    return value


def exchange(up, down, right, left):
    ahead = [(g, g + 1) for g in range(15)]
    back = [(g + 1, g) for g in range(15)]
    return (
        lax.ppermute(up, "gx", ahead),
        lax.ppermute(down, "gx", back),
        lax.ppermute(right, "gz", [(g, (g + 1) % 8) for g in range(8)]),
        lax.ppermute(left, "gz", [((g + 1) % 8, g) for g in range(8)]),
    )


def join(a, b):
    lane = lax.broadcasted_iota(jnp.int32, a.shape, a.ndim - 1)
    axis = a.ndim - 1
    low = jnp.where(lane < HALF, a, pltpu.roll(b, HALF, axis))
    high = jnp.where(lane < HALF, pltpu.roll(a, HALF, axis), b)
    return jnp.concatenate([low, high], axis=0)


def unpack_kernel(in_ref, line_ref, metric_ref, code_ref, *edges):
    q = []
    for f in range(5):
        field = join(in_ref[0, f * 8 : f * 8 + 8], in_ref[1, f * 8 : f * 8 + 8])
        line_ref[f] = field
        q.append(field)
    metric_ref[...] = join(in_ref[0, 40:48], in_ref[1, 40:48])
    code_ref[...] = join(in_ref[0, 48], in_ref[1, 48])
    inverse = 1.0 / q[0]
    emit_edges(q, inverse, pressure_of(q, inverse), *edges)


def unpack(packed):
    return pl.pallas_call(
        unpack_kernel,
        grid=(8,),
        out_shape=[shaped(5, ZB, YB, 1024), shaped(ZB, YB, 1024), shaped(ZB, 1024), *edge_shapes],
        in_specs=[pl.BlockSpec((2, 49, YB, LANES), lambda s: (s, 0, 0, 0))],
        out_specs=[line_spec, cell_spec, code_spec, *edge_specs],
        compiler_params=grant(16),
        cost_estimate=cost(10000000, 8000000),
        name="unpack",
    )(packed)


def inner_slopes(q, f, normal, span):
    row = lax.broadcasted_iota(jnp.int32, (YB, LANES), 0)
    rows = []
    for z in range(ZB):
        g = normal[f][z]
        back1 = jnp.where(row < 1, 0.0, turn(g, 1))
        back2 = jnp.where(row < 2, 0.0, turn(g, 2))
        ahead1 = jnp.where(row > 6, 0.0, turn(g, -1))
        ahead2 = jnp.where(row > 5, 0.0, turn(g, -2))
        slope = near * (ahead1 - back1) - far * (ahead2 - back2)
        for offset, weight in ((1, near), (-1, -near), (2, -far), (-2, far)):
            if 0 <= z + offset < ZB:
                slope = slope + weight * span[f][z + offset]
        rows.append(slope)
    return jnp.stack(rows)


WIDE = 256


def inner_kernel(second, *refs):
    if second:
        whole_ref, base_ref, metric_ref, d_ref, s_ref, out_ref, q_ref, fhi_ref, flo_ref = refs
    else:
        whole_ref, metric_ref, d_ref, s_ref, out_ref, q_ref, fhi_ref, flo_ref = refs
    step = pl.program_id(0)

    @pl.when(step == 0)
    def prepare():
        def part(s, carry):
            lanes = pl.ds(pl.multiple_of(s * LANES, LANES), LANES)
            q = [whole_ref[f, :, :, lanes] for f in range(5)]
            inverse = 1.0 / q[0]
            stream = flux(q, pressure_of(q, inverse), inverse, 0)
            for f in range(5):
                rows = pl.ds(f * 128, 128)
                q_ref[rows, lanes] = (q[f] - middle[f]).reshape(128, LANES).astype(bf16)
                value = stream[f].reshape(128, LANES)
                high = value.astype(bf16)
                fhi_ref[rows, lanes] = high
                flo_ref[rows, lanes] = (value - high.astype(f32)).astype(bf16)
            return carry

        lax.fori_loop(0, 8, part, 0)

    dot = functools.partial(
        lax.dot_general,
        dimension_numbers=(((1,), (1,)), ((), ())),
        preferred_element_type=f32,
    )
    deriv = d_ref[...]
    dhi = deriv.astype(bf16)
    dlo = (deriv - dhi.astype(f32)).astype(bf16)
    smooth = s_ref[...]
    shi = smooth.astype(bf16)
    slo = (smooth - shi.astype(f32)).astype(bf16)
    ones = jnp.ones((16, 1024), bf16)
    sums = (dot(ones, shi) + dot(ones, slo))[0:1]
    fhi = fhi_ref[...]
    stream = dot(q_ref[...], shi) - (dot(fhi, dhi) + dot(flo_ref[...], dhi) + dot(fhi, dlo))
    for f in range(5):
        part = stream[f * 128 : f * 128 + 128]
        part = part + middle[f] * sums if middle[f] else part
        out_ref[f] = part.reshape(ZB, YB, WIDE)

    def finish(c, carry):
        near_lanes = pl.ds(pl.multiple_of(c * LANES, LANES), LANES)
        lanes = pl.ds(pl.multiple_of(step * WIDE + c * LANES, LANES), LANES)
        q = [whole_ref[f, :, :, lanes] for f in range(5)]
        inverse = 1.0 / q[0]
        pressure = pressure_of(q, inverse)
        normal = flux(q, pressure, inverse, 1)
        span = flux(q, pressure, inverse, 2)
        scale = time_step * metric_ref[:, :, near_lanes]
        for f in range(5):
            total = out_ref[f, :, :, near_lanes] - inner_slopes(q, f, normal, span)
            value = q[f] + scale * total
            if second:
                value = 0.5 * base_ref[f, :, :, near_lanes] + 0.5 * value
            out_ref[f, :, :, near_lanes] = value
        return carry

    lax.fori_loop(0, WIDE // LANES, finish, 0)


def inner(state, metric, deriv, smooth, base=None):
    second = base is not None
    whole = pl.BlockSpec((5, ZB, YB, 1024), lambda n: (0, 0, 0, 0))
    part = pl.BlockSpec((5, ZB, YB, WIDE), lambda n: (0, 0, 0, n))
    cell = pl.BlockSpec((ZB, YB, WIDE), lambda n: (0, 0, n))
    matrix = pl.BlockSpec((WIDE, 1024), lambda n: (n, 0))
    return pl.pallas_call(
        functools.partial(inner_kernel, second),
        grid=(1024 // WIDE,),
        out_shape=shaped(5, ZB, YB, 1024),
        in_specs=[whole] + ([part] if second else []) + [cell, matrix, matrix],
        out_specs=part,
        scratch_shapes=[pltpu.VMEM((640, 1024), bf16)] * 3,
        compiler_params=grant(26),
        cost_estimate=cost(8 * 640 * 1024 * 1024, 14000000),
        name="inner2" if second else "inner1",
    )(state, *([base] if second else []), metric, deriv, smooth)


def first_kernel(part_ref, metric_ref, up, down, right, left, out_ref, *edges):
    scale = time_step * metric_ref[...]
    new = []
    for f in range(5):
        halo = jnp.stack([missing(f, z, up, down, right, left) for z in range(ZB)])
        value = part_ref[f] - scale * halo
        out_ref[f] = value
        new.append(value)
    inverse = 1.0 / new[0]
    emit_edges(new, inverse, pressure_of(new, inverse), *edges)


def first_section(part, metric, halos):
    return pl.pallas_call(
        first_kernel,
        grid=(8,),
        out_shape=[shaped(5, ZB, YB, 1024), *edge_shapes],
        in_specs=[line_spec, cell_spec, *edge_specs],
        out_specs=[line_spec, *edge_specs],
        compiler_params=grant(16),
        cost_estimate=cost(10000000, 9000000),
        name="first",
    )(part, metric, *halos)


def final_kernel(part_ref, metric_ref, up, down, right, left, out_ref, load_ref):
    metric = metric_ref[...]
    scale = (0.5 * time_step) * metric
    lane = lax.broadcasted_iota(jnp.int32, (8, YB, LANES), 2)
    final = []
    for f in range(5):
        halo = jnp.stack([missing(f, z, up, down, right, left) for z in range(ZB)])
        value = part_ref[f] - scale * halo
        final.append(value)
        low, high = value[0:8], value[8:16]
        out_ref[0, f * 8 : f * 8 + 8] = jnp.where(lane < HALF, low, pltpu.roll(high, HALF, 2))
        out_ref[1, f * 8 : f * 8 + 8] = jnp.where(lane < HALF, pltpu.roll(low, HALF, 2), high)
    load_ref[...] = (pressure_of(final, 1.0 / final[0]) - pressure_ref) * metric


def final_section(part, metric, halos):
    return pl.pallas_call(
        final_kernel,
        grid=(8,),
        out_shape=[pltpu.HBM((16, 40, YB, LANES), f32), shaped(ZB, YB, 1024)],
        in_specs=[line_spec, cell_spec, *edge_specs],
        out_specs=[pl.BlockSpec((2, 40, YB, LANES), lambda s: (s, 0, 0, 0)), cell_spec],
        compiler_params=grant(16),
        cost_estimate=cost(10000000, 9000000),
        name="final",
    )(part, metric, *halos)


def home_kernel(in_ref, d_hbm, m_hbm, e_hbm, flat, sem):
    targets = [d_hbm, m_hbm.at[0], m_hbm.at[1], m_hbm.at[2], e_hbm]
    stores = []
    for f in range(5):
        for zp in range(8):
            tile = in_ref[:, f * 8 + zp].reshape(LANES, LANES).T
            flat[f, pl.ds(zp, XB, stride=ZB), :] = tile[0:HALF]
            flat[f, pl.ds(zp + 8, XB, stride=ZB), :] = tile[HALF:LANES]
        store = pltpu.make_async_copy(flat.at[f], targets[f], sem.at[f])
        store.start()
        stores.append(store)
    for store in stores:
        store.wait()


def home(packed):
    vm = pl.BlockSpec(memory_space=pltpu.VMEM)
    hbm = pl.BlockSpec(memory_space=pl.ANY)
    d, m, e = pl.pallas_call(
        home_kernel,
        out_shape=[shaped(XB * ZB, LANES), shaped(3, XB * ZB, LANES), shaped(XB * ZB, LANES)],
        in_specs=[vm],
        out_specs=[hbm] * 3,
        scratch_shapes=[pltpu.VMEM((5, XB * ZB, LANES), f32), pltpu.SemaphoreType.DMA((5,))],
        compiler_params=grant(16),
        cost_estimate=cost(1000000, 5300000),
        name="home",
    )(packed)
    return (
        d.reshape(XB, ZB, LANES),
        m.reshape(3, XB, ZB, LANES),
        e.reshape(XB, ZB, LANES),
    )


def forces_kernel(load_ref, code_ref, table_ref, out_ref, sum_ref):
    sum_ref[...] = jnp.zeros_like(sum_ref)
    run_row = lax.broadcasted_iota(jnp.int32, (8, 1024), 0)
    shape_row = lax.broadcasted_iota(jnp.int32, (NSHAPE, 1024), 0).astype(f32).astype(bf16)
    one = jnp.ones((NSHAPE, 1024), bf16)
    none = jnp.zeros((NSHAPE, 1024), bf16)

    def step(z, carry):
        load = load_ref[z, pl.ds(0, 1), :]
        code = code_ref[pl.ds(z, 1), :].astype(jnp.int32)
        across = code[:, 0:1] >> 11
        along = (code >> 8) & 7
        shape = (code & 255).astype(f32).astype(bf16)
        hit = jnp.where(run_row == along, load, 0.0)
        high = hit.astype(bf16)
        low = (hit - high.astype(f32)).astype(bf16)
        shape_hits = jnp.where(shape_row == shape, one, none)
        both = lax.dot_general(
            jnp.concatenate([high, low], axis=0),
            shape_hits,
            (((1,), (1,)), ((), ())),
            preferred_element_type=f32,
        )
        both = both[0:8] + both[8:16]
        for r in range(8):
            sum_ref[r * 8 : r * 8 + 8] += jnp.where(across == r, both, 0.0)
        return carry

    lax.fori_loop(0, ZB, step, 0)
    out_ref[...] = jnp.dot(
        sum_ref[...], table_ref[...], precision=lax.Precision.HIGHEST, preferred_element_type=f32
    )


def forces(load, code, table):
    vm = pl.BlockSpec(memory_space=pltpu.VMEM)
    return pl.pallas_call(
        forces_kernel,
        out_shape=shaped(NP, LANES),
        in_specs=[vm] * 3,
        out_specs=vm,
        scratch_shapes=[pltpu.VMEM((NP, NSHAPE), f32)],
        compiler_params=grant(16),
        cost_estimate=cost(2 * 16 * 256 * 16384, 700000),
        name="forces",
    )(load, code, table)


def spread_forces(held):
    for bit in (1, 2, 4):
        held = held + lax.ppermute(held, "gz", [(g, g ^ bit) for g in range(8)])
    me = lax.axis_index("gx")
    bit = 8
    while bit:
        half = held.shape[0] // 2
        got = lax.ppermute(held[half:], "gx", [(g, g + bit) for g in range(0, 16, 2 * bit)])
        held = jnp.where((me & bit) != 0, got, held[:half])
        bit //= 2
    return held


def body(
    density,
    momentum,
    energy,
    metric,
    deriv_matrix,
    smooth_matrix,
    panel_of_cell,
    shape_index,
    mode_table,
):
    outgoing = pack(density, momentum, energy, metric, panel_of_cell, shape_index)
    packed = lax.all_to_all(outgoing, "gx", split_axis=0, concat_axis=0, tiled=True)
    state, cells, code, *edges = unpack(packed)
    halos = exchange(*edges)
    part = inner(state, cells, deriv_matrix, smooth_matrix)
    first, *edges = first_section(part, cells, halos)
    halos = exchange(*edges)
    part = inner(first, cells, deriv_matrix, smooth_matrix, base=state)
    returning, load = final_section(part, cells, halos)
    packed = lax.all_to_all(returning, "gx", split_axis=0, concat_axis=0, tiled=True)
    panel_forces = spread_forces(forces(load, code, mode_table))
    new_density, new_momentum, new_energy = home(packed)
    return new_density, new_momentum, new_energy, panel_forces


def solution(mesh):
    in_specs = (
        P("gx", "gz", None),
        P(None, "gx", "gz", None),
        P("gx", "gz", None),
        P("gx", "gz", None),
        P(),
        P(),
        P("gx", "gz"),
        P("gx", "gz"),
        P(),
    )
    out_specs = (P("gx", "gz", None), P(None, "gx", "gz", None), P("gx", "gz", None), P("gx", None))
    return jax.shard_map(body, mesh=mesh, in_specs=in_specs, out_specs=out_specs, check_vma=False)
```

time: 452 us -> 151 us (0.33)
  local copies, waits for them, and re-layouts: 114 us -> 0.04 us
  waiting for transfers between devices: 101 us -> 17.5 us
  other arithmetic: 79.7 us -> 0.61 us
  matrix products: 59.2 us -> 0 us
  Pallas kernels: 0 us -> 43.4 us
  blocking collectives: 63.9 us -> 48.8 us
  starting transfers between devices: 28 us -> 37.7 us
    all_to_all x4 -> x1, waiting for transfers between devices: 96.5 us -> 2.5 us  [body(): lax.all_to_all(returning, 'gx', split_axis=0, concat_axis=0, tiled=True)]
    psum x1 -> x0, blocking collectives: 63.9 us -> none  [body(): everything = lax.psum(partial_forces, ('gx', 'gz'))]
    dot_general x6 -> x0, matrix products: 59.2 us -> none  [the longest x2 37 us: x_terms(): jnp.einsum('ij,kjzy->kizy', smooth_matrix, state, precision=lax.Precision...]
    all_to_all x0 -> x1, blocking collectives: none -> 48.8 us  [body(): lax.all_to_all(outgoing, 'gx', split_axis=0, concat_axis=0, tiled=True)]
    pallas_call x0 -> x8, Pallas kernels: none -> 43.4 us  [the longest x2 23.4 us: inner(): pl.pallas_call(functools.partial(inner_kernel, second), grid=(1024 // WID...]
    add x2 -> x3, other arithmetic: 42.9 us -> 0.02 us  [spread_forces(): held = held + lax.ppermute(held, 'gz', [(g, g ^ bit) for g in range(8)])]
    unnamed x69 -> x6, local copies, waits for them, and re-layouts: 29.8 us -> 0.02 us
    unnamed x16 -> x0, other arithmetic: 27.4 us -> none
  transfers between devices with their start and end apart: 8 -> 16, of which waited for: 6 -> 10; matrix products, arithmetic and copies ran while one was open for 8% -> 0% of each run, Pallas kernels for 0% -> 19%
where the time goes in v2:
time: 151 us; the launch traced here: 149 us
  blocking collectives  48.8 us (32%)
  Pallas kernels  43.4 us (29%)
  starting transfers between devices  37.7 us (25%)
  waiting for transfers between devices  17.5 us (12%)
    all_to_all x1, blocking collectives, body(): lax.all_to_all(outgoing, 'gx', split_axis=0, concat_axis=0, tiled=True)  48.8 us
    pallas_call x2, Pallas kernels, inner(): pl.pallas_call(functools.partial(inner_kernel, second), grid=(1024 // WID...  23.4 us
    all_to_all x1, starting transfers between devices, body(): lax.all_to_all(returning, 'gx', split_axis=0, concat_axis=0, tiled=True)  9.79 us
    ppermute x4, starting transfers between devices, spread_forces(): lax.ppermute(held[half:], 'gx', [(g, g + bit) for g in range(0, 16, 2 * b...  9.17 us
    ppermute x4, waiting for transfers between devices, spread_forces(): lax.ppermute(held[half:], 'gx', [(g, g + bit) for g in range(0, 16, 2 * b...  6.87 us
    ppermute x3, waiting for transfers between devices, spread_forces(): held = held + lax.ppermute(held, 'gz', [(g, g ^ bit) for g in range(8)])  6.3 us
    ppermute x2, starting transfers between devices, exchange(): lax.ppermute(up, 'gx', ahead)  5.94 us
    ppermute x2, starting transfers between devices, exchange(): lax.ppermute(left, 'gz', [((g + 1) % 8, g) for g in range(8)])  5.89 us
  transfers between devices with their start and end apart: 16, of which 10 were waited for; matrix products, arithmetic and copies ran while one was open for 0% of the time, Pallas kernels for 19%

profile of v2, /device:TPU:0, one launch (start us, length us, event | category | flops | bytes accessed | tf_op | source)
XLA Modules:
  0.0 148.9 jit_solution(14132617931221783960)
XLA Ops:
  0.6 4.0 %pack.1 = f32[16,49,8,128]{3,2,1,0:T(8,128)} custom-call(f32[1024,128]{1,0:T(8,128)} %bitcast.10, f32[3,1024,128]{2,1,0:T(8,128)} %bitcast.9, f32[1024,128]{1,0:T(8,128)} %bitcast.11, f32[1024,128]{1,0:T(8,128)} %bitcast.12, s32[16,64]{1,0:T(8,128)} %bitcast.13, s32[16,64]{1,0:T(8,128)} %bitcast.14), custom_call_target="tpu_custom_call" | custom-call | flops 1000000 | bytes 6400000 | tf_op jit(solution)/shard_map/pack/pallas_call | solution.py:90
  4.7 48.8 %all_to_all.10.in_ref = f32[16,49,8,128]{3,2,1,0:T(8,128)S(1)} all-to-all(f32[16,49,8,128]{3,2,1,0:T(8,128)} %pack.1), channel_id=1, replica_groups=mesh['gx'=16,'gz'=8] {'gx'}, dimensions={0} | all-to-all | bytes 6422528 | tf_op jit(solution)/shard_map/all_to_all | solution.py:473
  53.5 2.5 %unpack.1 = (f32[5,16,8,1024]{3,2,1,0:T(8,128)S(1)}, f32[16,8,1024]{2,1,0:T(8,128)S(1)}, f32[16,1024]{1,0:T(8,128)S(1)}, f32[5,4,8,1024]{3,2,1,0:T(8,128)S(1)}, ...) custom-call(f32[16,49,8,128]{3,2,1,0:T(8,128)S(1)} %all_to_all.10.in_ref), custom_call_target="tpu_custom_call" | custom-call | flops 10000000 | bytes 8000000 | tf_op jit(solution)/shard_map/unpack/pallas_call | solution.py:196
  56.0 2.5 %collective-permute-start = (f32[5,4,8,1024]{3,2,1,0:T(8,128)S(1)}, f32[5,4,8,1024]{3,2,1,0:T(8,128)S(1)}, u32[]{:S(2)}, u32[]{:S(2)}) collective-permute-start(f32[5,4,8,1024]{3,2,1,0:T(8,128)S(1)} %get-tuple-element.23), channel_id=1, source_target_pairs={{0,8},{8,16},{16,24},{24,32},{32,40},{40,48},{48,56},{56,64},{64,7... | collective-permute-start | bytes 1966088 | tf_op jit(solution)/shard_map/ppermute | solution.py:168
  59.8 2.9 %collective-permute-start.3 = (f32[5,2,8,1024]{3,2,1,0:T(8,128)S(1)}, f32[5,2,8,1024]{3,2,1,0:T(8,128)S(1)}, u32[]{:S(2)}, u32[]{:S(2)}) collective-permute-start(f32[5,2,8,1024]{3,2,1,0:T(8,128)S(1)} %get-tuple-element.26), channel_id=1, source_target_pairs={{1,0},{2,1},{3,2},{4,3},{5,4},{6,5},{7,6},{0,7},{9,8},{10,9},{11,1... | collective-permute-start | bytes 983048 | tf_op jit(solution)/shard_map/ppermute | solution.py:171
  62.8 11.5 %inner1.1.part_ref = f32[5,16,8,1024]{3,2,1,0:T(8,128)S(1)} custom-call(f32[5,16,8,1024]{3,2,1,0:T(8,128)S(1)} %get-tuple-element.21.refs_0_.refs_1_, f32[16,8,1024]{2,1,0:T(8,128)S(1)} %get-tuple-element.22.refs_1_.metric_ref.refs_2_, f32[1024,1024]{1,0:T(8,128)S(1)} %copy-done.1, f32[1024,1024]{1,0:T(8,128)S(1)} %copy-done.2), custom_call_target="tpu_custom_call" | custom-call | flops 5368709120 | bytes 14000000 | tf_op jit(solution)/shard_map/inner1/pallas_call | solution.py:299
  75.5 2.9 %first.1 = (f32[5,16,8,1024]{3,2,1,0:T(8,128)S(1)}, f32[5,4,8,1024]{3,2,1,0:T(8,128)S(1)}, f32[5,4,8,1024]{3,2,1,0:T(8,128)S(1)}, f32[5,2,8,1024]{3,2,1,0:T(8,128)S(1)}, f32[5,2,8,1024]{3,2,1,0:T(8,128)S(1)}) custom-call(f32[5,16,8,1024]{3,2,1,0:T(8,128)S(1)} %inner1.1.part_ref, f32[16,8,1024]{2,1,0:T(8,128)S(1)} %get-tuple-element.22.refs_1_.metric_ref.refs_2_, ...), custom_call_target="tpu_custom_call" | custom-call | flops 10000000 | bytes 9000000 | tf_op jit(solution)/shard_map/first/pallas_call | solution.py:325
  78.3 3.4 %collective-permute-start.4 = (f32[5,4,8,1024]{3,2,1,0:T(8,128)S(1)}, f32[5,4,8,1024]{3,2,1,0:T(8,128)S(1)}, u32[]{:S(2)}, u32[]{:S(2)}) collective-permute-start(f32[5,4,8,1024]{3,2,1,0:T(8,128)S(1)} %get-tuple-element.28), channel_id=1, source_target_pairs={{0,8},{8,16},{16,24},{24,32},{32,40},{40,48},{48,56},{56,64},{64,7... | collective-permute-start | bytes 1966088 | tf_op jit(solution)/shard_map/ppermute | solution.py:168
  81.8 1.3 collective-permute-start.5
  83.1 2.9 %collective-permute-start.7 = (f32[5,2,8,1024]{3,2,1,0:T(8,128)S(1)}, f32[5,2,8,1024]{3,2,1,0:T(8,128)S(1)}, u32[]{:S(2)}, u32[]{:S(2)}) collective-permute-start(f32[5,2,8,1024]{3,2,1,0:T(8,128)S(1)} %get-tuple-element.31), channel_id=1, source_target_pairs={{1,0},{2,1},{3,2},{4,3},{5,4},{6,5},{7,6},{0,7},{9,8},{10,9},{11,1... | collective-permute-start | bytes 983048 | tf_op jit(solution)/shard_map/ppermute | solution.py:171
  86.0 11.9 %inner2.1.part_ref = f32[5,16,8,1024]{3,2,1,0:T(8,128)S(1)} custom-call(f32[5,16,8,1024]{3,2,1,0:T(8,128)S(1)} %get-tuple-element.27.refs_0_, f32[5,16,8,1024]{3,2,1,0:T(8,128)S(1)} %get-tuple-element.21.refs_0_.refs_1_, f32[16,8,1024]{2,1,0:T(8,128)S(1)} %get-tuple-element.22.refs_1_.metric_ref.refs_2_, f32[1024,1024]{1,0:T(8,128)S(1)} %copy-done.1, ...), custom_call_target="tpu_custom_call" | custom-call | flops 5368709120 | bytes 14000000 | tf_op jit(solution)/shard_map/inner2/pallas_call | solution.py:299
  98.7 4.3 %final.1 = (f32[16,40,8,128]{3,2,1,0:T(8,128)}, f32[16,8,1024]{2,1,0:T(8,128)S(1)}) custom-call(f32[5,16,8,1024]{3,2,1,0:T(8,128)S(1)} %inner2.1.part_ref, f32[16,8,1024]{2,1,0:T(8,128)S(1)} %get-tuple-element.22.refs_1_.metric_ref.refs_2_, f32[5,4,8,1024]{3,2,1,0:T(8,128)S(1)} %collective-permute-done.4.up, ...), custom_call_target="tpu_custom_call" | custom-call | flops 10000000 | bytes 9000000 | tf_op jit(solution)/shard_map/final/pallas_call | solution.py:353
  103.0 9.8 %all-to-all-start.1 = ((f32[16,40,8,128]{3,2,1,0:T(8,128)}), f32[16,40,8,128]{3,2,1,0:T(8,128)S(1)}, u32[]{:S(2)}, u32[]{:S(2)}) async-start(f32[16,40,8,128]{3,2,1,0:T(8,128)} %get-tuple-element.32), calls=%async_computation.1 | async-start | bytes 5242880 | tf_op jit(solution)/shard_map/all_to_all | solution.py:481
  112.8 4.5 %forces.1 = f32[64,128]{1,0:T(8,128)S(1)} custom-call(f32[16,8,1024]{2,1,0:T(8,128)S(1)} %get-tuple-element.36.load_ref, f32[16,1024]{1,0:T(8,128)S(1)} %get-tuple-element.37.code_ref, f32[256,128]{1,0:T(8,128)S(1)} %copy-done), custom_call_target="tpu_custom_call" | custom-call | flops 134217728 | bytes 700000 | tf_op jit(solution)/shard_map/forces/pallas_call | solution.py:436
  118.6 1.5 %collective-permute-start.9 = (f32[64,128]{1,0:T(8,128)S(1)}, f32[64,128]{1,0:T(8,128)S(1)}, u32[]{:S(2)}, u32[]{:S(2)}) collective-permute-start(f32[64,128]{1,0:T(8,128)S(1)} %add.9), channel_id=1, source_target_pairs={{0,2},{1,3},{2,0},{3,1},{4,6},{5,7},{6,4},{7,5},{8,10},{9,11},{10,... | collective-permute-start | bytes 98312 | tf_op jit(solution)/shard_map/ppermute | solution.py:450
  120.1 2.4 %collective-permute-done.9 = f32[64,128]{1,0:T(8,128)S(1)} collective-permute-done((f32[64,128]{1,0:T(8,128)S(1)}, f32[64,128]{1,0:T(8,128)S(1)}, u32[]{:S(2)}, u32[]{:S(2)}) %collective-permute-start.9) | collective-permute-done | bytes 32800 | tf_op jit(solution)/shard_map/ppermute | solution.py:450
  122.5 2.7 %collective-permute-start.10 = (f32[64,128]{1,0:T(8,128)S(1)}, f32[64,128]{1,0:T(8,128)S(1)}, u32[]{:S(2)}, u32[]{:S(2)}) collective-permute-start(f32[64,128]{1,0:T(8,128)S(1)} %add.10), channel_id=1, source_target_pairs={{0,4},{1,5},{2,6},{3,7},{4,0},{5,1},{6,2},{7,3},{8,12},{9,13},{10,... | collective-permute-start | bytes 98312 | tf_op jit(solution)/shard_map/ppermute | solution.py:450
  125.3 2.7 %collective-permute-done.10 = f32[64,128]{1,0:T(8,128)S(1)} collective-permute-done((f32[64,128]{1,0:T(8,128)S(1)}, f32[64,128]{1,0:T(8,128)S(1)}, u32[]{:S(2)}, u32[]{:S(2)}) %collective-permute-start.10) | collective-permute-done | bytes 32800 | tf_op jit(solution)/shard_map/ppermute | solution.py:450
  128.0 5.3 %collective-permute-start.11 = (f32[32,128]{1,0:T(8,128)S(1)}, f32[32,128]{1,0:T(8,128)S(1)}, u32[]{:S(2)}, u32[]{:S(2)}) collective-permute-start(f32[32,128]{1,0:T(8,128)S(1)} %slice.32), channel_id=1, source_target_pairs={{0,64},{1,65},{2,66},{3,67},{4,68},{5,69},{6,70},{7,71}} | collective-permute-start | bytes 49160 | tf_op jit(solution)/shard_map/ppermute | solution.py:455
  133.3 2.9 %collective-permute-done.11 = f32[32,128]{1,0:T(8,128)S(1)} collective-permute-done((f32[32,128]{1,0:T(8,128)S(1)}, f32[32,128]{1,0:T(8,128)S(1)}, u32[]{:S(2)}, u32[]{:S(2)}) %collective-permute-start.11) | collective-permute-done | bytes 16416 | tf_op jit(solution)/shard_map/ppermute | solution.py:455
  137.5 1.3 collective-permute-done.12
  140.2 1.3 collective-permute-done.13
  144.7 2.5 %all-to-all-done.1.in_ref = f32[16,40,8,128]{3,2,1,0:T(8,128)S(1)} async-done(((f32[16,40,8,128]{3,2,1,0:T(8,128)}), f32[16,40,8,128]{3,2,1,0:T(8,128)S(1)}, u32[]{:S(2)}, u32[]{:S(2)}) %all-to-all-start.1) | async-done | bytes 2621472 | tf_op jit(solution)/shard_map/all_to_all | solution.py:481
  147.2 1.8 %home.1 = (f32[1024,128]{1,0:T(8,128)}, f32[3,1024,128]{2,1,0:T(8,128)}, f32[1024,128]{1,0:T(8,128)}) custom-call(f32[16,40,8,128]{3,2,1,0:T(8,128)S(1)} %all-to-all-done.1.in_ref), custom_call_target="tpu_custom_call" | custom-call | flops 1000000 | bytes 5300000 | tf_op jit(solution)/shard_map/home/pallas_call | solution.py:383
  (34 shorter events, 10.2 us)
Async XLA Ops:
  4.7 58.1 %copy-start.1 = (f32[1024,1024]{1,0:T(8,128)S(1)}, f32[1024,1024]{1,0:T(8,128)}, u32[]{:S(2)}) copy-start(f32[1024,1024]{1,0:T(8,128)} %refs_3_.3) | copy-start | bytes 12582916
  4.7 58.1 %copy-start.2 = (f32[1024,1024]{1,0:T(8,128)S(1)}, f32[1024,1024]{1,0:T(8,128)}, u32[]{:S(2)}) copy-start(f32[1024,1024]{1,0:T(8,128)} %refs_4_.1) | copy-start | bytes 12582916
  56.0 18.3 %collective-permute-start = (f32[5,4,8,1024]{3,2,1,0:T(8,128)S(1)}, f32[5,4,8,1024]{3,2,1,0:T(8,128)S(1)}, u32[]{:S(2)}, u32[]{:S(2)}) collective-permute-start(f32[5,4,8,1024]{3,2,1,0:T(8,128)S(1)} %get-tuple-element.23), channel_id=1, source_target_pairs={{0,8},{8,16},{16,24},{24,32},{32,40},{40,48},{48,56},{56,64},{64,7... | collective-permute-start | bytes 1966088 | tf_op jit(solution)/shard_map/ppermute | solution.py:168
  58.5 17.0 %collective-permute-start.1 = (f32[5,4,8,1024]{3,2,1,0:T(8,128)S(1)}, f32[5,4,8,1024]{3,2,1,0:T(8,128)S(1)}, u32[]{:S(2)}, u32[]{:S(2)}) collective-permute-start(f32[5,4,8,1024]{3,2,1,0:T(8,128)S(1)} %get-tuple-element.24), channel_id=1, source_target_pairs={{8,0},{16,8},{24,16},{32,24},{40,32},{48,40},{56,48},{64,56},{72,6... | collective-permute-start | bytes 1966088 | tf_op jit(solution)/shard_map/ppermute | solution.py:169
  59.8 14.5 %collective-permute-start.2 = (f32[5,2,8,1024]{3,2,1,0:T(8,128)S(1)}, f32[5,2,8,1024]{3,2,1,0:T(8,128)S(1)}, u32[]{:S(2)}, u32[]{:S(2)}) collective-permute-start(f32[5,2,8,1024]{3,2,1,0:T(8,128)S(1)} %get-tuple-element.25), channel_id=1, source_target_pairs={{0,1},{1,2},{2,3},{3,4},{4,5},{5,6},{6,7},{7,0},{8,9},{9,10},{10,1... | collective-permute-start | bytes 983048 | tf_op jit(solution)/shard_map/ppermute | solution.py:170
  59.8 14.4 %collective-permute-start.3 = (f32[5,2,8,1024]{3,2,1,0:T(8,128)S(1)}, f32[5,2,8,1024]{3,2,1,0:T(8,128)S(1)}, u32[]{:S(2)}, u32[]{:S(2)}) collective-permute-start(f32[5,2,8,1024]{3,2,1,0:T(8,128)S(1)} %get-tuple-element.26), channel_id=1, source_target_pairs={{1,0},{2,1},{3,2},{4,3},{5,4},{6,5},{7,6},{0,7},{9,8},{10,9},{11,1... | collective-permute-start | bytes 983048 | tf_op jit(solution)/shard_map/ppermute | solution.py:171
  78.3 19.7 %collective-permute-start.4 = (f32[5,4,8,1024]{3,2,1,0:T(8,128)S(1)}, f32[5,4,8,1024]{3,2,1,0:T(8,128)S(1)}, u32[]{:S(2)}, u32[]{:S(2)}) collective-permute-start(f32[5,4,8,1024]{3,2,1,0:T(8,128)S(1)} %get-tuple-element.28), channel_id=1, source_target_pairs={{0,8},{8,16},{16,24},{24,32},{32,40},{40,48},{48,56},{56,64},{64,7... | collective-permute-start | bytes 1966088 | tf_op jit(solution)/shard_map/ppermute | solution.py:168
  81.8 16.9 %collective-permute-start.5 = (f32[5,4,8,1024]{3,2,1,0:T(8,128)S(1)}, f32[5,4,8,1024]{3,2,1,0:T(8,128)S(1)}, u32[]{:S(2)}, u32[]{:S(2)}) collective-permute-start(f32[5,4,8,1024]{3,2,1,0:T(8,128)S(1)} %get-tuple-element.29), channel_id=1, source_target_pairs={{8,0},{16,8},{24,16},{32,24},{40,32},{48,40},{56,48},{64,56},{72,6... | collective-permute-start | bytes 1966088 | tf_op jit(solution)/shard_map/ppermute | solution.py:169
  83.1 14.9 %collective-permute-start.6 = (f32[5,2,8,1024]{3,2,1,0:T(8,128)S(1)}, f32[5,2,8,1024]{3,2,1,0:T(8,128)S(1)}, u32[]{:S(2)}, u32[]{:S(2)}) collective-permute-start(f32[5,2,8,1024]{3,2,1,0:T(8,128)S(1)} %get-tuple-element.30), channel_id=1, source_target_pairs={{0,1},{1,2},{2,3},{3,4},{4,5},{5,6},{6,7},{7,0},{8,9},{9,10},{10,1... | collective-permute-start | bytes 983048 | tf_op jit(solution)/shard_map/ppermute | solution.py:170
  83.1 14.9 %collective-permute-start.7 = (f32[5,2,8,1024]{3,2,1,0:T(8,128)S(1)}, f32[5,2,8,1024]{3,2,1,0:T(8,128)S(1)}, u32[]{:S(2)}, u32[]{:S(2)}) collective-permute-start(f32[5,2,8,1024]{3,2,1,0:T(8,128)S(1)} %get-tuple-element.31), channel_id=1, source_target_pairs={{1,0},{2,1},{3,2},{4,3},{5,4},{6,5},{7,6},{0,7},{9,8},{10,9},{11,1... | collective-permute-start | bytes 983048 | tf_op jit(solution)/shard_map/ppermute | solution.py:171
  103.0 9.8 %copy-start = (f32[256,128]{1,0:T(8,128)S(1)}, f32[256,128]{1,0:T(8,128)}, u32[]{:S(2)}) copy-start(f32[256,128]{1,0:T(8,128)} %table_ref.1) | copy-start | bytes 393220
  103.0 44.2 %all-to-all-start.1 = ((f32[16,40,8,128]{3,2,1,0:T(8,128)}), f32[16,40,8,128]{3,2,1,0:T(8,128)S(1)}, u32[]{:S(2)}, u32[]{:S(2)}) async-start(f32[16,40,8,128]{3,2,1,0:T(8,128)} %get-tuple-element.32), calls=%async_computation.1 | async-start | bytes 5242880 | tf_op jit(solution)/shard_map/all_to_all | solution.py:481
  117.3 1.3 collective-permute-start.8
  118.6 3.9 %collective-permute-start.9 = (f32[64,128]{1,0:T(8,128)S(1)}, f32[64,128]{1,0:T(8,128)S(1)}, u32[]{:S(2)}, u32[]{:S(2)}) collective-permute-start(f32[64,128]{1,0:T(8,128)S(1)} %add.9), channel_id=1, source_target_pairs={{0,2},{1,3},{2,0},{3,1},{4,6},{5,7},{6,4},{7,5},{8,10},{9,11},{10,... | collective-permute-start | bytes 98312 | tf_op jit(solution)/shard_map/ppermute | solution.py:450
  122.5 5.4 %collective-permute-start.10 = (f32[64,128]{1,0:T(8,128)S(1)}, f32[64,128]{1,0:T(8,128)S(1)}, u32[]{:S(2)}, u32[]{:S(2)}) collective-permute-start(f32[64,128]{1,0:T(8,128)S(1)} %add.10), channel_id=1, source_target_pairs={{0,4},{1,5},{2,6},{3,7},{4,0},{5,1},{6,2},{7,3},{8,12},{9,13},{10,... | collective-permute-start | bytes 98312 | tf_op jit(solution)/shard_map/ppermute | solution.py:450
  128.0 8.3 %collective-permute-start.11 = (f32[32,128]{1,0:T(8,128)S(1)}, f32[32,128]{1,0:T(8,128)S(1)}, u32[]{:S(2)}, u32[]{:S(2)}) collective-permute-start(f32[32,128]{1,0:T(8,128)S(1)} %slice.32), channel_id=1, source_target_pairs={{0,64},{1,65},{2,66},{3,67},{4,68},{5,69},{6,70},{7,71}} | collective-permute-start | bytes 49160 | tf_op jit(solution)/shard_map/ppermute | solution.py:455
  136.3 2.6 %collective-permute-start.12 = (f32[16,128]{1,0:T(8,128)S(1)}, f32[16,128]{1,0:T(8,128)S(1)}, u32[]{:S(2)}, u32[]{:S(2)}) collective-permute-start(f32[16,128]{1,0:T(8,128)S(1)} %slice.34), channel_id=1, source_target_pairs={{0,32},{64,96},{1,33},{65,97},{2,34},{66,98},{3,35},{67,99},{4,36}... | collective-permute-start | bytes 24584 | tf_op jit(solution)/shard_map/ppermute | solution.py:455
  138.9 2.6 %collective-permute-start.13 = (f32[8,128]{1,0:T(8,128)S(1)}, f32[8,128]{1,0:T(8,128)S(1)}, u32[]{:S(2)}, u32[]{:S(2)}) collective-permute-start(f32[8,128]{1,0:T(8,128)S(1)} %slice.36), channel_id=1, source_target_pairs={{0,16},{32,48},{64,80},{96,112},{1,17},{33,49},{65,81},{97,113},{2... | collective-permute-start | bytes 12296 | tf_op jit(solution)/shard_map/ppermute | solution.py:455
  141.5 2.6 %collective-permute-start.14 = (f32[4,128]{1,0:T(4,128)S(1)}, f32[4,128]{1,0:T(4,128)S(1)}, u32[]{:S(2)}, u32[]{:S(2)}) collective-permute-start(f32[4,128]{1,0:T(4,128)S(1)} %slice.30), channel_id=1, source_target_pairs={{0,8},{16,24},{32,40},{48,56},{64,72},{80,88},{96,104},{112,120},{... | collective-permute-start | bytes 6152 | tf_op jit(solution)/shard_map/ppermute | solution.py:455

commit v3 on v2

--- a/solution.py
+++ b/solution.py
@@ -21,6 +21,8 @@
 middle = (1.5, 0.0, 0.0, 0.0, 5.0)
 near = 8.0 / 12.0
 far = 1.0 / 12.0
+
+SNAKE = tuple(g if (g // 4) % 2 == 0 else 4 * (g // 4) + 3 - g % 4 for g in range(16))
 
 f32 = jnp.float32
 bf16 = jnp.bfloat16
@@ -76,7 +78,8 @@
             low = raw[f, pl.ds(zp, XB, stride=ZB), :]
             high = raw[f, pl.ds(zp + 8, XB, stride=ZB), :]
             tile = jnp.concatenate([low, high], axis=0).T
-            tiles[f, :, zp] = tile.reshape(16, YB, LANES)
+            for peer in range(16):
+                tiles[f, peer, zp] = tile[SNAKE[peer] * YB : SNAKE[peer] * YB + YB]
         store = pltpu.make_async_copy(tiles.at[f], out_hbm.at[:, f * 8 : f * 8 + 8], out_sem.at[f])
         store.start()
         stores.append(store)
@@ -162,8 +165,8 @@
 
 
 def exchange(up, down, right, left):
-    ahead = [(g, g + 1) for g in range(15)]
-    back = [(g + 1, g) for g in range(15)]
+    ahead = [(SNAKE[b], SNAKE[b + 1]) for b in range(15)]
+    back = [(SNAKE[b + 1], SNAKE[b]) for b in range(15)]
     return (
         lax.ppermute(up, "gx", ahead),
         lax.ppermute(down, "gx", back),
@@ -227,9 +230,9 @@
 
 def inner_kernel(second, *refs):
     if second:
-        whole_ref, base_ref, metric_ref, d_ref, s_ref, out_ref, q_ref, fhi_ref, flo_ref = refs
+        whole_ref, base_ref, metric_ref, d_ref, s_ref, out_ref, q_ref, fhi_ref, flo_ref, slope_ref = refs
     else:
-        whole_ref, metric_ref, d_ref, s_ref, out_ref, q_ref, fhi_ref, flo_ref = refs
+        whole_ref, metric_ref, d_ref, s_ref, out_ref, q_ref, fhi_ref, flo_ref, slope_ref = refs
     step = pl.program_id(0)
 
     @pl.when(step == 0)
@@ -250,6 +253,17 @@
 
         lax.fori_loop(0, 8, part, 0)
 
+    wide = pl.ds(pl.multiple_of(step * WIDE, WIDE), WIDE)
+    for c in range(WIDE // LANES):
+        lanes = pl.ds(pl.multiple_of(step * WIDE + c * LANES, LANES), LANES)
+        q = [whole_ref[f, :, :, lanes] for f in range(5)]
+        inverse = 1.0 / q[0]
+        pressure = pressure_of(q, inverse)
+        normal = flux(q, pressure, inverse, 1)
+        span = flux(q, pressure, inverse, 2)
+        for f in range(5):
+            slope_ref[f, :, :, c * LANES : c * LANES + LANES] = inner_slopes(q, f, normal, span)
+
     dot = functools.partial(
         lax.dot_general,
         dimension_numbers=(((1,), (1,)), ((), ())),
@@ -270,24 +284,11 @@
         part = part + middle[f] * sums if middle[f] else part
         out_ref[f] = part.reshape(ZB, YB, WIDE)
 
-    def finish(c, carry):
-        near_lanes = pl.ds(pl.multiple_of(c * LANES, LANES), LANES)
-        lanes = pl.ds(pl.multiple_of(step * WIDE + c * LANES, LANES), LANES)
-        q = [whole_ref[f, :, :, lanes] for f in range(5)]
-        inverse = 1.0 / q[0]
-        pressure = pressure_of(q, inverse)
-        normal = flux(q, pressure, inverse, 1)
-        span = flux(q, pressure, inverse, 2)
-        scale = time_step * metric_ref[:, :, near_lanes]
-        for f in range(5):
-            total = out_ref[f, :, :, near_lanes] - inner_slopes(q, f, normal, span)
-            value = q[f] + scale * total
-            if second:
-                value = 0.5 * base_ref[f, :, :, near_lanes] + 0.5 * value
-            out_ref[f, :, :, near_lanes] = value
-        return carry
-
-    lax.fori_loop(0, WIDE // LANES, finish, 0)
+    for f in range(5):
+        value = whole_ref[f, :, :, wide] + time_step * metric_ref[...] * (out_ref[f] - slope_ref[f])
+        if second:
+            value = 0.5 * base_ref[f] + 0.5 * value
+        out_ref[f] = value
 
 
 def inner(state, metric, deriv, smooth, base=None):
@@ -302,7 +303,7 @@
         out_shape=shaped(5, ZB, YB, 1024),
         in_specs=[whole] + ([part] if second else []) + [cell, matrix, matrix],
         out_specs=part,
-        scratch_shapes=[pltpu.VMEM((640, 1024), bf16)] * 3,
+        scratch_shapes=[pltpu.VMEM((640, 1024), bf16)] * 3 + [pltpu.VMEM((5, ZB, YB, WIDE), f32)],
         compiler_params=grant(26),
         cost_estimate=cost(8 * 640 * 1024 * 1024, 14000000),
         name="inner2" if second else "inner1",
@@ -367,7 +368,7 @@
     stores = []
     for f in range(5):
         for zp in range(8):
-            tile = in_ref[:, f * 8 + zp].reshape(LANES, LANES).T
+            tile = jnp.concatenate([in_ref[SNAKE[b], f * 8 + zp] for b in range(16)], axis=0).T
             flat[f, pl.ds(zp, XB, stride=ZB), :] = tile[0:HALF]
             flat[f, pl.ds(zp + 8, XB, stride=ZB), :] = tile[HALF:LANES]
         store = pltpu.make_async_copy(flat.at[f], targets[f], sem.at[f])

time: 151 us -> 145 us (0.960); the launches traced: 149 us -> 145 us
  starting transfers between devices: 37.7 us -> 31.2 us
  waiting for transfers between devices: 17.5 us -> 21.2 us
  Pallas kernels: 43.4 us -> 41.8 us
    all_to_all x1, starting transfers between devices: 9.79 us -> 4.31 us  [body(): lax.all_to_all(returning, 'gx', split_axis=0, concat_axis=0, tiled=True)]
    ppermute x4, waiting for transfers between devices: 6.87 us -> 8.57 us  [spread_forces(): lax.ppermute(held[half:], 'gx', [(g, g + bit) for g in range(0, 16, 2 * b...]
    ppermute x2, waiting for transfers between devices: 1.84 us -> 3.4 us  [exchange(): lax.ppermute(down, 'gx', back)]
    pallas_call x2, Pallas kernels: 23.4 us -> 21.9 us  [inner(): pl.pallas_call(functools.partial(inner_kernel, second), grid=(1024 // WID...]
  transfers between devices with their start and end apart: 16 -> 16, of which waited for: 10 -> 10; matrix products, arithmetic and copies ran while one was open for 0% -> 0% of each run, Pallas kernels for 19% -> 18%
where the time goes in v3:
time: 145 us
  blocking collectives  48.8 us (34%)
  Pallas kernels  41.8 us (29%)
  starting transfers between devices  31.2 us (22%)
  waiting for transfers between devices  21.2 us (15%)
    all_to_all x1, blocking collectives, body(): lax.all_to_all(outgoing, 'gx', split_axis=0, concat_axis=0, tiled=True)  48.8 us
    pallas_call x2, Pallas kernels, inner(): pl.pallas_call(functools.partial(inner_kernel, second), grid=(1024 // WID...  21.9 us
    ppermute x4, starting transfers between devices, spread_forces(): lax.ppermute(held[half:], 'gx', [(g, g + bit) for g in range(0, 16, 2 * b...  9.17 us
    ppermute x4, waiting for transfers between devices, spread_forces(): lax.ppermute(held[half:], 'gx', [(g, g + bit) for g in range(0, 16, 2 * b...  8.57 us
    ppermute x3, waiting for transfers between devices, spread_forces(): held = held + lax.ppermute(held, 'gz', [(g, g ^ bit) for g in range(8)])  6.6 us
    ppermute x2, starting transfers between devices, exchange(): lax.ppermute(left, 'gz', [((g + 1) % 8, g) for g in range(8)])  5.89 us
    ppermute x2, starting transfers between devices, exchange(): lax.ppermute(up, 'gx', ahead)  5.19 us
    pallas_call x1, Pallas kernels, forces(): pl.pallas_call(forces_kernel, out_shape=shaped(NP, LANES), in_specs=[vm]...  4.55 us
  transfers between devices with their start and end apart: 16, of which 10 were waited for; matrix products, arithmetic and copies ran while one was open for 0% of the time, Pallas kernels for 18%

profile of v3, /device:TPU:0, one launch (start us, length us, event | category | flops | bytes accessed | tf_op | source)
XLA Modules:
  0.0 144.5 jit_solution(5089173666515915434)
XLA Ops:
  0.6 4.0 %pack.1 = f32[16,49,8,128]{3,2,1,0:T(8,128)} custom-call(f32[1024,128]{1,0:T(8,128)} %bitcast.10, f32[3,1024,128]{2,1,0:T(8,128)} %bitcast.9, f32[1024,128]{1,0:T(8,128)} %bitcast.11, f32[1024,128]{1,0:T(8,128)} %bitcast.12, s32[16,64]{1,0:T(8,128)} %bitcast.13, s32[16,64]{1,0:T(8,128)} %bitcast.14), custom_call_target="tpu_custom_call" | custom-call | flops 1000000 | bytes 6400000 | tf_op jit(solution)/shard_map/pack/pallas_call | solution.py:93
  4.7 48.8 %all_to_all.10.in_ref = f32[16,49,8,128]{3,2,1,0:T(8,128)S(1)} all-to-all(f32[16,49,8,128]{3,2,1,0:T(8,128)} %pack.1), channel_id=1, replica_groups=mesh['gx'=16,'gz'=8] {'gx'}, dimensions={0} | all-to-all | bytes 6422528 | tf_op jit(solution)/shard_map/all_to_all | solution.py:474
  53.5 2.5 %unpack.1 = (f32[5,16,8,1024]{3,2,1,0:T(8,128)S(1)}, f32[16,8,1024]{2,1,0:T(8,128)S(1)}, f32[16,1024]{1,0:T(8,128)S(1)}, f32[5,4,8,1024]{3,2,1,0:T(8,128)S(1)}, ...) custom-call(f32[16,49,8,128]{3,2,1,0:T(8,128)S(1)} %all_to_all.10.in_ref), custom_call_target="tpu_custom_call" | custom-call | flops 10000000 | bytes 8000000 | tf_op jit(solution)/shard_map/unpack/pallas_call | solution.py:199
  56.0 2.5 %collective-permute-start = (f32[5,4,8,1024]{3,2,1,0:T(8,128)S(1)}, f32[5,4,8,1024]{3,2,1,0:T(8,128)S(1)}, u32[]{:S(2)}, u32[]{:S(2)}) collective-permute-start(f32[5,4,8,1024]{3,2,1,0:T(8,128)S(1)} %get-tuple-element.23), channel_id=1, source_target_pairs={{0,8},{8,16},{16,24},{24,56},{56,48},{48,40},{40,32},{32,64},{64,7... | collective-permute-start | bytes 1966088 | tf_op jit(solution)/shard_map/ppermute | solution.py:171
  59.8 2.9 %collective-permute-start.3 = (f32[5,2,8,1024]{3,2,1,0:T(8,128)S(1)}, f32[5,2,8,1024]{3,2,1,0:T(8,128)S(1)}, u32[]{:S(2)}, u32[]{:S(2)}) collective-permute-start(f32[5,2,8,1024]{3,2,1,0:T(8,128)S(1)} %get-tuple-element.26), channel_id=1, source_target_pairs={{1,0},{2,1},{3,2},{4,3},{5,4},{6,5},{7,6},{0,7},{9,8},{10,9},{11,1... | collective-permute-start | bytes 983048 | tf_op jit(solution)/shard_map/ppermute | solution.py:174
  62.8 10.7 %inner1.1.part_ref = f32[5,16,8,1024]{3,2,1,0:T(8,128)S(1)} custom-call(f32[5,16,8,1024]{3,2,1,0:T(8,128)S(1)} %get-tuple-element.21.refs_0_.refs_1_, f32[16,8,1024]{2,1,0:T(8,128)S(1)} %get-tuple-element.22.refs_1_.metric_ref.refs_2_, f32[1024,1024]{1,0:T(8,128)S(1)} %copy-done.1, f32[1024,1024]{1,0:T(8,128)S(1)} %copy-done.2), custom_call_target="tpu_custom_call" | custom-call | flops 5368709120 | bytes 14000000 | tf_op jit(solution)/shard_map/inner1/pallas_call | solution.py:300
  73.5 1.9 %collective-permute-done.1.down = f32[5,4,8,1024]{3,2,1,0:T(8,128)S(1)} collective-permute-done((f32[5,4,8,1024]{3,2,1,0:T(8,128)S(1)}, f32[5,4,8,1024]{3,2,1,0:T(8,128)S(1)}, u32[]{:S(2)}, u32[]{:S(2)}) %collective-permute-start.1) | collective-permute-done | bytes 655392 | tf_op jit(solution)/shard_map/ppermute | solution.py:172
  75.5 2.9 %first.1 = (f32[5,16,8,1024]{3,2,1,0:T(8,128)S(1)}, f32[5,4,8,1024]{3,2,1,0:T(8,128)S(1)}, f32[5,4,8,1024]{3,2,1,0:T(8,128)S(1)}, f32[5,2,8,1024]{3,2,1,0:T(8,128)S(1)}, f32[5,2,8,1024]{3,2,1,0:T(8,128)S(1)}) custom-call(f32[5,16,8,1024]{3,2,1,0:T(8,128)S(1)} %inner1.1.part_ref, f32[16,8,1024]{2,1,0:T(8,128)S(1)} %get-tuple-element.22.refs_1_.metric_ref.refs_2_, ...), custom_call_target="tpu_custom_call" | custom-call | flops 10000000 | bytes 9000000 | tf_op jit(solution)/shard_map/first/pallas_call | solution.py:326
  78.3 2.7 %collective-permute-start.4 = (f32[5,4,8,1024]{3,2,1,0:T(8,128)S(1)}, f32[5,4,8,1024]{3,2,1,0:T(8,128)S(1)}, u32[]{:S(2)}, u32[]{:S(2)}) collective-permute-start(f32[5,4,8,1024]{3,2,1,0:T(8,128)S(1)} %get-tuple-element.28), channel_id=1, source_target_pairs={{0,8},{8,16},{16,24},{24,56},{56,48},{48,40},{40,32},{32,64},{64,7... | collective-permute-start | bytes 1966088 | tf_op jit(solution)/shard_map/ppermute | solution.py:171
  82.3 2.9 %collective-permute-start.7 = (f32[5,2,8,1024]{3,2,1,0:T(8,128)S(1)}, f32[5,2,8,1024]{3,2,1,0:T(8,128)S(1)}, u32[]{:S(2)}, u32[]{:S(2)}) collective-permute-start(f32[5,2,8,1024]{3,2,1,0:T(8,128)S(1)} %get-tuple-element.31), channel_id=1, source_target_pairs={{1,0},{2,1},{3,2},{4,3},{5,4},{6,5},{7,6},{0,7},{9,8},{10,9},{11,1... | collective-permute-start | bytes 983048 | tf_op jit(solution)/shard_map/ppermute | solution.py:174
  85.3 11.1 %inner2.1.part_ref = f32[5,16,8,1024]{3,2,1,0:T(8,128)S(1)} custom-call(f32[5,16,8,1024]{3,2,1,0:T(8,128)S(1)} %get-tuple-element.27.refs_0_, f32[5,16,8,1024]{3,2,1,0:T(8,128)S(1)} %get-tuple-element.21.refs_0_.refs_1_, f32[16,8,1024]{2,1,0:T(8,128)S(1)} %get-tuple-element.22.refs_1_.metric_ref.refs_2_, f32[1024,1024]{1,0:T(8,128)S(1)} %copy-done.1, ...), custom_call_target="tpu_custom_call" | custom-call | flops 5368709120 | bytes 14000000 | tf_op jit(solution)/shard_map/inner2/pallas_call | solution.py:300
  96.4 1.5 %collective-permute-done.5.down = f32[5,4,8,1024]{3,2,1,0:T(8,128)S(1)} collective-permute-done((f32[5,4,8,1024]{3,2,1,0:T(8,128)S(1)}, f32[5,4,8,1024]{3,2,1,0:T(8,128)S(1)}, u32[]{:S(2)}, u32[]{:S(2)}) %collective-permute-start.5) | collective-permute-done | bytes 655392 | tf_op jit(solution)/shard_map/ppermute | solution.py:172
  97.9 4.3 %final.1 = (f32[16,40,8,128]{3,2,1,0:T(8,128)}, f32[16,8,1024]{2,1,0:T(8,128)S(1)}) custom-call(f32[5,16,8,1024]{3,2,1,0:T(8,128)S(1)} %inner2.1.part_ref, f32[16,8,1024]{2,1,0:T(8,128)S(1)} %get-tuple-element.22.refs_1_.metric_ref.refs_2_, f32[5,4,8,1024]{3,2,1,0:T(8,128)S(1)} %collective-permute-done.4.up, ...), custom_call_target="tpu_custom_call" | custom-call | flops 10000000 | bytes 9000000 | tf_op jit(solution)/shard_map/final/pallas_call | solution.py:354
  102.2 4.3 %all-to-all-start.1 = ((f32[16,40,8,128]{3,2,1,0:T(8,128)}), f32[16,40,8,128]{3,2,1,0:T(8,128)S(1)}, u32[]{:S(2)}, u32[]{:S(2)}) async-start(f32[16,40,8,128]{3,2,1,0:T(8,128)} %get-tuple-element.32), calls=%async_computation.1 | async-start | bytes 5242880 | tf_op jit(solution)/shard_map/all_to_all | solution.py:482
  106.5 4.5 %forces.1 = f32[64,128]{1,0:T(8,128)S(1)} custom-call(f32[16,8,1024]{2,1,0:T(8,128)S(1)} %get-tuple-element.36.load_ref, f32[16,1024]{1,0:T(8,128)S(1)} %get-tuple-element.37.code_ref, f32[256,128]{1,0:T(8,128)S(1)} %copy-done), custom_call_target="tpu_custom_call" | custom-call | flops 134217728 | bytes 700000 | tf_op jit(solution)/shard_map/forces/pallas_call | solution.py:437
  113.7 2.6 %collective-permute-done.9 = f32[64,128]{1,0:T(8,128)S(1)} collective-permute-done((f32[64,128]{1,0:T(8,128)S(1)}, f32[64,128]{1,0:T(8,128)S(1)}, u32[]{:S(2)}, u32[]{:S(2)}) %collective-permute-start.9) | collective-permute-done | bytes 32800 | tf_op jit(solution)/shard_map/ppermute | solution.py:451
  116.3 2.6 %collective-permute-start.10 = (f32[64,128]{1,0:T(8,128)S(1)}, f32[64,128]{1,0:T(8,128)S(1)}, u32[]{:S(2)}, u32[]{:S(2)}) collective-permute-start(f32[64,128]{1,0:T(8,128)S(1)} %add.10), channel_id=1, source_target_pairs={{0,4},{1,5},{2,6},{3,7},{4,0},{5,1},{6,2},{7,3},{8,12},{9,13},{10,... | collective-permute-start | bytes 98312 | tf_op jit(solution)/shard_map/ppermute | solution.py:451
  118.9 2.8 %collective-permute-done.10 = f32[64,128]{1,0:T(8,128)S(1)} collective-permute-done((f32[64,128]{1,0:T(8,128)S(1)}, f32[64,128]{1,0:T(8,128)S(1)}, u32[]{:S(2)}, u32[]{:S(2)}) %collective-permute-start.10) | collective-permute-done | bytes 32800 | tf_op jit(solution)/shard_map/ppermute | solution.py:451
  121.7 5.3 %collective-permute-start.11 = (f32[32,128]{1,0:T(8,128)S(1)}, f32[32,128]{1,0:T(8,128)S(1)}, u32[]{:S(2)}, u32[]{:S(2)}) collective-permute-start(f32[32,128]{1,0:T(8,128)S(1)} %slice.32), channel_id=1, source_target_pairs={{0,64},{1,65},{2,66},{3,67},{4,68},{5,69},{6,70},{7,71}} | collective-permute-start | bytes 49160 | tf_op jit(solution)/shard_map/ppermute | solution.py:456
  127.1 3.3 %collective-permute-done.11 = f32[32,128]{1,0:T(8,128)S(1)} collective-permute-done((f32[32,128]{1,0:T(8,128)S(1)}, f32[32,128]{1,0:T(8,128)S(1)}, u32[]{:S(2)}, u32[]{:S(2)}) %collective-permute-start.11) | collective-permute-done | bytes 16416 | tf_op jit(solution)/shard_map/ppermute | solution.py:456
  131.7 1.3 collective-permute-done.12
  134.4 2.6 %collective-permute-done.13 = f32[8,128]{1,0:T(8,128)S(1)} collective-permute-done((f32[8,128]{1,0:T(8,128)S(1)}, f32[8,128]{1,0:T(8,128)S(1)}, u32[]{:S(2)}, u32[]{:S(2)}) %collective-permute-start.13) | collective-permute-done | bytes 4128 | tf_op jit(solution)/shard_map/ppermute | solution.py:456
  140.1 2.6 %all-to-all-done.1.in_ref = f32[16,40,8,128]{3,2,1,0:T(8,128)S(1)} async-done(((f32[16,40,8,128]{3,2,1,0:T(8,128)}), f32[16,40,8,128]{3,2,1,0:T(8,128)S(1)}, u32[]{:S(2)}, u32[]{:S(2)}) %all-to-all-start.1) | async-done | bytes 2621472 | tf_op jit(solution)/shard_map/all_to_all | solution.py:482
  142.8 1.8 %home.1 = (f32[1024,128]{1,0:T(8,128)}, f32[3,1024,128]{2,1,0:T(8,128)}, f32[1024,128]{1,0:T(8,128)}) custom-call(f32[16,40,8,128]{3,2,1,0:T(8,128)S(1)} %all-to-all-done.1.in_ref), custom_call_target="tpu_custom_call" | custom-call | flops 1000000 | bytes 5300000 | tf_op jit(solution)/shard_map/home/pallas_call | solution.py:384
  (34 shorter events, 11.0 us)
Async XLA Ops:
  4.7 58.1 %copy-start.1 = (f32[1024,1024]{1,0:T(8,128)S(1)}, f32[1024,1024]{1,0:T(8,128)}, u32[]{:S(2)}) copy-start(f32[1024,1024]{1,0:T(8,128)} %refs_3_.3) | copy-start | bytes 12582916
  4.7 58.1 %copy-start.2 = (f32[1024,1024]{1,0:T(8,128)S(1)}, f32[1024,1024]{1,0:T(8,128)}, u32[]{:S(2)}) copy-start(f32[1024,1024]{1,0:T(8,128)} %refs_4_.1) | copy-start | bytes 12582916
  56.0 17.5 %collective-permute-start = (f32[5,4,8,1024]{3,2,1,0:T(8,128)S(1)}, f32[5,4,8,1024]{3,2,1,0:T(8,128)S(1)}, u32[]{:S(2)}, u32[]{:S(2)}) collective-permute-start(f32[5,4,8,1024]{3,2,1,0:T(8,128)S(1)} %get-tuple-element.23), channel_id=1, source_target_pairs={{0,8},{8,16},{16,24},{24,56},{56,48},{48,40},{40,32},{32,64},{64,7... | collective-permute-start | bytes 1966088 | tf_op jit(solution)/shard_map/ppermute | solution.py:171
  58.5 17.0 %collective-permute-start.1 = (f32[5,4,8,1024]{3,2,1,0:T(8,128)S(1)}, f32[5,4,8,1024]{3,2,1,0:T(8,128)S(1)}, u32[]{:S(2)}, u32[]{:S(2)}) collective-permute-start(f32[5,4,8,1024]{3,2,1,0:T(8,128)S(1)} %get-tuple-element.24), channel_id=1, source_target_pairs={{8,0},{16,8},{24,16},{56,24},{48,56},{40,48},{32,40},{64,32},{72,6... | collective-permute-start | bytes 1966088 | tf_op jit(solution)/shard_map/ppermute | solution.py:172
  59.8 13.7 %collective-permute-start.2 = (f32[5,2,8,1024]{3,2,1,0:T(8,128)S(1)}, f32[5,2,8,1024]{3,2,1,0:T(8,128)S(1)}, u32[]{:S(2)}, u32[]{:S(2)}) collective-permute-start(f32[5,2,8,1024]{3,2,1,0:T(8,128)S(1)} %get-tuple-element.25), channel_id=1, source_target_pairs={{0,1},{1,2},{2,3},{3,4},{4,5},{5,6},{6,7},{7,0},{8,9},{9,10},{10,1... | collective-permute-start | bytes 983048 | tf_op jit(solution)/shard_map/ppermute | solution.py:173
  59.8 13.7 %collective-permute-start.3 = (f32[5,2,8,1024]{3,2,1,0:T(8,128)S(1)}, f32[5,2,8,1024]{3,2,1,0:T(8,128)S(1)}, u32[]{:S(2)}, u32[]{:S(2)}) collective-permute-start(f32[5,2,8,1024]{3,2,1,0:T(8,128)S(1)} %get-tuple-element.26), channel_id=1, source_target_pairs={{1,0},{2,1},{3,2},{4,3},{5,4},{6,5},{7,6},{0,7},{9,8},{10,9},{11,1... | collective-permute-start | bytes 983048 | tf_op jit(solution)/shard_map/ppermute | solution.py:174
  78.3 18.1 %collective-permute-start.4 = (f32[5,4,8,1024]{3,2,1,0:T(8,128)S(1)}, f32[5,4,8,1024]{3,2,1,0:T(8,128)S(1)}, u32[]{:S(2)}, u32[]{:S(2)}) collective-permute-start(f32[5,4,8,1024]{3,2,1,0:T(8,128)S(1)} %get-tuple-element.28), channel_id=1, source_target_pairs={{0,8},{8,16},{16,24},{24,56},{56,48},{48,40},{40,32},{32,64},{64,7... | collective-permute-start | bytes 1966088 | tf_op jit(solution)/shard_map/ppermute | solution.py:171
  81.0 16.9 %collective-permute-start.5 = (f32[5,4,8,1024]{3,2,1,0:T(8,128)S(1)}, f32[5,4,8,1024]{3,2,1,0:T(8,128)S(1)}, u32[]{:S(2)}, u32[]{:S(2)}) collective-permute-start(f32[5,4,8,1024]{3,2,1,0:T(8,128)S(1)} %get-tuple-element.29), channel_id=1, source_target_pairs={{8,0},{16,8},{24,16},{56,24},{48,56},{40,48},{32,40},{64,32},{72,6... | collective-permute-start | bytes 1966088 | tf_op jit(solution)/shard_map/ppermute | solution.py:172
  82.3 14.1 %collective-permute-start.6 = (f32[5,2,8,1024]{3,2,1,0:T(8,128)S(1)}, f32[5,2,8,1024]{3,2,1,0:T(8,128)S(1)}, u32[]{:S(2)}, u32[]{:S(2)}) collective-permute-start(f32[5,2,8,1024]{3,2,1,0:T(8,128)S(1)} %get-tuple-element.30), channel_id=1, source_target_pairs={{0,1},{1,2},{2,3},{3,4},{4,5},{5,6},{6,7},{7,0},{8,9},{9,10},{10,1... | collective-permute-start | bytes 983048 | tf_op jit(solution)/shard_map/ppermute | solution.py:173
  82.3 14.1 %collective-permute-start.7 = (f32[5,2,8,1024]{3,2,1,0:T(8,128)S(1)}, f32[5,2,8,1024]{3,2,1,0:T(8,128)S(1)}, u32[]{:S(2)}, u32[]{:S(2)}) collective-permute-start(f32[5,2,8,1024]{3,2,1,0:T(8,128)S(1)} %get-tuple-element.31), channel_id=1, source_target_pairs={{1,0},{2,1},{3,2},{4,3},{5,4},{6,5},{7,6},{0,7},{9,8},{10,9},{11,1... | collective-permute-start | bytes 983048 | tf_op jit(solution)/shard_map/ppermute | solution.py:174
  102.2 4.3 %copy-start = (f32[256,128]{1,0:T(8,128)S(1)}, f32[256,128]{1,0:T(8,128)}, u32[]{:S(2)}) copy-start(f32[256,128]{1,0:T(8,128)} %table_ref.1) | copy-start | bytes 393220
  102.2 40.6 %all-to-all-start.1 = ((f32[16,40,8,128]{3,2,1,0:T(8,128)}), f32[16,40,8,128]{3,2,1,0:T(8,128)S(1)}, u32[]{:S(2)}, u32[]{:S(2)}) async-start(f32[16,40,8,128]{3,2,1,0:T(8,128)} %get-tuple-element.32), calls=%async_computation.1 | async-start | bytes 5242880 | tf_op jit(solution)/shard_map/all_to_all | solution.py:482
  111.1 1.3 collective-permute-start.8
  112.4 3.9 %collective-permute-start.9 = (f32[64,128]{1,0:T(8,128)S(1)}, f32[64,128]{1,0:T(8,128)S(1)}, u32[]{:S(2)}, u32[]{:S(2)}) collective-permute-start(f32[64,128]{1,0:T(8,128)S(1)} %add.9), channel_id=1, source_target_pairs={{0,2},{1,3},{2,0},{3,1},{4,6},{5,7},{6,4},{7,5},{8,10},{9,11},{10,... | collective-permute-start | bytes 98312 | tf_op jit(solution)/shard_map/ppermute | solution.py:451
  116.3 5.4 %collective-permute-start.10 = (f32[64,128]{1,0:T(8,128)S(1)}, f32[64,128]{1,0:T(8,128)S(1)}, u32[]{:S(2)}, u32[]{:S(2)}) collective-permute-start(f32[64,128]{1,0:T(8,128)S(1)} %add.10), channel_id=1, source_target_pairs={{0,4},{1,5},{2,6},{3,7},{4,0},{5,1},{6,2},{7,3},{8,12},{9,13},{10,... | collective-permute-start | bytes 98312 | tf_op jit(solution)/shard_map/ppermute | solution.py:451
  121.7 8.7 %collective-permute-start.11 = (f32[32,128]{1,0:T(8,128)S(1)}, f32[32,128]{1,0:T(8,128)S(1)}, u32[]{:S(2)}, u32[]{:S(2)}) collective-permute-start(f32[32,128]{1,0:T(8,128)S(1)} %slice.32), channel_id=1, source_target_pairs={{0,64},{1,65},{2,66},{3,67},{4,68},{5,69},{6,70},{7,71}} | collective-permute-start | bytes 49160 | tf_op jit(solution)/shard_map/ppermute | solution.py:456
  130.4 2.6 %collective-permute-start.12 = (f32[16,128]{1,0:T(8,128)S(1)}, f32[16,128]{1,0:T(8,128)S(1)}, u32[]{:S(2)}, u32[]{:S(2)}) collective-permute-start(f32[16,128]{1,0:T(8,128)S(1)} %slice.34), channel_id=1, source_target_pairs={{0,32},{64,96},{1,33},{65,97},{2,34},{66,98},{3,35},{67,99},{4,36}... | collective-permute-start | bytes 24584 | tf_op jit(solution)/shard_map/ppermute | solution.py:456
  133.1 3.9 %collective-permute-start.13 = (f32[8,128]{1,0:T(8,128)S(1)}, f32[8,128]{1,0:T(8,128)S(1)}, u32[]{:S(2)}, u32[]{:S(2)}) collective-permute-start(f32[8,128]{1,0:T(8,128)S(1)} %slice.36), channel_id=1, source_target_pairs={{0,16},{32,48},{64,80},{96,112},{1,17},{33,49},{65,81},{97,113},{2... | collective-permute-start | bytes 12296 | tf_op jit(solution)/shard_map/ppermute | solution.py:456
  137.0 2.6 %collective-permute-start.14 = (f32[4,128]{1,0:T(4,128)S(1)}, f32[4,128]{1,0:T(4,128)S(1)}, u32[]{:S(2)}, u32[]{:S(2)}) collective-permute-start(f32[4,128]{1,0:T(4,128)S(1)} %slice.30), channel_id=1, source_target_pairs={{0,8},{16,24},{32,40},{48,56},{64,72},{80,88},{96,104},{112,120},{... | collective-permute-start | bytes 6152 | tf_op jit(solution)/shard_map/ppermute | solution.py:456

commit v4 on v3

--- a/solution.py
+++ b/solution.py
@@ -61,18 +61,29 @@
     return pltpu.roll(v, shift, v.ndim - 2) if shift else v
 
 
-def pack_kernel(d_hbm, m_hbm, e_hbm, g_hbm, panel_ref, shape_ref, out_hbm, raw, tiles, code_ref, in_sem, out_sem):
+def pack_kernel(
+    d_hbm, m_hbm, e_hbm, g_hbm, panel_hbm, shape_hbm, out_hbm, raw, tiles, index, code_ref, in_sem, out_sem
+):
     sources = [d_hbm, m_hbm.at[0], m_hbm.at[1], m_hbm.at[2], e_hbm, g_hbm]
     loads = [pltpu.make_async_copy(sources[f], raw.at[f], in_sem.at[f]) for f in range(6)]
+    loads += [
+        pltpu.make_async_copy(panel_hbm, index.at[0], in_sem.at[6]),
+        pltpu.make_async_copy(shape_hbm, index.at[1], in_sem.at[7]),
+    ]
     for load in loads:
         load.start()
-    turned = (panel_ref[...] * NSHAPE + shape_ref[...]).astype(f32)
-    for peer in range(16):
-        code_ref[peer, :, 0:HALF] = turned[0:8]
-        code_ref[peer, :, HALF:LANES] = turned[8:16]
-    stores = [pltpu.make_async_copy(code_ref, out_hbm.at[:, 48], out_sem.at[6])]
-    stores[0].start()
+    stores = []
     for f in range(6):
+        if f == 5:
+            loads[6].wait()
+            loads[7].wait()
+            turned = (index[0] * NSHAPE + index[1]).astype(f32)
+            for peer in range(16):
+                code_ref[peer, :, 0:HALF] = turned[0:8]
+                code_ref[peer, :, HALF:LANES] = turned[8:16]
+            store = pltpu.make_async_copy(code_ref, out_hbm.at[:, 48], out_sem.at[6])
+            store.start()
+            stores.append(store)
         loads[f].wait()
         for zp in range(8):
             low = raw[f, pl.ds(zp, XB, stride=ZB), :]
@@ -88,18 +99,18 @@
 
 
 def pack(density, momentum, energy, metric, panels, shapes):
-    vm = pl.BlockSpec(memory_space=pltpu.VMEM)
     hbm = pl.BlockSpec(memory_space=pl.ANY)
     return pl.pallas_call(
         pack_kernel,
         out_shape=shaped(16, 49, YB, LANES),
-        in_specs=[hbm] * 4 + [vm] * 2,
+        in_specs=[hbm] * 6,
         out_specs=hbm,
         scratch_shapes=[
             pltpu.VMEM((6, XB * ZB, LANES), f32),
             pltpu.VMEM((6, 16, 8, YB, LANES), f32),
+            pltpu.VMEM((2, ZB, XB), jnp.int32),
             pltpu.VMEM((16, YB, LANES), f32),
-            pltpu.SemaphoreType.DMA((6,)),
+            pltpu.SemaphoreType.DMA((8,)),
             pltpu.SemaphoreType.DMA((7,)),
         ],
         compiler_params=pltpu.CompilerParams(),
@@ -143,12 +154,30 @@
 
 
 edge_shapes = [shaped(5, 4, YB, 1024)] * 2 + [shaped(5, 2, YB, 1024)] * 2
-yedge_spec = pl.BlockSpec((5, 4, YB, LANES), lambda s: (0, 0, 0, s))
-zedge_spec = pl.BlockSpec((5, 2, YB, LANES), lambda s: (0, 0, 0, s))
+STEPS = 2
+STRIP = 1024 // STEPS
+PARTS = STRIP // LANES
+yedge_spec = pl.BlockSpec((5, 4, YB, STRIP), lambda s: (0, 0, 0, s))
+zedge_spec = pl.BlockSpec((5, 2, YB, STRIP), lambda s: (0, 0, 0, s))
 edge_specs = [yedge_spec] * 2 + [zedge_spec] * 2
-line_spec = pl.BlockSpec((5, ZB, YB, LANES), lambda s: (0, 0, 0, s))
-cell_spec = pl.BlockSpec((ZB, YB, LANES), lambda s: (0, 0, s))
-code_spec = pl.BlockSpec((ZB, LANES), lambda s: (0, s))
+line_spec = pl.BlockSpec((5, ZB, YB, STRIP), lambda s: (0, 0, 0, s))
+cell_spec = pl.BlockSpec((ZB, YB, STRIP), lambda s: (0, 0, s))
+code_spec = pl.BlockSpec((ZB, STRIP), lambda s: (0, s))
+
+
+def by_lanes(kernel, packed_at=None):
+    def run(*refs):
+        for c in range(PARTS):
+            lanes = pl.ds(c * LANES, LANES)
+            views = []
+            for i, ref in enumerate(refs):
+                if i == packed_at:
+                    views.append(ref.at[pl.ds(2 * c, 2)])
+                else:
+                    views.append(ref.at[(slice(None),) * (len(ref.shape) - 1) + (lanes,)])
+            kernel(*views)
+
+    return run
 
 
 def missing(f, z, up_ref, down_ref, right_ref, left_ref):
@@ -197,10 +226,10 @@
 
 def unpack(packed):
     return pl.pallas_call(
-        unpack_kernel,
-        grid=(8,),
+        by_lanes(unpack_kernel, 0),
+        grid=(STEPS,),
         out_shape=[shaped(5, ZB, YB, 1024), shaped(ZB, YB, 1024), shaped(ZB, 1024), *edge_shapes],
-        in_specs=[pl.BlockSpec((2, 49, YB, LANES), lambda s: (s, 0, 0, 0))],
+        in_specs=[pl.BlockSpec((2 * PARTS, 49, YB, LANES), lambda s: (s, 0, 0, 0))],
         out_specs=[line_spec, cell_spec, code_spec, *edge_specs],
         compiler_params=grant(16),
         cost_estimate=cost(10000000, 8000000),
@@ -230,9 +259,9 @@
 
 def inner_kernel(second, *refs):
     if second:
-        whole_ref, base_ref, metric_ref, d_ref, s_ref, out_ref, q_ref, fhi_ref, flo_ref, slope_ref = refs
+        whole_ref, base_ref, metric_ref, d_ref, s_ref, out_ref, q_ref, fhi_ref, flo_ref, slope_ref, x_ref = refs
     else:
-        whole_ref, metric_ref, d_ref, s_ref, out_ref, q_ref, fhi_ref, flo_ref, slope_ref = refs
+        whole_ref, metric_ref, d_ref, s_ref, out_ref, q_ref, fhi_ref, flo_ref, slope_ref, x_ref = refs
     step = pl.program_id(0)
 
     @pl.when(step == 0)
@@ -269,10 +298,10 @@
         dimension_numbers=(((1,), (1,)), ((), ())),
         preferred_element_type=f32,
     )
-    deriv = d_ref[...]
+    deriv = d_ref[wide, :]
     dhi = deriv.astype(bf16)
     dlo = (deriv - dhi.astype(f32)).astype(bf16)
-    smooth = s_ref[...]
+    smooth = s_ref[wide, :]
     shi = smooth.astype(bf16)
     slo = (smooth - shi.astype(f32)).astype(bf16)
     ones = jnp.ones((16, 1024), bf16)
@@ -282,28 +311,26 @@
     for f in range(5):
         part = stream[f * 128 : f * 128 + 128]
         part = part + middle[f] * sums if middle[f] else part
-        out_ref[f] = part.reshape(ZB, YB, WIDE)
-
-    for f in range(5):
-        value = whole_ref[f, :, :, wide] + time_step * metric_ref[...] * (out_ref[f] - slope_ref[f])
+        x_ref[f] = part.reshape(ZB, YB, WIDE)
+
+    for f in range(5):
+        scale = time_step * metric_ref[:, :, wide]
+        value = whole_ref[f, :, :, wide] + scale * (x_ref[f] - slope_ref[f])
         if second:
-            value = 0.5 * base_ref[f] + 0.5 * value
-        out_ref[f] = value
+            value = 0.5 * base_ref[f, :, :, wide] + 0.5 * value
+        out_ref[f, :, :, wide] = value
 
 
 def inner(state, metric, deriv, smooth, base=None):
     second = base is not None
-    whole = pl.BlockSpec((5, ZB, YB, 1024), lambda n: (0, 0, 0, 0))
-    part = pl.BlockSpec((5, ZB, YB, WIDE), lambda n: (0, 0, 0, n))
-    cell = pl.BlockSpec((ZB, YB, WIDE), lambda n: (0, 0, n))
-    matrix = pl.BlockSpec((WIDE, 1024), lambda n: (n, 0))
+    whole = pl.BlockSpec(memory_space=pltpu.VMEM)
     return pl.pallas_call(
         functools.partial(inner_kernel, second),
         grid=(1024 // WIDE,),
         out_shape=shaped(5, ZB, YB, 1024),
-        in_specs=[whole] + ([part] if second else []) + [cell, matrix, matrix],
-        out_specs=part,
-        scratch_shapes=[pltpu.VMEM((640, 1024), bf16)] * 3 + [pltpu.VMEM((5, ZB, YB, WIDE), f32)],
+        in_specs=[whole] * (5 if second else 4),
+        out_specs=whole,
+        scratch_shapes=[pltpu.VMEM((640, 1024), bf16)] * 3 + [pltpu.VMEM((5, ZB, YB, WIDE), f32)] * 2,
         compiler_params=grant(26),
         cost_estimate=cost(8 * 640 * 1024 * 1024, 14000000),
         name="inner2" if second else "inner1",
@@ -324,8 +351,8 @@
 
 def first_section(part, metric, halos):
     return pl.pallas_call(
-        first_kernel,
-        grid=(8,),
+        by_lanes(first_kernel),
+        grid=(STEPS,),
         out_shape=[shaped(5, ZB, YB, 1024), *edge_shapes],
         in_specs=[line_spec, cell_spec, *edge_specs],
         out_specs=[line_spec, *edge_specs],
@@ -352,11 +379,11 @@
 
 def final_section(part, metric, halos):
     return pl.pallas_call(
-        final_kernel,
-        grid=(8,),
+        by_lanes(final_kernel, 6),
+        grid=(STEPS,),
         out_shape=[pltpu.HBM((16, 40, YB, LANES), f32), shaped(ZB, YB, 1024)],
         in_specs=[line_spec, cell_spec, *edge_specs],
-        out_specs=[pl.BlockSpec((2, 40, YB, LANES), lambda s: (s, 0, 0, 0)), cell_spec],
+        out_specs=[pl.BlockSpec((2 * PARTS, 40, YB, LANES), lambda s: (s, 0, 0, 0)), cell_spec],
         compiler_params=grant(16),
         cost_estimate=cost(10000000, 9000000),
         name="final",

time: 145 us -> 140 us (0.966)
  Pallas kernels: 41.8 us -> 37.2 us
    pallas_call x3, Pallas kernels: 9.63 us -> 6.29 us  [the longest x1 2.44 us: final_section(): pl.pallas_call(by_lanes(final_kernel, 6), grid=(STEPS,), out_shape=[pltpu...]
where the time goes in v4:
time: 140 us
  blocking collectives  48.8 us (35%)
  Pallas kernels  37.2 us (27%)
  starting transfers between devices  31.2 us (22%)
  waiting for transfers between devices  21.4 us (15%)
    all_to_all x1, blocking collectives, body(): lax.all_to_all(outgoing, 'gx', split_axis=0, concat_axis=0, tiled=True)  48.8 us
    pallas_call x2, Pallas kernels, inner(): pl.pallas_call(functools.partial(inner_kernel, second), grid=(1024 // WID...  21.2 us
    ppermute x4, starting transfers between devices, spread_forces(): lax.ppermute(held[half:], 'gx', [(g, g + bit) for g in range(0, 16, 2 * b...  9.17 us
    ppermute x4, waiting for transfers between devices, spread_forces(): lax.ppermute(held[half:], 'gx', [(g, g + bit) for g in range(0, 16, 2 * b...  8.5 us
    ppermute x3, waiting for transfers between devices, spread_forces(): held = held + lax.ppermute(held, 'gz', [(g, g ^ bit) for g in range(8)])  6.31 us
    ppermute x2, starting transfers between devices, exchange(): lax.ppermute(left, 'gz', [((g + 1) % 8, g) for g in range(8)])  5.89 us
    ppermute x2, starting transfers between devices, exchange(): lax.ppermute(up, 'gx', ahead)  5.02 us
    pallas_call x1, Pallas kernels, forces(): pl.pallas_call(forces_kernel, out_shape=shaped(NP, LANES), in_specs=[vm]...  4.55 us
  transfers between devices with their start and end apart: 16, of which 10 were waited for; matrix products, arithmetic and copies ran while one was open for 0% of the time, Pallas kernels for 18%

profile of v4, /device:TPU:0, one launch (start us, length us, event | category | flops | bytes accessed | tf_op | source)
XLA Modules:
  0.0 140.1 jit_solution(9470769267600125039)
XLA Ops:
  0.6 3.4 %pack.1 = f32[16,49,8,128]{3,2,1,0:T(8,128)} custom-call(f32[1024,128]{1,0:T(8,128)} %bitcast.10, f32[3,1024,128]{2,1,0:T(8,128)} %bitcast.9, f32[1024,128]{1,0:T(8,128)} %bitcast.11, f32[1024,128]{1,0:T(8,128)} %bitcast.12, s32[16,64]{1,0:T(8,128)} %bitcast.13, s32[16,64]{1,0:T(8,128)} %bitcast.14), custom_call_target="tpu_custom_call" | custom-call | flops 1000000 | bytes 6400000 | tf_op jit(solution)/shard_map/pack/pallas_call | solution.py:103
  4.0 48.8 %all_to_all.10.refs_0_ = f32[16,49,8,128]{3,2,1,0:T(8,128)S(1)} all-to-all(f32[16,49,8,128]{3,2,1,0:T(8,128)} %pack.1), channel_id=1, replica_groups=mesh['gx'=16,'gz'=8] {'gx'}, dimensions={0} | all-to-all | bytes 6422528 | tf_op jit(solution)/shard_map/all_to_all | solution.py:501
  52.8 1.7 %unpack.1 = (f32[5,16,8,1024]{3,2,1,0:T(8,128)S(1)}, f32[16,8,1024]{2,1,0:T(8,128)S(1)}, f32[16,1024]{1,0:T(8,128)S(1)}, f32[5,4,8,1024]{3,2,1,0:T(8,128)S(1)}, ...) custom-call(f32[16,49,8,128]{3,2,1,0:T(8,128)S(1)} %all_to_all.10.refs_0_), custom_call_target="tpu_custom_call" | custom-call | flops 10000000 | bytes 8000000 | tf_op jit(solution)/shard_map/unpack/pallas_call | solution.py:228
  54.5 2.5 %collective-permute-start = (f32[5,4,8,1024]{3,2,1,0:T(8,128)S(1)}, f32[5,4,8,1024]{3,2,1,0:T(8,128)S(1)}, u32[]{:S(2)}, u32[]{:S(2)}) collective-permute-start(f32[5,4,8,1024]{3,2,1,0:T(8,128)S(1)} %get-tuple-element.23), channel_id=1, source_target_pairs={{0,8},{8,16},{16,24},{24,56},{56,48},{48,40},{40,32},{32,64},{64,7... | collective-permute-start | bytes 1966088 | tf_op jit(solution)/shard_map/ppermute | solution.py:200
  58.4 2.9 %collective-permute-start.3 = (f32[5,2,8,1024]{3,2,1,0:T(8,128)S(1)}, f32[5,2,8,1024]{3,2,1,0:T(8,128)S(1)}, u32[]{:S(2)}, u32[]{:S(2)}) collective-permute-start(f32[5,2,8,1024]{3,2,1,0:T(8,128)S(1)} %get-tuple-element.26), channel_id=1, source_target_pairs={{1,0},{2,1},{3,2},{4,3},{5,4},{6,5},{7,6},{0,7},{9,8},{10,9},{11,1... | collective-permute-start | bytes 983048 | tf_op jit(solution)/shard_map/ppermute | solution.py:203
  61.3 10.5 %inner1.1.refs_0_ = f32[5,16,8,1024]{3,2,1,0:T(8,128)S(1)} custom-call(f32[5,16,8,1024]{3,2,1,0:T(8,128)S(1)} %get-tuple-element.21.refs_0_.refs_1_, f32[16,8,1024]{2,1,0:T(8,128)S(1)} %get-tuple-element.22.refs_1_.refs_2_, f32[1024,1024]{1,0:T(8,128)S(1)} %copy-done.1, f32[1024,1024]{1,0:T(8,128)S(1)} %copy-done.2), custom_call_target="tpu_custom_call" | custom-call | flops 5368709120 | bytes 14000000 | tf_op jit(solution)/shard_map/inner1/pallas_call | solution.py:327
  71.8 2.2 %collective-permute-done.1.refs_3_ = f32[5,4,8,1024]{3,2,1,0:T(8,128)S(1)} collective-permute-done((f32[5,4,8,1024]{3,2,1,0:T(8,128)S(1)}, f32[5,4,8,1024]{3,2,1,0:T(8,128)S(1)}, u32[]{:S(2)}, u32[]{:S(2)}) %collective-permute-start.1) | collective-permute-done | bytes 655392 | tf_op jit(solution)/shard_map/ppermute | solution.py:201
  74.0 2.2 %first.1 = (f32[5,16,8,1024]{3,2,1,0:T(8,128)S(1)}, f32[5,4,8,1024]{3,2,1,0:T(8,128)S(1)}, f32[5,4,8,1024]{3,2,1,0:T(8,128)S(1)}, f32[5,2,8,1024]{3,2,1,0:T(8,128)S(1)}, f32[5,2,8,1024]{3,2,1,0:T(8,128)S(1)}) custom-call(f32[5,16,8,1024]{3,2,1,0:T(8,128)S(1)} %inner1.1.refs_0_, f32[16,8,1024]{2,1,0:T(8,128)S(1)} %get-tuple-element.22.refs_1_.refs_2_, ...), custom_call_target="tpu_custom_call" | custom-call | flops 10000000 | bytes 9000000 | tf_op jit(solution)/shard_map/first/pallas_call | solution.py:353
  76.2 2.5 %collective-permute-start.4 = (f32[5,4,8,1024]{3,2,1,0:T(8,128)S(1)}, f32[5,4,8,1024]{3,2,1,0:T(8,128)S(1)}, u32[]{:S(2)}, u32[]{:S(2)}) collective-permute-start(f32[5,4,8,1024]{3,2,1,0:T(8,128)S(1)} %get-tuple-element.28), channel_id=1, source_target_pairs={{0,8},{8,16},{16,24},{24,56},{56,48},{48,40},{40,32},{32,64},{64,7... | collective-permute-start | bytes 1966088 | tf_op jit(solution)/shard_map/ppermute | solution.py:200
  80.0 2.9 %collective-permute-start.7 = (f32[5,2,8,1024]{3,2,1,0:T(8,128)S(1)}, f32[5,2,8,1024]{3,2,1,0:T(8,128)S(1)}, u32[]{:S(2)}, u32[]{:S(2)}) collective-permute-start(f32[5,2,8,1024]{3,2,1,0:T(8,128)S(1)} %get-tuple-element.31), channel_id=1, source_target_pairs={{1,0},{2,1},{3,2},{4,3},{5,4},{6,5},{7,6},{0,7},{9,8},{10,9},{11,1... | collective-permute-start | bytes 983048 | tf_op jit(solution)/shard_map/ppermute | solution.py:203
  83.0 10.7 %inner2.1.refs_0_ = f32[5,16,8,1024]{3,2,1,0:T(8,128)S(1)} custom-call(f32[5,16,8,1024]{3,2,1,0:T(8,128)S(1)} %get-tuple-element.27.refs_0_, f32[5,16,8,1024]{3,2,1,0:T(8,128)S(1)} %get-tuple-element.21.refs_0_.refs_1_, f32[16,8,1024]{2,1,0:T(8,128)S(1)} %get-tuple-element.22.refs_1_.refs_2_, f32[1024,1024]{1,0:T(8,128)S(1)} %copy-done.1, ...), custom_call_target="tpu_custom_call" | custom-call | flops 5368709120 | bytes 14000000 | tf_op jit(solution)/shard_map/inner2/pallas_call | solution.py:327
  93.8 1.8 %collective-permute-done.5.refs_3_ = f32[5,4,8,1024]{3,2,1,0:T(8,128)S(1)} collective-permute-done((f32[5,4,8,1024]{3,2,1,0:T(8,128)S(1)}, f32[5,4,8,1024]{3,2,1,0:T(8,128)S(1)}, u32[]{:S(2)}, u32[]{:S(2)}) %collective-permute-start.5) | collective-permute-done | bytes 655392 | tf_op jit(solution)/shard_map/ppermute | solution.py:201
  95.6 2.4 %final.1 = (f32[16,40,8,128]{3,2,1,0:T(8,128)}, f32[16,8,1024]{2,1,0:T(8,128)S(1)}) custom-call(f32[5,16,8,1024]{3,2,1,0:T(8,128)S(1)} %inner2.1.refs_0_, f32[16,8,1024]{2,1,0:T(8,128)S(1)} %get-tuple-element.22.refs_1_.refs_2_, f32[5,4,8,1024]{3,2,1,0:T(8,128)S(1)} %collective-permute-done.4.refs_2_, f32[5,4,8,1024]{3,2,1,0:T(8,128)S(1)} %collective-permute-done.5.refs_3_, ...), custom_call_target="tpu_custom_call" | custom-call | flops 10000000 | bytes 9000000 | tf_op jit(solution)/shard_map/final/pallas_call | solution.py:381
  98.0 4.2 %all-to-all-start.1 = ((f32[16,40,8,128]{3,2,1,0:T(8,128)}), f32[16,40,8,128]{3,2,1,0:T(8,128)S(1)}, u32[]{:S(2)}, u32[]{:S(2)}) async-start(f32[16,40,8,128]{3,2,1,0:T(8,128)} %get-tuple-element.32), calls=%async_computation.1 | async-start | bytes 5242880 | tf_op jit(solution)/shard_map/all_to_all | solution.py:509
  102.2 4.5 %forces.1 = f32[64,128]{1,0:T(8,128)S(1)} custom-call(f32[16,8,1024]{2,1,0:T(8,128)S(1)} %get-tuple-element.36.load_ref, f32[16,1024]{1,0:T(8,128)S(1)} %get-tuple-element.37.code_ref, f32[256,128]{1,0:T(8,128)S(1)} %copy-done), custom_call_target="tpu_custom_call" | custom-call | flops 134217728 | bytes 700000 | tf_op jit(solution)/shard_map/forces/pallas_call | solution.py:464
  108.0 1.5 %collective-permute-start.9 = (f32[64,128]{1,0:T(8,128)S(1)}, f32[64,128]{1,0:T(8,128)S(1)}, u32[]{:S(2)}, u32[]{:S(2)}) collective-permute-start(f32[64,128]{1,0:T(8,128)S(1)} %add.9), channel_id=1, source_target_pairs={{0,2},{1,3},{2,0},{3,1},{4,6},{5,7},{6,4},{7,5},{8,10},{9,11},{10,... | collective-permute-start | bytes 98312 | tf_op jit(solution)/shard_map/ppermute | solution.py:478
  109.5 2.4 %collective-permute-done.9 = f32[64,128]{1,0:T(8,128)S(1)} collective-permute-done((f32[64,128]{1,0:T(8,128)S(1)}, f32[64,128]{1,0:T(8,128)S(1)}, u32[]{:S(2)}, u32[]{:S(2)}) %collective-permute-start.9) | collective-permute-done | bytes 32800 | tf_op jit(solution)/shard_map/ppermute | solution.py:478
  112.0 2.7 %collective-permute-start.10 = (f32[64,128]{1,0:T(8,128)S(1)}, f32[64,128]{1,0:T(8,128)S(1)}, u32[]{:S(2)}, u32[]{:S(2)}) collective-permute-start(f32[64,128]{1,0:T(8,128)S(1)} %add.10), channel_id=1, source_target_pairs={{0,4},{1,5},{2,6},{3,7},{4,0},{5,1},{6,2},{7,3},{8,12},{9,13},{10,... | collective-permute-start | bytes 98312 | tf_op jit(solution)/shard_map/ppermute | solution.py:478
  114.7 2.7 %collective-permute-done.10 = f32[64,128]{1,0:T(8,128)S(1)} collective-permute-done((f32[64,128]{1,0:T(8,128)S(1)}, f32[64,128]{1,0:T(8,128)S(1)}, u32[]{:S(2)}, u32[]{:S(2)}) %collective-permute-start.10) | collective-permute-done | bytes 32800 | tf_op jit(solution)/shard_map/ppermute | solution.py:478
  117.4 5.3 %collective-permute-start.11 = (f32[32,128]{1,0:T(8,128)S(1)}, f32[32,128]{1,0:T(8,128)S(1)}, u32[]{:S(2)}, u32[]{:S(2)}) collective-permute-start(f32[32,128]{1,0:T(8,128)S(1)} %slice.32), channel_id=1, source_target_pairs={{0,64},{1,65},{2,66},{3,67},{4,68},{5,69},{6,70},{7,71}} | collective-permute-start | bytes 49160 | tf_op jit(solution)/shard_map/ppermute | solution.py:483
  122.7 3.3 %collective-permute-done.11 = f32[32,128]{1,0:T(8,128)S(1)} collective-permute-done((f32[32,128]{1,0:T(8,128)S(1)}, f32[32,128]{1,0:T(8,128)S(1)}, u32[]{:S(2)}, u32[]{:S(2)}) %collective-permute-start.11) | collective-permute-done | bytes 16416 | tf_op jit(solution)/shard_map/ppermute | solution.py:483
  130.0 2.6 %collective-permute-done.13 = f32[8,128]{1,0:T(8,128)S(1)} collective-permute-done((f32[8,128]{1,0:T(8,128)S(1)}, f32[8,128]{1,0:T(8,128)S(1)}, u32[]{:S(2)}, u32[]{:S(2)}) %collective-permute-start.13) | collective-permute-done | bytes 4128 | tf_op jit(solution)/shard_map/ppermute | solution.py:483
  135.7 2.6 %all-to-all-done.1.in_ref = f32[16,40,8,128]{3,2,1,0:T(8,128)S(1)} async-done(((f32[16,40,8,128]{3,2,1,0:T(8,128)}), f32[16,40,8,128]{3,2,1,0:T(8,128)S(1)}, u32[]{:S(2)}, u32[]{:S(2)}) %all-to-all-start.1) | async-done | bytes 2621472 | tf_op jit(solution)/shard_map/all_to_all | solution.py:509
  138.3 1.8 %home.1 = (f32[1024,128]{1,0:T(8,128)}, f32[3,1024,128]{2,1,0:T(8,128)}, f32[1024,128]{1,0:T(8,128)}) custom-call(f32[16,40,8,128]{3,2,1,0:T(8,128)S(1)} %all-to-all-done.1.in_ref), custom_call_target="tpu_custom_call" | custom-call | flops 1000000 | bytes 5300000 | tf_op jit(solution)/shard_map/home/pallas_call | solution.py:411
  (34 shorter events, 11.0 us)
Async XLA Ops:
  4.0 57.3 %copy-start.1 = (f32[1024,1024]{1,0:T(8,128)S(1)}, f32[1024,1024]{1,0:T(8,128)}, u32[]{:S(2)}) copy-start(f32[1024,1024]{1,0:T(8,128)} %refs_3_.3) | copy-start | bytes 12582916
  4.0 57.3 %copy-start.2 = (f32[1024,1024]{1,0:T(8,128)S(1)}, f32[1024,1024]{1,0:T(8,128)}, u32[]{:S(2)}) copy-start(f32[1024,1024]{1,0:T(8,128)} %refs_4_.1) | copy-start | bytes 12582916
  54.5 17.3 %collective-permute-start = (f32[5,4,8,1024]{3,2,1,0:T(8,128)S(1)}, f32[5,4,8,1024]{3,2,1,0:T(8,128)S(1)}, u32[]{:S(2)}, u32[]{:S(2)}) collective-permute-start(f32[5,4,8,1024]{3,2,1,0:T(8,128)S(1)} %get-tuple-element.23), channel_id=1, source_target_pairs={{0,8},{8,16},{16,24},{24,56},{56,48},{48,40},{40,32},{32,64},{64,7... | collective-permute-start | bytes 1966088 | tf_op jit(solution)/shard_map/ppermute | solution.py:200
  57.0 17.0 %collective-permute-start.1 = (f32[5,4,8,1024]{3,2,1,0:T(8,128)S(1)}, f32[5,4,8,1024]{3,2,1,0:T(8,128)S(1)}, u32[]{:S(2)}, u32[]{:S(2)}) collective-permute-start(f32[5,4,8,1024]{3,2,1,0:T(8,128)S(1)} %get-tuple-element.24), channel_id=1, source_target_pairs={{8,0},{16,8},{24,16},{56,24},{48,56},{40,48},{32,40},{64,32},{72,6... | collective-permute-start | bytes 1966088 | tf_op jit(solution)/shard_map/ppermute | solution.py:201
  58.3 13.5 %collective-permute-start.2 = (f32[5,2,8,1024]{3,2,1,0:T(8,128)S(1)}, f32[5,2,8,1024]{3,2,1,0:T(8,128)S(1)}, u32[]{:S(2)}, u32[]{:S(2)}) collective-permute-start(f32[5,2,8,1024]{3,2,1,0:T(8,128)S(1)} %get-tuple-element.25), channel_id=1, source_target_pairs={{0,1},{1,2},{2,3},{3,4},{4,5},{5,6},{6,7},{7,0},{8,9},{9,10},{10,1... | collective-permute-start | bytes 983048 | tf_op jit(solution)/shard_map/ppermute | solution.py:202
  58.4 13.5 %collective-permute-start.3 = (f32[5,2,8,1024]{3,2,1,0:T(8,128)S(1)}, f32[5,2,8,1024]{3,2,1,0:T(8,128)S(1)}, u32[]{:S(2)}, u32[]{:S(2)}) collective-permute-start(f32[5,2,8,1024]{3,2,1,0:T(8,128)S(1)} %get-tuple-element.26), channel_id=1, source_target_pairs={{1,0},{2,1},{3,2},{4,3},{5,4},{6,5},{7,6},{0,7},{9,8},{10,9},{11,1... | collective-permute-start | bytes 983048 | tf_op jit(solution)/shard_map/ppermute | solution.py:203
  76.2 17.6 %collective-permute-start.4 = (f32[5,4,8,1024]{3,2,1,0:T(8,128)S(1)}, f32[5,4,8,1024]{3,2,1,0:T(8,128)S(1)}, u32[]{:S(2)}, u32[]{:S(2)}) collective-permute-start(f32[5,4,8,1024]{3,2,1,0:T(8,128)S(1)} %get-tuple-element.28), channel_id=1, source_target_pairs={{0,8},{8,16},{16,24},{24,56},{56,48},{48,40},{40,32},{32,64},{64,7... | collective-permute-start | bytes 1966088 | tf_op jit(solution)/shard_map/ppermute | solution.py:200
  78.7 16.9 %collective-permute-start.5 = (f32[5,4,8,1024]{3,2,1,0:T(8,128)S(1)}, f32[5,4,8,1024]{3,2,1,0:T(8,128)S(1)}, u32[]{:S(2)}, u32[]{:S(2)}) collective-permute-start(f32[5,4,8,1024]{3,2,1,0:T(8,128)S(1)} %get-tuple-element.29), channel_id=1, source_target_pairs={{8,0},{16,8},{24,16},{56,24},{48,56},{40,48},{32,40},{64,32},{72,6... | collective-permute-start | bytes 1966088 | tf_op jit(solution)/shard_map/ppermute | solution.py:201
  80.0 13.7 %collective-permute-start.6 = (f32[5,2,8,1024]{3,2,1,0:T(8,128)S(1)}, f32[5,2,8,1024]{3,2,1,0:T(8,128)S(1)}, u32[]{:S(2)}, u32[]{:S(2)}) collective-permute-start(f32[5,2,8,1024]{3,2,1,0:T(8,128)S(1)} %get-tuple-element.30), channel_id=1, source_target_pairs={{0,1},{1,2},{2,3},{3,4},{4,5},{5,6},{6,7},{7,0},{8,9},{9,10},{10,1... | collective-permute-start | bytes 983048 | tf_op jit(solution)/shard_map/ppermute | solution.py:202
  80.0 13.7 %collective-permute-start.7 = (f32[5,2,8,1024]{3,2,1,0:T(8,128)S(1)}, f32[5,2,8,1024]{3,2,1,0:T(8,128)S(1)}, u32[]{:S(2)}, u32[]{:S(2)}) collective-permute-start(f32[5,2,8,1024]{3,2,1,0:T(8,128)S(1)} %get-tuple-element.31), channel_id=1, source_target_pairs={{1,0},{2,1},{3,2},{4,3},{5,4},{6,5},{7,6},{0,7},{9,8},{10,9},{11,1... | collective-permute-start | bytes 983048 | tf_op jit(solution)/shard_map/ppermute | solution.py:203
  98.0 4.2 %copy-start = (f32[256,128]{1,0:T(8,128)S(1)}, f32[256,128]{1,0:T(8,128)}, u32[]{:S(2)}) copy-start(f32[256,128]{1,0:T(8,128)} %table_ref.1) | copy-start | bytes 393220
  98.0 40.3 %all-to-all-start.1 = ((f32[16,40,8,128]{3,2,1,0:T(8,128)}), f32[16,40,8,128]{3,2,1,0:T(8,128)S(1)}, u32[]{:S(2)}, u32[]{:S(2)}) async-start(f32[16,40,8,128]{3,2,1,0:T(8,128)} %get-tuple-element.32), calls=%async_computation.1 | async-start | bytes 5242880 | tf_op jit(solution)/shard_map/all_to_all | solution.py:509
  106.8 1.3 collective-permute-start.8
  108.0 3.9 %collective-permute-start.9 = (f32[64,128]{1,0:T(8,128)S(1)}, f32[64,128]{1,0:T(8,128)S(1)}, u32[]{:S(2)}, u32[]{:S(2)}) collective-permute-start(f32[64,128]{1,0:T(8,128)S(1)} %add.9), channel_id=1, source_target_pairs={{0,2},{1,3},{2,0},{3,1},{4,6},{5,7},{6,4},{7,5},{8,10},{9,11},{10,... | collective-permute-start | bytes 98312 | tf_op jit(solution)/shard_map/ppermute | solution.py:478
  112.0 5.4 %collective-permute-start.10 = (f32[64,128]{1,0:T(8,128)S(1)}, f32[64,128]{1,0:T(8,128)S(1)}, u32[]{:S(2)}, u32[]{:S(2)}) collective-permute-start(f32[64,128]{1,0:T(8,128)S(1)} %add.10), channel_id=1, source_target_pairs={{0,4},{1,5},{2,6},{3,7},{4,0},{5,1},{6,2},{7,3},{8,12},{9,13},{10,... | collective-permute-start | bytes 98312 | tf_op jit(solution)/shard_map/ppermute | solution.py:478
  117.4 8.6 %collective-permute-start.11 = (f32[32,128]{1,0:T(8,128)S(1)}, f32[32,128]{1,0:T(8,128)S(1)}, u32[]{:S(2)}, u32[]{:S(2)}) collective-permute-start(f32[32,128]{1,0:T(8,128)S(1)} %slice.32), channel_id=1, source_target_pairs={{0,64},{1,65},{2,66},{3,67},{4,68},{5,69},{6,70},{7,71}} | collective-permute-start | bytes 49160 | tf_op jit(solution)/shard_map/ppermute | solution.py:483
  126.1 2.6 %collective-permute-start.12 = (f32[16,128]{1,0:T(8,128)S(1)}, f32[16,128]{1,0:T(8,128)S(1)}, u32[]{:S(2)}, u32[]{:S(2)}) collective-permute-start(f32[16,128]{1,0:T(8,128)S(1)} %slice.34), channel_id=1, source_target_pairs={{0,32},{64,96},{1,33},{65,97},{2,34},{66,98},{3,35},{67,99},{4,36}... | collective-permute-start | bytes 24584 | tf_op jit(solution)/shard_map/ppermute | solution.py:483
  128.7 3.9 %collective-permute-start.13 = (f32[8,128]{1,0:T(8,128)S(1)}, f32[8,128]{1,0:T(8,128)S(1)}, u32[]{:S(2)}, u32[]{:S(2)}) collective-permute-start(f32[8,128]{1,0:T(8,128)S(1)} %slice.36), channel_id=1, source_target_pairs={{0,16},{32,48},{64,80},{96,112},{1,17},{33,49},{65,81},{97,113},{2... | collective-permute-start | bytes 12296 | tf_op jit(solution)/shard_map/ppermute | solution.py:483
  132.6 2.6 %collective-permute-start.14 = (f32[4,128]{1,0:T(4,128)S(1)}, f32[4,128]{1,0:T(4,128)S(1)}, u32[]{:S(2)}, u32[]{:S(2)}) collective-permute-start(f32[4,128]{1,0:T(4,128)S(1)} %slice.30), channel_id=1, source_target_pairs={{0,8},{16,24},{32,40},{48,56},{64,72},{80,88},{96,104},{112,120},{... | collective-permute-start | bytes 6152 | tf_op jit(solution)/shard_map/ppermute | solution.py:483

commit v5 on v4

--- a/solution.py
+++ b/solution.py
@@ -157,22 +157,19 @@
 STEPS = 2
 STRIP = 1024 // STEPS
 PARTS = STRIP // LANES
-yedge_spec = pl.BlockSpec((5, 4, YB, STRIP), lambda s: (0, 0, 0, s))
-zedge_spec = pl.BlockSpec((5, 2, YB, STRIP), lambda s: (0, 0, 0, s))
-edge_specs = [yedge_spec] * 2 + [zedge_spec] * 2
-line_spec = pl.BlockSpec((5, ZB, YB, STRIP), lambda s: (0, 0, 0, s))
-cell_spec = pl.BlockSpec((ZB, YB, STRIP), lambda s: (0, 0, s))
-code_spec = pl.BlockSpec((ZB, STRIP), lambda s: (0, s))
-
-
-def by_lanes(kernel, packed_at=None):
+in_place = pl.BlockSpec(memory_space=pltpu.VMEM)
+
+
+def by_lanes(kernel, packed_at=None, blocked=False):
     def run(*refs):
+        strip = pl.program_id(0)
         for c in range(PARTS):
-            lanes = pl.ds(c * LANES, LANES)
+            lanes = pl.ds(pl.multiple_of(strip * STRIP + c * LANES, LANES), LANES)
+            peer = 2 * c if blocked else strip * (2 * PARTS) + 2 * c
             views = []
             for i, ref in enumerate(refs):
                 if i == packed_at:
-                    views.append(ref.at[pl.ds(2 * c, 2)])
+                    views.append(ref.at[pl.ds(peer, 2)])
                 else:
                     views.append(ref.at[(slice(None),) * (len(ref.shape) - 1) + (lanes,)])
             kernel(*views)
@@ -229,8 +226,8 @@
         by_lanes(unpack_kernel, 0),
         grid=(STEPS,),
         out_shape=[shaped(5, ZB, YB, 1024), shaped(ZB, YB, 1024), shaped(ZB, 1024), *edge_shapes],
-        in_specs=[pl.BlockSpec((2 * PARTS, 49, YB, LANES), lambda s: (s, 0, 0, 0))],
-        out_specs=[line_spec, cell_spec, code_spec, *edge_specs],
+        in_specs=[in_place],
+        out_specs=[in_place] * 7,
         compiler_params=grant(16),
         cost_estimate=cost(10000000, 8000000),
         name="unpack",
@@ -354,8 +351,8 @@
         by_lanes(first_kernel),
         grid=(STEPS,),
         out_shape=[shaped(5, ZB, YB, 1024), *edge_shapes],
-        in_specs=[line_spec, cell_spec, *edge_specs],
-        out_specs=[line_spec, *edge_specs],
+        in_specs=[in_place] * 6,
+        out_specs=[in_place] * 5,
         compiler_params=grant(16),
         cost_estimate=cost(10000000, 9000000),
         name="first",
@@ -379,11 +376,11 @@
 
 def final_section(part, metric, halos):
     return pl.pallas_call(
-        by_lanes(final_kernel, 6),
+        by_lanes(final_kernel, 6, blocked=True),
         grid=(STEPS,),
         out_shape=[pltpu.HBM((16, 40, YB, LANES), f32), shaped(ZB, YB, 1024)],
-        in_specs=[line_spec, cell_spec, *edge_specs],
-        out_specs=[pl.BlockSpec((2 * PARTS, 40, YB, LANES), lambda s: (s, 0, 0, 0)), cell_spec],
+        in_specs=[in_place] * 6,
+        out_specs=[pl.BlockSpec((2 * PARTS, 40, YB, LANES), lambda s: (s, 0, 0, 0)), in_place],
         compiler_params=grant(16),
         cost_estimate=cost(10000000, 9000000),
         name="final",

time: 140 us -> 140 us (level)
  transfers between devices with their start and end apart: 16 -> 16, of which waited for: 10 -> 10; matrix products, arithmetic and copies ran while one was open for 0% -> 0% of each run, Pallas kernels for 18% -> 19%
where the time goes in v5:
time: 140 us; the launch traced here: 139 us
  blocking collectives  48.8 us (35%)
  Pallas kernels  36.4 us (26%)
  starting transfers between devices  31.2 us (22%)
  waiting for transfers between devices  21.4 us (15%)
    all_to_all x1, blocking collectives, body(): lax.all_to_all(outgoing, 'gx', split_axis=0, concat_axis=0, tiled=True)  48.8 us
    pallas_call x2, Pallas kernels, inner(): pl.pallas_call(functools.partial(inner_kernel, second), grid=(1024 // WID...  21.3 us
    ppermute x4, starting transfers between devices, spread_forces(): lax.ppermute(held[half:], 'gx', [(g, g + bit) for g in range(0, 16, 2 * b...  9.17 us
    ppermute x4, waiting for transfers between devices, spread_forces(): lax.ppermute(held[half:], 'gx', [(g, g + bit) for g in range(0, 16, 2 * b...  8.52 us
    ppermute x3, waiting for transfers between devices, spread_forces(): held = held + lax.ppermute(held, 'gz', [(g, g ^ bit) for g in range(8)])  6.31 us
    ppermute x2, starting transfers between devices, exchange(): lax.ppermute(left, 'gz', [((g + 1) % 8, g) for g in range(8)])  5.89 us
    ppermute x2, starting transfers between devices, exchange(): lax.ppermute(up, 'gx', ahead)  5.02 us
    pallas_call x1, Pallas kernels, forces(): pl.pallas_call(forces_kernel, out_shape=shaped(NP, LANES), in_specs=[vm]...  4.55 us
  transfers between devices with their start and end apart: 16, of which 10 were waited for; matrix products, arithmetic and copies ran while one was open for 0% of the time, Pallas kernels for 19%

profile of v5, /device:TPU:0, one launch (start us, length us, event | category | flops | bytes accessed | tf_op | source)
XLA Modules:
  0.0 139.3 jit_solution(15464309497679049068)
XLA Ops:
  0.6 3.4 %pack.1 = f32[16,49,8,128]{3,2,1,0:T(8,128)} custom-call(f32[1024,128]{1,0:T(8,128)} %bitcast.10, f32[3,1024,128]{2,1,0:T(8,128)} %bitcast.9, f32[1024,128]{1,0:T(8,128)} %bitcast.11, f32[1024,128]{1,0:T(8,128)} %bitcast.12, s32[16,64]{1,0:T(8,128)} %bitcast.13, s32[16,64]{1,0:T(8,128)} %bitcast.14), custom_call_target="tpu_custom_call" | custom-call | flops 1000000 | bytes 6400000 | tf_op jit(solution)/shard_map/pack/pallas_call | solution.py:103
  4.0 48.8 %all_to_all.10.refs_0_ = f32[16,49,8,128]{3,2,1,0:T(8,128)S(1)} all-to-all(f32[16,49,8,128]{3,2,1,0:T(8,128)} %pack.1), channel_id=1, replica_groups=mesh['gx'=16,'gz'=8] {'gx'}, dimensions={0} | all-to-all | bytes 6422528 | tf_op jit(solution)/shard_map/all_to_all | solution.py:498
  54.2 2.5 %collective-permute-start = (f32[5,4,8,1024]{3,2,1,0:T(8,128)S(1)}, f32[5,4,8,1024]{3,2,1,0:T(8,128)S(1)}, u32[]{:S(2)}, u32[]{:S(2)}) collective-permute-start(f32[5,4,8,1024]{3,2,1,0:T(8,128)S(1)} %get-tuple-element.23), channel_id=1, source_target_pairs={{0,8},{8,16},{16,24},{24,56},{56,48},{48,40},{40,32},{32,64},{64,7... | collective-permute-start | bytes 1966088 | tf_op jit(solution)/shard_map/ppermute | solution.py:197
  58.0 2.9 %collective-permute-start.3 = (f32[5,2,8,1024]{3,2,1,0:T(8,128)S(1)}, f32[5,2,8,1024]{3,2,1,0:T(8,128)S(1)}, u32[]{:S(2)}, u32[]{:S(2)}) collective-permute-start(f32[5,2,8,1024]{3,2,1,0:T(8,128)S(1)} %get-tuple-element.26), channel_id=1, source_target_pairs={{1,0},{2,1},{3,2},{4,3},{5,4},{6,5},{7,6},{0,7},{9,8},{10,9},{11,1... | collective-permute-start | bytes 983048 | tf_op jit(solution)/shard_map/ppermute | solution.py:200
  61.0 10.5 %inner1.1.refs_0_ = f32[5,16,8,1024]{3,2,1,0:T(8,128)S(1)} custom-call(f32[5,16,8,1024]{3,2,1,0:T(8,128)S(1)} %get-tuple-element.21.refs_0_.refs_1_, f32[16,8,1024]{2,1,0:T(8,128)S(1)} %get-tuple-element.22.refs_1_.refs_2_, f32[1024,1024]{1,0:T(8,128)S(1)} %copy-done.1, f32[1024,1024]{1,0:T(8,128)S(1)} %copy-done.2), custom_call_target="tpu_custom_call" | custom-call | flops 5368709120 | bytes 14000000 | tf_op jit(solution)/shard_map/inner1/pallas_call | solution.py:324
  71.5 2.2 %collective-permute-done.1.refs_3_ = f32[5,4,8,1024]{3,2,1,0:T(8,128)S(1)} collective-permute-done((f32[5,4,8,1024]{3,2,1,0:T(8,128)S(1)}, f32[5,4,8,1024]{3,2,1,0:T(8,128)S(1)}, u32[]{:S(2)}, u32[]{:S(2)}) %collective-permute-start.1) | collective-permute-done | bytes 655392 | tf_op jit(solution)/shard_map/ppermute | solution.py:198
  73.7 2.0 %first.1 = (f32[5,16,8,1024]{3,2,1,0:T(8,128)S(1)}, f32[5,4,8,1024]{3,2,1,0:T(8,128)S(1)}, f32[5,4,8,1024]{3,2,1,0:T(8,128)S(1)}, f32[5,2,8,1024]{3,2,1,0:T(8,128)S(1)}, f32[5,2,8,1024]{3,2,1,0:T(8,128)S(1)}) custom-call(f32[5,16,8,1024]{3,2,1,0:T(8,128)S(1)} %inner1.1.refs_0_, f32[16,8,1024]{2,1,0:T(8,128)S(1)} %get-tuple-element.22.refs_1_.refs_2_, ...), custom_call_target="tpu_custom_call" | custom-call | flops 10000000 | bytes 9000000 | tf_op jit(solution)/shard_map/first/pallas_call | solution.py:350
  75.6 2.5 %collective-permute-start.4 = (f32[5,4,8,1024]{3,2,1,0:T(8,128)S(1)}, f32[5,4,8,1024]{3,2,1,0:T(8,128)S(1)}, u32[]{:S(2)}, u32[]{:S(2)}) collective-permute-start(f32[5,4,8,1024]{3,2,1,0:T(8,128)S(1)} %get-tuple-element.28), channel_id=1, source_target_pairs={{0,8},{8,16},{16,24},{24,56},{56,48},{48,40},{40,32},{32,64},{64,7... | collective-permute-start | bytes 1966088 | tf_op jit(solution)/shard_map/ppermute | solution.py:197
  79.5 2.9 %collective-permute-start.7 = (f32[5,2,8,1024]{3,2,1,0:T(8,128)S(1)}, f32[5,2,8,1024]{3,2,1,0:T(8,128)S(1)}, u32[]{:S(2)}, u32[]{:S(2)}) collective-permute-start(f32[5,2,8,1024]{3,2,1,0:T(8,128)S(1)} %get-tuple-element.31), channel_id=1, source_target_pairs={{1,0},{2,1},{3,2},{4,3},{5,4},{6,5},{7,6},{0,7},{9,8},{10,9},{11,1... | collective-permute-start | bytes 983048 | tf_op jit(solution)/shard_map/ppermute | solution.py:200
  82.4 10.7 %inner2.1.refs_0_ = f32[5,16,8,1024]{3,2,1,0:T(8,128)S(1)} custom-call(f32[5,16,8,1024]{3,2,1,0:T(8,128)S(1)} %get-tuple-element.27.refs_0_, f32[5,16,8,1024]{3,2,1,0:T(8,128)S(1)} %get-tuple-element.21.refs_0_.refs_1_, f32[16,8,1024]{2,1,0:T(8,128)S(1)} %get-tuple-element.22.refs_1_.refs_2_, f32[1024,1024]{1,0:T(8,128)S(1)} %copy-done.1, ...), custom_call_target="tpu_custom_call" | custom-call | flops 5368709120 | bytes 14000000 | tf_op jit(solution)/shard_map/inner2/pallas_call | solution.py:324
  93.2 1.8 %collective-permute-done.5.refs_3_ = f32[5,4,8,1024]{3,2,1,0:T(8,128)S(1)} collective-permute-done((f32[5,4,8,1024]{3,2,1,0:T(8,128)S(1)}, f32[5,4,8,1024]{3,2,1,0:T(8,128)S(1)}, u32[]{:S(2)}, u32[]{:S(2)}) %collective-permute-start.5) | collective-permute-done | bytes 655392 | tf_op jit(solution)/shard_map/ppermute | solution.py:198
  95.0 2.1 %final.1 = (f32[16,40,8,128]{3,2,1,0:T(8,128)}, f32[16,8,1024]{2,1,0:T(8,128)S(1)}) custom-call(f32[5,16,8,1024]{3,2,1,0:T(8,128)S(1)} %inner2.1.refs_0_, f32[16,8,1024]{2,1,0:T(8,128)S(1)} %get-tuple-element.22.refs_1_.refs_2_, f32[5,4,8,1024]{3,2,1,0:T(8,128)S(1)} %collective-permute-done.4.refs_2_, f32[5,4,8,1024]{3,2,1,0:T(8,128)S(1)} %collective-permute-done.5.refs_3_, ...), custom_call_target="tpu_custom_call" | custom-call | flops 10000000 | bytes 9000000 | tf_op jit(solution)/shard_map/final/pallas_call | solution.py:378
  97.2 4.2 %all-to-all-start.1 = ((f32[16,40,8,128]{3,2,1,0:T(8,128)}), f32[16,40,8,128]{3,2,1,0:T(8,128)S(1)}, u32[]{:S(2)}, u32[]{:S(2)}) async-start(f32[16,40,8,128]{3,2,1,0:T(8,128)} %get-tuple-element.32), calls=%async_computation.1 | async-start | bytes 5242880 | tf_op jit(solution)/shard_map/all_to_all | solution.py:506
  101.4 4.5 %forces.1 = f32[64,128]{1,0:T(8,128)S(1)} custom-call(f32[16,8,1024]{2,1,0:T(8,128)S(1)} %get-tuple-element.36.load_ref, f32[16,1024]{1,0:T(8,128)S(1)} %get-tuple-element.37.code_ref, f32[256,128]{1,0:T(8,128)S(1)} %copy-done), custom_call_target="tpu_custom_call" | custom-call | flops 134217728 | bytes 700000 | tf_op jit(solution)/shard_map/forces/pallas_call | solution.py:461
  107.2 1.5 %collective-permute-start.9 = (f32[64,128]{1,0:T(8,128)S(1)}, f32[64,128]{1,0:T(8,128)S(1)}, u32[]{:S(2)}, u32[]{:S(2)}) collective-permute-start(f32[64,128]{1,0:T(8,128)S(1)} %add.9), channel_id=1, source_target_pairs={{0,2},{1,3},{2,0},{3,1},{4,6},{5,7},{6,4},{7,5},{8,10},{9,11},{10,... | collective-permute-start | bytes 98312 | tf_op jit(solution)/shard_map/ppermute | solution.py:475
  108.7 2.4 %collective-permute-done.9 = f32[64,128]{1,0:T(8,128)S(1)} collective-permute-done((f32[64,128]{1,0:T(8,128)S(1)}, f32[64,128]{1,0:T(8,128)S(1)}, u32[]{:S(2)}, u32[]{:S(2)}) %collective-permute-start.9) | collective-permute-done | bytes 32800 | tf_op jit(solution)/shard_map/ppermute | solution.py:475
  111.1 2.7 %collective-permute-start.10 = (f32[64,128]{1,0:T(8,128)S(1)}, f32[64,128]{1,0:T(8,128)S(1)}, u32[]{:S(2)}, u32[]{:S(2)}) collective-permute-start(f32[64,128]{1,0:T(8,128)S(1)} %add.10), channel_id=1, source_target_pairs={{0,4},{1,5},{2,6},{3,7},{4,0},{5,1},{6,2},{7,3},{8,12},{9,13},{10,... | collective-permute-start | bytes 98312 | tf_op jit(solution)/shard_map/ppermute | solution.py:475
  113.9 2.7 %collective-permute-done.10 = f32[64,128]{1,0:T(8,128)S(1)} collective-permute-done((f32[64,128]{1,0:T(8,128)S(1)}, f32[64,128]{1,0:T(8,128)S(1)}, u32[]{:S(2)}, u32[]{:S(2)}) %collective-permute-start.10) | collective-permute-done | bytes 32800 | tf_op jit(solution)/shard_map/ppermute | solution.py:475
  116.6 5.3 %collective-permute-start.11 = (f32[32,128]{1,0:T(8,128)S(1)}, f32[32,128]{1,0:T(8,128)S(1)}, u32[]{:S(2)}, u32[]{:S(2)}) collective-permute-start(f32[32,128]{1,0:T(8,128)S(1)} %slice.32), channel_id=1, source_target_pairs={{0,64},{1,65},{2,66},{3,67},{4,68},{5,69},{6,70},{7,71}} | collective-permute-start | bytes 49160 | tf_op jit(solution)/shard_map/ppermute | solution.py:480
  121.9 3.3 %collective-permute-done.11 = f32[32,128]{1,0:T(8,128)S(1)} collective-permute-done((f32[32,128]{1,0:T(8,128)S(1)}, f32[32,128]{1,0:T(8,128)S(1)}, u32[]{:S(2)}, u32[]{:S(2)}) %collective-permute-start.11) | collective-permute-done | bytes 16416 | tf_op jit(solution)/shard_map/ppermute | solution.py:480
  126.5 1.3 collective-permute-done.12
  129.2 2.6 %collective-permute-done.13 = f32[8,128]{1,0:T(8,128)S(1)} collective-permute-done((f32[8,128]{1,0:T(8,128)S(1)}, f32[8,128]{1,0:T(8,128)S(1)}, u32[]{:S(2)}, u32[]{:S(2)}) %collective-permute-start.13) | collective-permute-done | bytes 4128 | tf_op jit(solution)/shard_map/ppermute | solution.py:480
  134.9 2.6 %all-to-all-done.1.in_ref = f32[16,40,8,128]{3,2,1,0:T(8,128)S(1)} async-done(((f32[16,40,8,128]{3,2,1,0:T(8,128)}), f32[16,40,8,128]{3,2,1,0:T(8,128)S(1)}, u32[]{:S(2)}, u32[]{:S(2)}) %all-to-all-start.1) | async-done | bytes 2621472 | tf_op jit(solution)/shard_map/all_to_all | solution.py:506
  137.5 1.8 %home.1 = (f32[1024,128]{1,0:T(8,128)}, f32[3,1024,128]{2,1,0:T(8,128)}, f32[1024,128]{1,0:T(8,128)}) custom-call(f32[16,40,8,128]{3,2,1,0:T(8,128)S(1)} %all-to-all-done.1.in_ref), custom_call_target="tpu_custom_call" | custom-call | flops 1000000 | bytes 5300000 | tf_op jit(solution)/shard_map/home/pallas_call | solution.py:408
  (34 shorter events, 11.0 us)
Async XLA Ops:
  4.0 56.9 %copy-start.1 = (f32[1024,1024]{1,0:T(8,128)S(1)}, f32[1024,1024]{1,0:T(8,128)}, u32[]{:S(2)}) copy-start(f32[1024,1024]{1,0:T(8,128)} %refs_3_.3) | copy-start | bytes 12582916
  4.0 56.9 %copy-start.2 = (f32[1024,1024]{1,0:T(8,128)S(1)}, f32[1024,1024]{1,0:T(8,128)}, u32[]{:S(2)}) copy-start(f32[1024,1024]{1,0:T(8,128)} %refs_4_.1) | copy-start | bytes 12582916
  54.2 17.3 %collective-permute-start = (f32[5,4,8,1024]{3,2,1,0:T(8,128)S(1)}, f32[5,4,8,1024]{3,2,1,0:T(8,128)S(1)}, u32[]{:S(2)}, u32[]{:S(2)}) collective-permute-start(f32[5,4,8,1024]{3,2,1,0:T(8,128)S(1)} %get-tuple-element.23), channel_id=1, source_target_pairs={{0,8},{8,16},{16,24},{24,56},{56,48},{48,40},{40,32},{32,64},{64,7... | collective-permute-start | bytes 1966088 | tf_op jit(solution)/shard_map/ppermute | solution.py:197
  56.7 17.0 %collective-permute-start.1 = (f32[5,4,8,1024]{3,2,1,0:T(8,128)S(1)}, f32[5,4,8,1024]{3,2,1,0:T(8,128)S(1)}, u32[]{:S(2)}, u32[]{:S(2)}) collective-permute-start(f32[5,4,8,1024]{3,2,1,0:T(8,128)S(1)} %get-tuple-element.24), channel_id=1, source_target_pairs={{8,0},{16,8},{24,16},{56,24},{48,56},{40,48},{32,40},{64,32},{72,6... | collective-permute-start | bytes 1966088 | tf_op jit(solution)/shard_map/ppermute | solution.py:198
  58.0 13.5 %collective-permute-start.2 = (f32[5,2,8,1024]{3,2,1,0:T(8,128)S(1)}, f32[5,2,8,1024]{3,2,1,0:T(8,128)S(1)}, u32[]{:S(2)}, u32[]{:S(2)}) collective-permute-start(f32[5,2,8,1024]{3,2,1,0:T(8,128)S(1)} %get-tuple-element.25), channel_id=1, source_target_pairs={{0,1},{1,2},{2,3},{3,4},{4,5},{5,6},{6,7},{7,0},{8,9},{9,10},{10,1... | collective-permute-start | bytes 983048 | tf_op jit(solution)/shard_map/ppermute | solution.py:199
  58.0 13.5 %collective-permute-start.3 = (f32[5,2,8,1024]{3,2,1,0:T(8,128)S(1)}, f32[5,2,8,1024]{3,2,1,0:T(8,128)S(1)}, u32[]{:S(2)}, u32[]{:S(2)}) collective-permute-start(f32[5,2,8,1024]{3,2,1,0:T(8,128)S(1)} %get-tuple-element.26), channel_id=1, source_target_pairs={{1,0},{2,1},{3,2},{4,3},{5,4},{6,5},{7,6},{0,7},{9,8},{10,9},{11,1... | collective-permute-start | bytes 983048 | tf_op jit(solution)/shard_map/ppermute | solution.py:200
  75.6 17.6 %collective-permute-start.4 = (f32[5,4,8,1024]{3,2,1,0:T(8,128)S(1)}, f32[5,4,8,1024]{3,2,1,0:T(8,128)S(1)}, u32[]{:S(2)}, u32[]{:S(2)}) collective-permute-start(f32[5,4,8,1024]{3,2,1,0:T(8,128)S(1)} %get-tuple-element.28), channel_id=1, source_target_pairs={{0,8},{8,16},{16,24},{24,56},{56,48},{48,40},{40,32},{32,64},{64,7... | collective-permute-start | bytes 1966088 | tf_op jit(solution)/shard_map/ppermute | solution.py:197
  78.2 16.9 %collective-permute-start.5 = (f32[5,4,8,1024]{3,2,1,0:T(8,128)S(1)}, f32[5,4,8,1024]{3,2,1,0:T(8,128)S(1)}, u32[]{:S(2)}, u32[]{:S(2)}) collective-permute-start(f32[5,4,8,1024]{3,2,1,0:T(8,128)S(1)} %get-tuple-element.29), channel_id=1, source_target_pairs={{8,0},{16,8},{24,16},{56,24},{48,56},{40,48},{32,40},{64,32},{72,6... | collective-permute-start | bytes 1966088 | tf_op jit(solution)/shard_map/ppermute | solution.py:198
  79.5 13.7 %collective-permute-start.6 = (f32[5,2,8,1024]{3,2,1,0:T(8,128)S(1)}, f32[5,2,8,1024]{3,2,1,0:T(8,128)S(1)}, u32[]{:S(2)}, u32[]{:S(2)}) collective-permute-start(f32[5,2,8,1024]{3,2,1,0:T(8,128)S(1)} %get-tuple-element.30), channel_id=1, source_target_pairs={{0,1},{1,2},{2,3},{3,4},{4,5},{5,6},{6,7},{7,0},{8,9},{9,10},{10,1... | collective-permute-start | bytes 983048 | tf_op jit(solution)/shard_map/ppermute | solution.py:199
  79.5 13.7 %collective-permute-start.7 = (f32[5,2,8,1024]{3,2,1,0:T(8,128)S(1)}, f32[5,2,8,1024]{3,2,1,0:T(8,128)S(1)}, u32[]{:S(2)}, u32[]{:S(2)}) collective-permute-start(f32[5,2,8,1024]{3,2,1,0:T(8,128)S(1)} %get-tuple-element.31), channel_id=1, source_target_pairs={{1,0},{2,1},{3,2},{4,3},{5,4},{6,5},{7,6},{0,7},{9,8},{10,9},{11,1... | collective-permute-start | bytes 983048 | tf_op jit(solution)/shard_map/ppermute | solution.py:200
  97.2 4.2 %copy-start = (f32[256,128]{1,0:T(8,128)S(1)}, f32[256,128]{1,0:T(8,128)}, u32[]{:S(2)}) copy-start(f32[256,128]{1,0:T(8,128)} %table_ref.1) | copy-start | bytes 393220
  97.2 40.3 %all-to-all-start.1 = ((f32[16,40,8,128]{3,2,1,0:T(8,128)}), f32[16,40,8,128]{3,2,1,0:T(8,128)S(1)}, u32[]{:S(2)}, u32[]{:S(2)}) async-start(f32[16,40,8,128]{3,2,1,0:T(8,128)} %get-tuple-element.32), calls=%async_computation.1 | async-start | bytes 5242880 | tf_op jit(solution)/shard_map/all_to_all | solution.py:506
  105.9 1.3 collective-permute-start.8
  107.2 3.9 %collective-permute-start.9 = (f32[64,128]{1,0:T(8,128)S(1)}, f32[64,128]{1,0:T(8,128)S(1)}, u32[]{:S(2)}, u32[]{:S(2)}) collective-permute-start(f32[64,128]{1,0:T(8,128)S(1)} %add.9), channel_id=1, source_target_pairs={{0,2},{1,3},{2,0},{3,1},{4,6},{5,7},{6,4},{7,5},{8,10},{9,11},{10,... | collective-permute-start | bytes 98312 | tf_op jit(solution)/shard_map/ppermute | solution.py:475
  111.1 5.4 %collective-permute-start.10 = (f32[64,128]{1,0:T(8,128)S(1)}, f32[64,128]{1,0:T(8,128)S(1)}, u32[]{:S(2)}, u32[]{:S(2)}) collective-permute-start(f32[64,128]{1,0:T(8,128)S(1)} %add.10), channel_id=1, source_target_pairs={{0,4},{1,5},{2,6},{3,7},{4,0},{5,1},{6,2},{7,3},{8,12},{9,13},{10,... | collective-permute-start | bytes 98312 | tf_op jit(solution)/shard_map/ppermute | solution.py:475
  116.6 8.7 %collective-permute-start.11 = (f32[32,128]{1,0:T(8,128)S(1)}, f32[32,128]{1,0:T(8,128)S(1)}, u32[]{:S(2)}, u32[]{:S(2)}) collective-permute-start(f32[32,128]{1,0:T(8,128)S(1)} %slice.32), channel_id=1, source_target_pairs={{0,64},{1,65},{2,66},{3,67},{4,68},{5,69},{6,70},{7,71}} | collective-permute-start | bytes 49160 | tf_op jit(solution)/shard_map/ppermute | solution.py:480
  125.2 2.6 %collective-permute-start.12 = (f32[16,128]{1,0:T(8,128)S(1)}, f32[16,128]{1,0:T(8,128)S(1)}, u32[]{:S(2)}, u32[]{:S(2)}) collective-permute-start(f32[16,128]{1,0:T(8,128)S(1)} %slice.34), channel_id=1, source_target_pairs={{0,32},{64,96},{1,33},{65,97},{2,34},{66,98},{3,35},{67,99},{4,36}... | collective-permute-start | bytes 24584 | tf_op jit(solution)/shard_map/ppermute | solution.py:480
  127.9 3.9 %collective-permute-start.13 = (f32[8,128]{1,0:T(8,128)S(1)}, f32[8,128]{1,0:T(8,128)S(1)}, u32[]{:S(2)}, u32[]{:S(2)}) collective-permute-start(f32[8,128]{1,0:T(8,128)S(1)} %slice.36), channel_id=1, source_target_pairs={{0,16},{32,48},{64,80},{96,112},{1,17},{33,49},{65,81},{97,113},{2... | collective-permute-start | bytes 12296 | tf_op jit(solution)/shard_map/ppermute | solution.py:480
  131.8 2.6 %collective-permute-start.14 = (f32[4,128]{1,0:T(4,128)S(1)}, f32[4,128]{1,0:T(4,128)S(1)}, u32[]{:S(2)}, u32[]{:S(2)}) collective-permute-start(f32[4,128]{1,0:T(4,128)S(1)} %slice.30), channel_id=1, source_target_pairs={{0,8},{16,24},{32,40},{48,56},{64,72},{80,88},{96,104},{112,120},{... | collective-permute-start | bytes 6152 | tf_op jit(solution)/shard_map/ppermute | solution.py:480

commit v6 on v5

--- a/solution.py
+++ b/solution.py
@@ -259,29 +259,30 @@
         whole_ref, base_ref, metric_ref, d_ref, s_ref, out_ref, q_ref, fhi_ref, flo_ref, slope_ref, x_ref = refs
     else:
         whole_ref, metric_ref, d_ref, s_ref, out_ref, q_ref, fhi_ref, flo_ref, slope_ref, x_ref = refs
-    step = pl.program_id(0)
-
-    @pl.when(step == 0)
-    def prepare():
-        def part(s, carry):
-            lanes = pl.ds(pl.multiple_of(s * LANES, LANES), LANES)
-            q = [whole_ref[f, :, :, lanes] for f in range(5)]
-            inverse = 1.0 / q[0]
-            stream = flux(q, pressure_of(q, inverse), inverse, 0)
-            for f in range(5):
-                rows = pl.ds(f * 128, 128)
-                q_ref[rows, lanes] = (q[f] - middle[f]).reshape(128, LANES).astype(bf16)
-                value = stream[f].reshape(128, LANES)
-                high = value.astype(bf16)
-                fhi_ref[rows, lanes] = high
-                flo_ref[rows, lanes] = (value - high.astype(f32)).astype(bf16)
-            return carry
-
-        lax.fori_loop(0, 8, part, 0)
-
-    wide = pl.ds(pl.multiple_of(step * WIDE, WIDE), WIDE)
+    for s in range(8):
+        lanes = slice(s * LANES, s * LANES + LANES)
+        q = [whole_ref[f, :, :, lanes] for f in range(5)]
+        inverse = 1.0 / q[0]
+        stream = flux(q, pressure_of(q, inverse), inverse, 0)
+        for f in range(5):
+            rows = slice(f * 128, f * 128 + 128)
+            q_ref[rows, lanes] = (q[f] - middle[f]).reshape(128, LANES).astype(bf16)
+            value = stream[f].reshape(128, LANES)
+            high = value.astype(bf16)
+            fhi_ref[rows, lanes] = high
+            flo_ref[rows, lanes] = (value - high.astype(f32)).astype(bf16)
+    for step in range(1024 // WIDE):
+        inner_strip(step, second, refs, slope_ref.at[step % 2], x_ref.at[step % 2])
+
+
+def inner_strip(step, second, refs, slope_ref, x_ref):
+    if second:
+        whole_ref, base_ref, metric_ref, d_ref, s_ref, out_ref, q_ref, fhi_ref, flo_ref = refs[:9]
+    else:
+        whole_ref, metric_ref, d_ref, s_ref, out_ref, q_ref, fhi_ref, flo_ref = refs[:8]
+    wide = slice(step * WIDE, step * WIDE + WIDE)
     for c in range(WIDE // LANES):
-        lanes = pl.ds(pl.multiple_of(step * WIDE + c * LANES, LANES), LANES)
+        lanes = slice(step * WIDE + c * LANES, step * WIDE + c * LANES + LANES)
         q = [whole_ref[f, :, :, lanes] for f in range(5)]
         inverse = 1.0 / q[0]
         pressure = pressure_of(q, inverse)
@@ -320,14 +321,13 @@
 
 def inner(state, metric, deriv, smooth, base=None):
     second = base is not None
-    whole = pl.BlockSpec(memory_space=pltpu.VMEM)
+    whole = in_place
     return pl.pallas_call(
         functools.partial(inner_kernel, second),
-        grid=(1024 // WIDE,),
         out_shape=shaped(5, ZB, YB, 1024),
         in_specs=[whole] * (5 if second else 4),
         out_specs=whole,
-        scratch_shapes=[pltpu.VMEM((640, 1024), bf16)] * 3 + [pltpu.VMEM((5, ZB, YB, WIDE), f32)] * 2,
+        scratch_shapes=[pltpu.VMEM((640, 1024), bf16)] * 3 + [pltpu.VMEM((2, 5, ZB, YB, WIDE), f32)] * 2,
         compiler_params=grant(26),
         cost_estimate=cost(8 * 640 * 1024 * 1024, 14000000),
         name="inner2" if second else "inner1",

time: 140 us -> 138 us (0.986)
  Pallas kernels: 36.4 us -> 33.5 us
    pallas_call x2, Pallas kernels: 21.3 us -> 18.3 us  [inner(): pl.pallas_call(functools.partial(inner_kernel, second), out_shape=shaped(...]
    ppermute x4, waiting for transfers between devices: 8.52 us -> 6.78 us  [spread_forces(): lax.ppermute(held[half:], 'gx', [(g, g + bit) for g in range(0, 16, 2 * b...]
    ppermute x2, waiting for transfers between devices: 3.98 us -> 5.58 us  [exchange(): lax.ppermute(down, 'gx', back)]
  transfers between devices with their start and end apart: 16 -> 16, of which waited for: 10 -> 10; matrix products, arithmetic and copies ran while one was open for 0% -> 0% of each run, Pallas kernels for 19% -> 17%
where the time goes in v6:
time: 138 us
  blocking collectives  48.8 us (35%)
  Pallas kernels  33.5 us (24%)
  starting transfers between devices  32.4 us (23%)
  waiting for transfers between devices  21.2 us (15%)
    all_to_all x1, blocking collectives, body(): lax.all_to_all(outgoing, 'gx', split_axis=0, concat_axis=0, tiled=True)  48.8 us
    pallas_call x2, Pallas kernels, inner(): pl.pallas_call(functools.partial(inner_kernel, second), out_shape=shaped(...  18.3 us
    ppermute x4, starting transfers between devices, spread_forces(): lax.ppermute(held[half:], 'gx', [(g, g + bit) for g in range(0, 16, 2 * b...  9.17 us
    ppermute x4, waiting for transfers between devices, spread_forces(): lax.ppermute(held[half:], 'gx', [(g, g + bit) for g in range(0, 16, 2 * b...  6.78 us
    ppermute x3, waiting for transfers between devices, spread_forces(): held = held + lax.ppermute(held, 'gz', [(g, g ^ bit) for g in range(8)])  6.01 us
    ppermute x2, starting transfers between devices, exchange(): lax.ppermute(left, 'gz', [((g + 1) % 8, g) for g in range(8)])  5.89 us
    ppermute x2, waiting for transfers between devices, exchange(): lax.ppermute(down, 'gx', back)  5.58 us
    ppermute x2, starting transfers between devices, exchange(): lax.ppermute(up, 'gx', ahead)  5.02 us
  transfers between devices with their start and end apart: 16, of which 10 were waited for; matrix products, arithmetic and copies ran while one was open for 0% of the time, Pallas kernels for 17%

profile of v6, /device:TPU:0, one launch (start us, length us, event | category | flops | bytes accessed | tf_op | source)
XLA Modules:
  0.0 137.6 jit_solution(16323894635442104034)
XLA Ops:
  0.6 3.4 %pack.1 = f32[16,49,8,128]{3,2,1,0:T(8,128)} custom-call(f32[1024,128]{1,0:T(8,128)} %bitcast.10, f32[3,1024,128]{2,1,0:T(8,128)} %bitcast.9, f32[1024,128]{1,0:T(8,128)} %bitcast.11, f32[1024,128]{1,0:T(8,128)} %bitcast.12, s32[16,64]{1,0:T(8,128)} %bitcast.13, s32[16,64]{1,0:T(8,128)} %bitcast.14), custom_call_target="tpu_custom_call" | custom-call | flops 1000000 | bytes 6400000 | tf_op jit(solution)/shard_map/pack/pallas_call | solution.py:103
  4.0 48.8 %all_to_all.10.refs_0_ = f32[16,49,8,128]{3,2,1,0:T(8,128)S(1)} all-to-all(f32[16,49,8,128]{3,2,1,0:T(8,128)} %pack.1), channel_id=1, replica_groups=mesh['gx'=16,'gz'=8] {'gx'}, dimensions={0} | all-to-all | bytes 6422528 | tf_op jit(solution)/shard_map/all_to_all | solution.py:498
  54.2 2.5 %collective-permute-start = (f32[5,4,8,1024]{3,2,1,0:T(8,128)S(1)}, f32[5,4,8,1024]{3,2,1,0:T(8,128)S(1)}, u32[]{:S(2)}, u32[]{:S(2)}) collective-permute-start(f32[5,4,8,1024]{3,2,1,0:T(8,128)S(1)} %get-tuple-element.23), channel_id=1, source_target_pairs={{0,8},{8,16},{16,24},{24,56},{56,48},{48,40},{40,32},{32,64},{64,7... | collective-permute-start | bytes 1966088 | tf_op jit(solution)/shard_map/ppermute | solution.py:197
  58.0 2.9 %collective-permute-start.3 = (f32[5,2,8,1024]{3,2,1,0:T(8,128)S(1)}, f32[5,2,8,1024]{3,2,1,0:T(8,128)S(1)}, u32[]{:S(2)}, u32[]{:S(2)}) collective-permute-start(f32[5,2,8,1024]{3,2,1,0:T(8,128)S(1)} %get-tuple-element.26), channel_id=1, source_target_pairs={{1,0},{2,1},{3,2},{4,3},{5,4},{6,5},{7,6},{0,7},{9,8},{10,9},{11,1... | collective-permute-start | bytes 983048 | tf_op jit(solution)/shard_map/ppermute | solution.py:200
  61.0 9.0 %inner1.1.refs_0_ = f32[5,16,8,1024]{3,2,1,0:T(8,128)S(1)} custom-call(f32[5,16,8,1024]{3,2,1,0:T(8,128)S(1)} %get-tuple-element.21.refs_0_.refs_1_, f32[16,8,1024]{2,1,0:T(8,128)S(1)} %get-tuple-element.22.refs_1_.refs_2_, f32[1024,1024]{1,0:T(8,128)S(1)} %copy-done.1, f32[1024,1024]{1,0:T(8,128)S(1)} %copy-done.2), custom_call_target="tpu_custom_call" | custom-call | flops 5368709120 | bytes 14000000 | tf_op jit(solution)/shard_map/inner1/pallas_call | solution.py:325
  70.0 3.6 %collective-permute-done.1.refs_3_ = f32[5,4,8,1024]{3,2,1,0:T(8,128)S(1)} collective-permute-done((f32[5,4,8,1024]{3,2,1,0:T(8,128)S(1)}, f32[5,4,8,1024]{3,2,1,0:T(8,128)S(1)}, u32[]{:S(2)}, u32[]{:S(2)}) %collective-permute-start.1) | collective-permute-done | bytes 655392 | tf_op jit(solution)/shard_map/ppermute | solution.py:198
  73.7 2.0 %first.1 = (f32[5,16,8,1024]{3,2,1,0:T(8,128)S(1)}, f32[5,4,8,1024]{3,2,1,0:T(8,128)S(1)}, f32[5,4,8,1024]{3,2,1,0:T(8,128)S(1)}, f32[5,2,8,1024]{3,2,1,0:T(8,128)S(1)}, f32[5,2,8,1024]{3,2,1,0:T(8,128)S(1)}) custom-call(f32[5,16,8,1024]{3,2,1,0:T(8,128)S(1)} %inner1.1.refs_0_, f32[16,8,1024]{2,1,0:T(8,128)S(1)} %get-tuple-element.22.refs_1_.refs_2_, ...), custom_call_target="tpu_custom_call" | custom-call | flops 10000000 | bytes 9000000 | tf_op jit(solution)/shard_map/first/pallas_call | solution.py:350
  75.6 2.5 %collective-permute-start.4 = (f32[5,4,8,1024]{3,2,1,0:T(8,128)S(1)}, f32[5,4,8,1024]{3,2,1,0:T(8,128)S(1)}, u32[]{:S(2)}, u32[]{:S(2)}) collective-permute-start(f32[5,4,8,1024]{3,2,1,0:T(8,128)S(1)} %get-tuple-element.28), channel_id=1, source_target_pairs={{0,8},{8,16},{16,24},{24,56},{56,48},{48,40},{40,32},{32,64},{64,7... | collective-permute-start | bytes 1966088 | tf_op jit(solution)/shard_map/ppermute | solution.py:197
  78.2 1.5 %collective-permute-start.5 = (f32[5,4,8,1024]{3,2,1,0:T(8,128)S(1)}, f32[5,4,8,1024]{3,2,1,0:T(8,128)S(1)}, u32[]{:S(2)}, u32[]{:S(2)}) collective-permute-start(f32[5,4,8,1024]{3,2,1,0:T(8,128)S(1)} %get-tuple-element.29), channel_id=1, source_target_pairs={{8,0},{16,8},{24,16},{56,24},{48,56},{40,48},{32,40},{64,32},{72,6... | collective-permute-start | bytes 1966088 | tf_op jit(solution)/shard_map/ppermute | solution.py:198
  79.7 2.9 %collective-permute-start.7 = (f32[5,2,8,1024]{3,2,1,0:T(8,128)S(1)}, f32[5,2,8,1024]{3,2,1,0:T(8,128)S(1)}, u32[]{:S(2)}, u32[]{:S(2)}) collective-permute-start(f32[5,2,8,1024]{3,2,1,0:T(8,128)S(1)} %get-tuple-element.31), channel_id=1, source_target_pairs={{1,0},{2,1},{3,2},{4,3},{5,4},{6,5},{7,6},{0,7},{9,8},{10,9},{11,1... | collective-permute-start | bytes 983048 | tf_op jit(solution)/shard_map/ppermute | solution.py:200
  82.6 9.3 %inner2.1.refs_0_ = f32[5,16,8,1024]{3,2,1,0:T(8,128)S(1)} custom-call(f32[5,16,8,1024]{3,2,1,0:T(8,128)S(1)} %get-tuple-element.27.refs_0_, f32[5,16,8,1024]{3,2,1,0:T(8,128)S(1)} %get-tuple-element.21.refs_0_.refs_1_, f32[16,8,1024]{2,1,0:T(8,128)S(1)} %get-tuple-element.22.refs_1_.refs_2_, f32[1024,1024]{1,0:T(8,128)S(1)} %copy-done.1, ...), custom_call_target="tpu_custom_call" | custom-call | flops 5368709120 | bytes 14000000 | tf_op jit(solution)/shard_map/inner2/pallas_call | solution.py:325
  91.9 2.0 %collective-permute-done.5.refs_3_ = f32[5,4,8,1024]{3,2,1,0:T(8,128)S(1)} collective-permute-done((f32[5,4,8,1024]{3,2,1,0:T(8,128)S(1)}, f32[5,4,8,1024]{3,2,1,0:T(8,128)S(1)}, u32[]{:S(2)}, u32[]{:S(2)}) %collective-permute-start.5) | collective-permute-done | bytes 655392 | tf_op jit(solution)/shard_map/ppermute | solution.py:198
  93.9 2.1 %final.1 = (f32[16,40,8,128]{3,2,1,0:T(8,128)}, f32[16,8,1024]{2,1,0:T(8,128)S(1)}) custom-call(f32[5,16,8,1024]{3,2,1,0:T(8,128)S(1)} %inner2.1.refs_0_, f32[16,8,1024]{2,1,0:T(8,128)S(1)} %get-tuple-element.22.refs_1_.refs_2_, f32[5,4,8,1024]{3,2,1,0:T(8,128)S(1)} %collective-permute-done.4.refs_2_, f32[5,4,8,1024]{3,2,1,0:T(8,128)S(1)} %collective-permute-done.5.refs_3_, ...), custom_call_target="tpu_custom_call" | custom-call | flops 10000000 | bytes 9000000 | tf_op jit(solution)/shard_map/final/pallas_call | solution.py:378
  96.0 4.9 %all-to-all-start.1 = ((f32[16,40,8,128]{3,2,1,0:T(8,128)}), f32[16,40,8,128]{3,2,1,0:T(8,128)S(1)}, u32[]{:S(2)}, u32[]{:S(2)}) async-start(f32[16,40,8,128]{3,2,1,0:T(8,128)} %get-tuple-element.32), calls=%async_computation.1 | async-start | bytes 5242880 | tf_op jit(solution)/shard_map/all_to_all | solution.py:506
  101.0 4.5 %forces.1 = f32[64,128]{1,0:T(8,128)S(1)} custom-call(f32[16,8,1024]{2,1,0:T(8,128)S(1)} %get-tuple-element.36.load_ref, f32[16,1024]{1,0:T(8,128)S(1)} %get-tuple-element.37.code_ref, f32[256,128]{1,0:T(8,128)S(1)} %copy-done), custom_call_target="tpu_custom_call" | custom-call | flops 134217728 | bytes 700000 | tf_op jit(solution)/shard_map/forces/pallas_call | solution.py:461
  106.8 1.5 %collective-permute-start.9 = (f32[64,128]{1,0:T(8,128)S(1)}, f32[64,128]{1,0:T(8,128)S(1)}, u32[]{:S(2)}, u32[]{:S(2)}) collective-permute-start(f32[64,128]{1,0:T(8,128)S(1)} %add.9), channel_id=1, source_target_pairs={{0,2},{1,3},{2,0},{3,1},{4,6},{5,7},{6,4},{7,5},{8,10},{9,11},{10,... | collective-permute-start | bytes 98312 | tf_op jit(solution)/shard_map/ppermute | solution.py:475
  108.3 2.4 %collective-permute-done.9 = f32[64,128]{1,0:T(8,128)S(1)} collective-permute-done((f32[64,128]{1,0:T(8,128)S(1)}, f32[64,128]{1,0:T(8,128)S(1)}, u32[]{:S(2)}, u32[]{:S(2)}) %collective-permute-start.9) | collective-permute-done | bytes 32800 | tf_op jit(solution)/shard_map/ppermute | solution.py:475
  110.8 3.0 %collective-permute-start.10 = (f32[64,128]{1,0:T(8,128)S(1)}, f32[64,128]{1,0:T(8,128)S(1)}, u32[]{:S(2)}, u32[]{:S(2)}) collective-permute-start(f32[64,128]{1,0:T(8,128)S(1)} %add.10), channel_id=1, source_target_pairs={{0,4},{1,5},{2,6},{3,7},{4,0},{5,1},{6,2},{7,3},{8,12},{9,13},{10,... | collective-permute-start | bytes 98312 | tf_op jit(solution)/shard_map/ppermute | solution.py:475
  113.8 2.4 %collective-permute-done.10 = f32[64,128]{1,0:T(8,128)S(1)} collective-permute-done((f32[64,128]{1,0:T(8,128)S(1)}, f32[64,128]{1,0:T(8,128)S(1)}, u32[]{:S(2)}, u32[]{:S(2)}) %collective-permute-start.10) | collective-permute-done | bytes 32800 | tf_op jit(solution)/shard_map/ppermute | solution.py:475
  116.2 5.3 %collective-permute-start.11 = (f32[32,128]{1,0:T(8,128)S(1)}, f32[32,128]{1,0:T(8,128)S(1)}, u32[]{:S(2)}, u32[]{:S(2)}) collective-permute-start(f32[32,128]{1,0:T(8,128)S(1)} %slice.32), channel_id=1, source_target_pairs={{0,64},{1,65},{2,66},{3,67},{4,68},{5,69},{6,70},{7,71}} | collective-permute-start | bytes 49160 | tf_op jit(solution)/shard_map/ppermute | solution.py:480
  121.5 2.7 %collective-permute-done.11 = f32[32,128]{1,0:T(8,128)S(1)} collective-permute-done((f32[32,128]{1,0:T(8,128)S(1)}, f32[32,128]{1,0:T(8,128)S(1)}, u32[]{:S(2)}, u32[]{:S(2)}) %collective-permute-start.11) | collective-permute-done | bytes 16416 | tf_op jit(solution)/shard_map/ppermute | solution.py:480
  128.2 1.5 %collective-permute-done.13 = f32[8,128]{1,0:T(8,128)S(1)} collective-permute-done((f32[8,128]{1,0:T(8,128)S(1)}, f32[8,128]{1,0:T(8,128)S(1)}, u32[]{:S(2)}, u32[]{:S(2)}) %collective-permute-start.13) | collective-permute-done | bytes 4128 | tf_op jit(solution)/shard_map/ppermute | solution.py:480
  132.8 2.9 %all-to-all-done.1.in_ref = f32[16,40,8,128]{3,2,1,0:T(8,128)S(1)} async-done(((f32[16,40,8,128]{3,2,1,0:T(8,128)}), f32[16,40,8,128]{3,2,1,0:T(8,128)S(1)}, u32[]{:S(2)}, u32[]{:S(2)}) %all-to-all-start.1) | async-done | bytes 2621472 | tf_op jit(solution)/shard_map/all_to_all | solution.py:506
  135.7 1.8 %home.1 = (f32[1024,128]{1,0:T(8,128)}, f32[3,1024,128]{2,1,0:T(8,128)}, f32[1024,128]{1,0:T(8,128)}) custom-call(f32[16,40,8,128]{3,2,1,0:T(8,128)S(1)} %all-to-all-done.1.in_ref), custom_call_target="tpu_custom_call" | custom-call | flops 1000000 | bytes 5300000 | tf_op jit(solution)/shard_map/home/pallas_call | solution.py:408
  (34 shorter events, 11.1 us)
Async XLA Ops:
  4.0 56.9 %copy-start.1 = (f32[1024,1024]{1,0:T(8,128)S(1)}, f32[1024,1024]{1,0:T(8,128)}, u32[]{:S(2)}) copy-start(f32[1024,1024]{1,0:T(8,128)} %refs_3_.3) | copy-start | bytes 12582916
  4.0 56.9 %copy-start.2 = (f32[1024,1024]{1,0:T(8,128)S(1)}, f32[1024,1024]{1,0:T(8,128)}, u32[]{:S(2)}) copy-start(f32[1024,1024]{1,0:T(8,128)} %refs_4_.1) | copy-start | bytes 12582916
  54.2 15.9 %collective-permute-start = (f32[5,4,8,1024]{3,2,1,0:T(8,128)S(1)}, f32[5,4,8,1024]{3,2,1,0:T(8,128)S(1)}, u32[]{:S(2)}, u32[]{:S(2)}) collective-permute-start(f32[5,4,8,1024]{3,2,1,0:T(8,128)S(1)} %get-tuple-element.23), channel_id=1, source_target_pairs={{0,8},{8,16},{16,24},{24,56},{56,48},{48,40},{40,32},{32,64},{64,7... | collective-permute-start | bytes 1966088 | tf_op jit(solution)/shard_map/ppermute | solution.py:197
  56.7 17.0 %collective-permute-start.1 = (f32[5,4,8,1024]{3,2,1,0:T(8,128)S(1)}, f32[5,4,8,1024]{3,2,1,0:T(8,128)S(1)}, u32[]{:S(2)}, u32[]{:S(2)}) collective-permute-start(f32[5,4,8,1024]{3,2,1,0:T(8,128)S(1)} %get-tuple-element.24), channel_id=1, source_target_pairs={{8,0},{16,8},{24,16},{56,24},{48,56},{40,48},{32,40},{64,32},{72,6... | collective-permute-start | bytes 1966088 | tf_op jit(solution)/shard_map/ppermute | solution.py:198
  58.0 12.0 %collective-permute-start.2 = (f32[5,2,8,1024]{3,2,1,0:T(8,128)S(1)}, f32[5,2,8,1024]{3,2,1,0:T(8,128)S(1)}, u32[]{:S(2)}, u32[]{:S(2)}) collective-permute-start(f32[5,2,8,1024]{3,2,1,0:T(8,128)S(1)} %get-tuple-element.25), channel_id=1, source_target_pairs={{0,1},{1,2},{2,3},{3,4},{4,5},{5,6},{6,7},{7,0},{8,9},{9,10},{10,1... | collective-permute-start | bytes 983048 | tf_op jit(solution)/shard_map/ppermute | solution.py:199
  58.0 12.0 %collective-permute-start.3 = (f32[5,2,8,1024]{3,2,1,0:T(8,128)S(1)}, f32[5,2,8,1024]{3,2,1,0:T(8,128)S(1)}, u32[]{:S(2)}, u32[]{:S(2)}) collective-permute-start(f32[5,2,8,1024]{3,2,1,0:T(8,128)S(1)} %get-tuple-element.26), channel_id=1, source_target_pairs={{1,0},{2,1},{3,2},{4,3},{5,4},{6,5},{7,6},{0,7},{9,8},{10,9},{11,1... | collective-permute-start | bytes 983048 | tf_op jit(solution)/shard_map/ppermute | solution.py:200
  75.6 16.3 %collective-permute-start.4 = (f32[5,4,8,1024]{3,2,1,0:T(8,128)S(1)}, f32[5,4,8,1024]{3,2,1,0:T(8,128)S(1)}, u32[]{:S(2)}, u32[]{:S(2)}) collective-permute-start(f32[5,4,8,1024]{3,2,1,0:T(8,128)S(1)} %get-tuple-element.28), channel_id=1, source_target_pairs={{0,8},{8,16},{16,24},{24,56},{56,48},{48,40},{40,32},{32,64},{64,7... | collective-permute-start | bytes 1966088 | tf_op jit(solution)/shard_map/ppermute | solution.py:197
  78.2 15.7 %collective-permute-start.5 = (f32[5,4,8,1024]{3,2,1,0:T(8,128)S(1)}, f32[5,4,8,1024]{3,2,1,0:T(8,128)S(1)}, u32[]{:S(2)}, u32[]{:S(2)}) collective-permute-start(f32[5,4,8,1024]{3,2,1,0:T(8,128)S(1)} %get-tuple-element.29), channel_id=1, source_target_pairs={{8,0},{16,8},{24,16},{56,24},{48,56},{40,48},{32,40},{64,32},{72,6... | collective-permute-start | bytes 1966088 | tf_op jit(solution)/shard_map/ppermute | solution.py:198
  79.6 12.3 %collective-permute-start.6 = (f32[5,2,8,1024]{3,2,1,0:T(8,128)S(1)}, f32[5,2,8,1024]{3,2,1,0:T(8,128)S(1)}, u32[]{:S(2)}, u32[]{:S(2)}) collective-permute-start(f32[5,2,8,1024]{3,2,1,0:T(8,128)S(1)} %get-tuple-element.30), channel_id=1, source_target_pairs={{0,1},{1,2},{2,3},{3,4},{4,5},{5,6},{6,7},{7,0},{8,9},{9,10},{10,1... | collective-permute-start | bytes 983048 | tf_op jit(solution)/shard_map/ppermute | solution.py:199
  79.7 12.2 %collective-permute-start.7 = (f32[5,2,8,1024]{3,2,1,0:T(8,128)S(1)}, f32[5,2,8,1024]{3,2,1,0:T(8,128)S(1)}, u32[]{:S(2)}, u32[]{:S(2)}) collective-permute-start(f32[5,2,8,1024]{3,2,1,0:T(8,128)S(1)} %get-tuple-element.31), channel_id=1, source_target_pairs={{1,0},{2,1},{3,2},{4,3},{5,4},{6,5},{7,6},{0,7},{9,8},{10,9},{11,1... | collective-permute-start | bytes 983048 | tf_op jit(solution)/shard_map/ppermute | solution.py:200
  96.0 5.0 %copy-start = (f32[256,128]{1,0:T(8,128)S(1)}, f32[256,128]{1,0:T(8,128)}, u32[]{:S(2)}) copy-start(f32[256,128]{1,0:T(8,128)} %table_ref.1) | copy-start | bytes 393220
  96.0 39.6 %all-to-all-start.1 = ((f32[16,40,8,128]{3,2,1,0:T(8,128)}), f32[16,40,8,128]{3,2,1,0:T(8,128)S(1)}, u32[]{:S(2)}, u32[]{:S(2)}) async-start(f32[16,40,8,128]{3,2,1,0:T(8,128)} %get-tuple-element.32), calls=%async_computation.1 | async-start | bytes 5242880 | tf_op jit(solution)/shard_map/all_to_all | solution.py:506
  105.5 1.3 collective-permute-start.8
  106.8 3.9 %collective-permute-start.9 = (f32[64,128]{1,0:T(8,128)S(1)}, f32[64,128]{1,0:T(8,128)S(1)}, u32[]{:S(2)}, u32[]{:S(2)}) collective-permute-start(f32[64,128]{1,0:T(8,128)S(1)} %add.9), channel_id=1, source_target_pairs={{0,2},{1,3},{2,0},{3,1},{4,6},{5,7},{6,4},{7,5},{8,10},{9,11},{10,... | collective-permute-start | bytes 98312 | tf_op jit(solution)/shard_map/ppermute | solution.py:475
  110.8 5.4 %collective-permute-start.10 = (f32[64,128]{1,0:T(8,128)S(1)}, f32[64,128]{1,0:T(8,128)S(1)}, u32[]{:S(2)}, u32[]{:S(2)}) collective-permute-start(f32[64,128]{1,0:T(8,128)S(1)} %add.10), channel_id=1, source_target_pairs={{0,4},{1,5},{2,6},{3,7},{4,0},{5,1},{6,2},{7,3},{8,12},{9,13},{10,... | collective-permute-start | bytes 98312 | tf_op jit(solution)/shard_map/ppermute | solution.py:475
  116.2 8.0 %collective-permute-start.11 = (f32[32,128]{1,0:T(8,128)S(1)}, f32[32,128]{1,0:T(8,128)S(1)}, u32[]{:S(2)}, u32[]{:S(2)}) collective-permute-start(f32[32,128]{1,0:T(8,128)S(1)} %slice.32), channel_id=1, source_target_pairs={{0,64},{1,65},{2,66},{3,67},{4,68},{5,69},{6,70},{7,71}} | collective-permute-start | bytes 49160 | tf_op jit(solution)/shard_map/ppermute | solution.py:480
  124.2 2.6 %collective-permute-start.12 = (f32[16,128]{1,0:T(8,128)S(1)}, f32[16,128]{1,0:T(8,128)S(1)}, u32[]{:S(2)}, u32[]{:S(2)}) collective-permute-start(f32[16,128]{1,0:T(8,128)S(1)} %slice.34), channel_id=1, source_target_pairs={{0,32},{64,96},{1,33},{65,97},{2,34},{66,98},{3,35},{67,99},{4,36}... | collective-permute-start | bytes 24584 | tf_op jit(solution)/shard_map/ppermute | solution.py:480
  126.9 2.7 %collective-permute-start.13 = (f32[8,128]{1,0:T(8,128)S(1)}, f32[8,128]{1,0:T(8,128)S(1)}, u32[]{:S(2)}, u32[]{:S(2)}) collective-permute-start(f32[8,128]{1,0:T(8,128)S(1)} %slice.36), channel_id=1, source_target_pairs={{0,16},{32,48},{64,80},{96,112},{1,17},{33,49},{65,81},{97,113},{2... | collective-permute-start | bytes 12296 | tf_op jit(solution)/shard_map/ppermute | solution.py:480
  129.6 2.6 %collective-permute-start.14 = (f32[4,128]{1,0:T(4,128)S(1)}, f32[4,128]{1,0:T(4,128)S(1)}, u32[]{:S(2)}, u32[]{:S(2)}) collective-permute-start(f32[4,128]{1,0:T(4,128)S(1)} %slice.30), channel_id=1, source_target_pairs={{0,8},{16,24},{32,40},{48,56},{64,72},{80,88},{96,104},{112,120},{... | collective-permute-start | bytes 6152 | tf_op jit(solution)/shard_map/ppermute | solution.py:480
